TPU v7x, 256 devices: a whole 4x4x8 slice. The times are simulated.
256 devices in a mesh: blk: 32 (over z, y), view: 8 (over x, core).
Axes of the slice: x: 4, y: 4, z: 8, core: 2. Of those that a mesh axis runs over, the one named last changes fastest.
Arguments:
- estimate: float32 [512, 128, 256], P('blk'), may hold values from 0.3 to 3
- views: float32 [8, 512, 128, 256], P('view', 'blk'), may hold values from 0.3 to 3
- axial_taps: float32 [8, 33], P('view'), may hold values from 0.1 to 1
- lateral_taps: float32 [8, 2, 17], P('view'), may hold values from 0.05 to 1
- cover: int32 [8, 2], P('view'), may hold values from 0 to 512, as said below
Outputs:
- refined: float32 [512, 128, 256], P('blk')
Inputs may be any that keep to these rules, and one draw needn't show every extreme that they name: cover[v, 0] < cover[v, 1]; every first plane is at most 128 and every end at least 384; some view starts at plane 0 and some view ends at 512.
All inputs are finite; a program needn't handle non-finite values.
Results may differ from a plain program's by a relative error of at most 0.00015.
Values sent between devices are 32-bit elements; how exact they have to be, the bound alone decides.
No kernel may reach another device: no remote copies, remote signals or barrier semaphores. Data moves between devices by JAX's collectives and lax.ppermute only.
A program may use at most 64 MiB of HBM per device.

v0:
```python
import jax
import jax.numpy as jnp
from jax import lax
from jax.sharding import PartitionSpec as P

RAD = 8
RZ = 16
ITERS = 2


def padded(block, sides, width):
    for axis, dim in sides:
        count = lax.axis_size(axis)
        forward = [(i, i + 1) for i in range(count - 1)]
        backward = [(target, source) for source, target in forward]
        low = lax.ppermute(
            lax.slice_in_dim(block, block.shape[dim] - width, None, axis=dim), axis, forward
        )
        high = lax.ppermute(lax.slice_in_dim(block, 0, width, axis=dim), axis, backward)
        block = jnp.concatenate([low, block, high], axis=dim)
    return block


def banded(taps, count, reach):
    taps = taps / jnp.sum(taps)
    rows = jnp.arange(count)[:, None]
    cols = jnp.arange(count)[None, :]
    offset = cols - rows
    where_in = jnp.abs(offset) <= reach
    index = jnp.clip(offset + reach, 0, 2 * reach)
    return jnp.where(where_in, jnp.take(taps, index), jnp.float32(0.0))


def local_axial(taps, planes_dev, reach, flipped):
    taps = taps / jnp.sum(taps)
    rows = jnp.arange(planes_dev)[:, None]
    cols = jnp.arange(planes_dev + 2 * reach)[None, :]
    if flipped:
        offset = rows + reach - cols
    else:
        offset = cols - reach - rows
    where_in = jnp.abs(offset) <= reach
    index = jnp.clip(offset + reach, 0, 2 * reach)
    return jnp.where(where_in, jnp.take(taps, index), jnp.float32(0.0))


def local(estimate, views, axial_taps, lateral_taps, cover):
    hi = lax.Precision.HIGHEST
    planes_dev, rows_all, cols_all = estimate.shape
    ky = banded(lateral_taps[0, 0], rows_all, RAD)
    kx = banded(lateral_taps[0, 1], cols_all, RAD)
    planes = lax.axis_index("blk") * planes_dev + jnp.arange(planes_dev)
    inside = (planes >= cover[0, 0]) & (planes < cover[0, 1])
    recorded = views[0]
    kz_ahead = local_axial(axial_taps[0], planes_dev, RZ, False)
    kz_behind = local_axial(axial_taps[0], planes_dev, RZ, True)
    for step in range(ITERS):
        widened = padded(estimate, (("blk", 0),), RZ)
        blurred = jnp.einsum("wc,cyx->wyx", kz_ahead, widened, precision=hi)
        blurred = jnp.einsum("zyx,wx->zyw", blurred, kx, precision=hi)
        blurred = jnp.einsum("zyx,wy->zwx", blurred, ky, precision=hi)
        ratio = recorded / blurred
        back = jnp.einsum("zyx,xw->zyw", ratio, kx, precision=hi)
        back = jnp.einsum("zyx,yw->zwx", back, ky, precision=hi)
        spread = padded(back, (("blk", 0),), RZ)
        returned = jnp.einsum("wc,cyx->wyx", kz_behind, spread, precision=hi)
        log_terms = jnp.where(inside[:, None, None], jnp.log(returned), jnp.float32(0.0))
        total = lax.psum(log_terms, "view")
        estimate = estimate * jnp.exp(total)
    return estimate


def solution(mesh):
    in_specs = (
        P("blk", None, None),
        P("view", "blk", None, None),
        P("view", None),
        P("view", None, None),
        P("view", None),
    )
    out_specs = P("blk", None, None)
    return jax.shard_map(local, mesh=mesh, in_specs=in_specs, out_specs=out_specs, check_vma=False)
```

profile of v0, /device:TPU:8, one launch (start us, length us, event | category | flops | bytes accessed | tf_op | source)
XLA Modules:
  0.0 520.1 jit_solution(3957215918461065242)
XLA Ops:
  6.5 4.1 collective-permute-start.1
  15.2 4.8 gather_fusion.1
  23.4 32.7 %collective-permute-done.1 = f32[16,128,256]{2,1,0:T(8,128)} collective-permute-done((f32[16,128,256]{2,1,0:T(8,128)}, f32[16,128,256]{2,1,0:T(8,128)}, u32[]{:S(2)}, u32[]{:S(2)}) %collective-permute-start.1) | collective-permute-done | bytes 2097184 | tf_op jit(solution)/shard_map/ppermute | solution.py:19
  61.1 6.6 %fusion.6 = f32[16,128,256]{2,0,1:T(8,128)S(1)} fusion(f32[48,128,256]{2,1,0:T(8,128)S(1)} %pad_maximum_fusion, f32[16,48]{1,0:T(8,128)S(1)} %reshape.365, s32[48]{0:T(128)S(1)} %iota_add_fusion), kind=kOutput, calls=%fused_computation.11 | convolution fusion | flops 301999872 | bytes 8391872 | tf_op jit(solution)/shard_map/wc,cyx->wyx/dot_general | solution.py:59
  67.6 13.7 %fusion.18 = f32[16,128,256]{2,1,0:T(8,128)S(1)} fusion(f32[16,128,256]{2,0,1:T(8,128)S(1)} %fusion.6, f32[]{:T(128)} %bitcast.55, f32[]{:T(128)} %bitcast.56, f32[]{:T(128)} %bitcast.57, f32[]{:T(128)} %bitcast.58, f32[]{:T(128)} %bitcast.59, f32[]{:T(128)} %bitcast.61, f32[]{:T(128)} %bitcast.60, f32[]{:T(128)} %bitcast.36, f32[]{:T(128)} %bitcast.38, ...), kind=kOutput, calls=%fused_computation.25 | convolution fusion | flops 1613955072 | bytes 4194372 | tf_op jit(solution)/shard_map/zyx,wx->zyw/dot_general | solution.py:60
  81.4 13.1 %fusion.76 = f32[128,16,256]{2,0,1:T(8,128)S(1)} fusion(f32[16,128,256]{2,1,0:T(8,128)S(1)} %fusion.18, f32[]{:T(128)} %bitcast.24, f32[]{:T(128)} %bitcast.25, f32[]{:T(128)} %bitcast.26, f32[]{:T(128)} %bitcast.27, f32[]{:T(128)} %bitcast.28, f32[]{:T(128)} %bitcast.30, f32[]{:T(128)} %bitcast.29, f32[]{:T(128)} %bitcast.5, f32[]{:T(128)} %bitcast.7, ...), kind=kOutput, calls=%fused_computation.88 | convolution fusion | flops 806141952 | bytes 4194372 | tf_op jit(solution)/shard_map/zyx,wy->zwx/dot_general | solution.py:61
  94.4 12.7 %fusion.13 = f32[16,128,256]{2,1,0:T(8,128)S(1)} fusion(f32[128,16,256]{2,0,1:T(8,128)S(1)} %fusion.76, f32[1,16,128,256]{3,2,1,0:T(8,128)S(1)} %copy-done.3, f32[]{:T(128)} %bitcast.55, f32[]{:T(128)} %bitcast.56, f32[]{:T(128)} %bitcast.57, f32[]{:T(128)} %bitcast.58, f32[]{:T(128)} %bitcast.59, f32[]{:T(128)} %bitcast.61, f32[]{:T(128)} %bitcast.60, ...), kind=kOutput, calls=%fused_computation.20 | convolution fusion | flops 1614479360 | bytes 6291524 | tf_op jit(solution)/shard_map/zyx,xw->zyw/dot_general | solution.py:63
  107.1 12.7 %convolution_bitcast_fusion.1 = f32[16,128,256]{2,1,0:T(8,128)S(1)} fusion(f32[16,128,256]{2,1,0:T(8,128)S(1)} %fusion.13, f32[]{:T(128)} %bitcast.24, f32[]{:T(128)} %bitcast.25, f32[]{:T(128)} %bitcast.26, f32[]{:T(128)} %bitcast.27, f32[]{:T(128)} %bitcast.28, f32[]{:T(128)} %bitcast.30, f32[]{:T(128)} %bitcast.29, f32[]{:T(128)} %bitcast.5, ...), kind=kOutput, calls=%fused_computation.32 | convolution fusion | flops 806141952 | bytes 4194372 | tf_op jit(solution)/shard_map/zyx,yw->zwx/dot_general | solution.py:64
  121.8 3.9 collective-permute-start.2
  125.9 4.8 gather_fusion
  132.5 35.3 %collective-permute-done.3 = f32[16,128,256]{2,1,0:T(8,128)} collective-permute-done((f32[16,128,256]{2,1,0:T(8,128)S(1)}, f32[16,128,256]{2,1,0:T(8,128)}, u32[]{:S(2)}, u32[]{:S(2)}) %collective-permute-start.3) | collective-permute-done | bytes 2097184 | tf_op jit(solution)/shard_map/ppermute | solution.py:19
  172.0 7.8 %log_select_fusion.1 = f32[16,128,256]{2,0,1:T(8,128)} fusion(f32[48,128,256]{2,1,0:T(8,128)S(1)} %pad_maximum_fusion.1, pred[16]{0:T(512)(128)(4,1)S(1)} %compare_and_fusion, f32[16,48]{1,0:T(8,128)S(1)} %reshape.361, s32[16]{0:T(128)S(1)} %iota_add_fusion.1), kind=kOutput, calls=%fused_computation.30 | convolution fusion | flops 302524160 | bytes 8391760 | tf_op jit(solution)/shard_map/wc,cyx->wyx/dot_general | solution.py:66
  179.9 80.9 %all-reduce.3.cloned.1.call-done = f32[16,128,256]{2,0,1:T(8,128)} async-done(((f32[16,128,256]{2,0,1:T(8,128)}), f32[16,128,256]{2,0,1:T(8,128)}) %all-reduce.3.cloned.1.call-update) | async-done | bytes 2097168 | tf_op jit(solution)/shard_map/psum | solution.py:68
  260.8 3.6 copy_multiply_fusion
  266.9 3.8 collective-permute-start.4
  270.7 41.1 %collective-permute-done.5 = f32[16,128,256]{2,0,1:T(8,128)S(1)} collective-permute-done((f32[16,128,256]{2,0,1:T(8,128)S(1)}, f32[16,128,256]{2,0,1:T(8,128)S(1)}, u32[]{:S(2)}, u32[]{:S(2)}) %collective-permute-start.5) | collective-permute-done | bytes 2097184 | tf_op jit(solution)/shard_map/ppermute | solution.py:19
  317.1 13.8 %fusion.16 = f32[16,128,256]{2,1,0:T(8,128)S(1)} fusion(f32[16,128,256]{2,0,1:T(8,128)S(1)} %fusion, f32[]{:T(128)} %bitcast.55, f32[]{:T(128)} %bitcast.56, f32[]{:T(128)} %bitcast.57, f32[]{:T(128)} %bitcast.58, f32[]{:T(128)} %bitcast.59, f32[]{:T(128)} %bitcast.61, f32[]{:T(128)} %bitcast.60, f32[]{:T(128)} %bitcast.36, f32[]{:T(128)} %bitcast.38, ...), kind=kOutput, calls=%fused_computation.23 | convolution fusion | flops 1613955072 | bytes 4194372 | tf_op jit(solution)/shard_map/zyx,wx->zyw/dot_general | solution.py:60
  330.9 12.9 %fusion.73 = f32[128,16,256]{2,0,1:T(8,128)S(1)} fusion(f32[16,128,256]{2,1,0:T(8,128)S(1)} %fusion.16, f32[]{:T(128)} %bitcast.24, f32[]{:T(128)} %bitcast.25, f32[]{:T(128)} %bitcast.26, f32[]{:T(128)} %bitcast.27, f32[]{:T(128)} %bitcast.28, f32[]{:T(128)} %bitcast.30, f32[]{:T(128)} %bitcast.29, f32[]{:T(128)} %bitcast.5, f32[]{:T(128)} %bitcast.7, ...), kind=kOutput, calls=%fused_computation.85 | convolution fusion | flops 806141952 | bytes 4194372 | tf_op jit(solution)/shard_map/zyx,wy->zwx/dot_general | solution.py:61
  343.7 12.8 %fusion.12 = f32[16,128,256]{2,1,0:T(8,128)S(1)} fusion(f32[128,16,256]{2,0,1:T(8,128)S(1)} %fusion.73, f32[1,16,128,256]{3,2,1,0:T(8,128)S(1)} %copy-done.4, f32[]{:T(128)} %bitcast.55, f32[]{:T(128)} %bitcast.56, f32[]{:T(128)} %bitcast.57, f32[]{:T(128)} %bitcast.58, f32[]{:T(128)} %bitcast.59, f32[]{:T(128)} %bitcast.61, f32[]{:T(128)} %bitcast.60, ...), kind=kOutput, calls=%fused_computation.18 | convolution fusion | flops 1614479360 | bytes 6291524 | tf_op jit(solution)/shard_map/zyx,xw->zyw/dot_general | solution.py:63
  356.5 12.9 %convolution_bitcast_fusion = f32[16,128,256]{2,1,0:T(8,128)S(1)} fusion(f32[16,128,256]{2,1,0:T(8,128)S(1)} %fusion.12, f32[]{:T(128)} %bitcast.24, f32[]{:T(128)} %bitcast.25, f32[]{:T(128)} %bitcast.26, f32[]{:T(128)} %bitcast.27, f32[]{:T(128)} %bitcast.28, f32[]{:T(128)} %bitcast.30, f32[]{:T(128)} %bitcast.29, f32[]{:T(128)} %bitcast.5, f32[]{:T(128)} %bitcast.7, ...), kind=kOutput, calls=%fused_computation.31 | convolution fusion | flops 806141952 | bytes 4194372 | tf_op jit(solution)/shard_map/zyx,yw->zwx/dot_general | solution.py:64
  371.4 3.9 collective-permute-start.6
  375.3 40.3 %collective-permute-done.7 = f32[16,128,256]{2,1,0:T(8,128)S(1)} collective-permute-done((f32[16,128,256]{2,1,0:T(8,128)S(1)}, f32[16,128,256]{2,1,0:T(8,128)S(1)}, u32[]{:S(2)}, u32[]{:S(2)}) %collective-permute-start.7) | collective-permute-done | bytes 2097184 | tf_op jit(solution)/shard_map/ppermute | solution.py:19
  418.2 7.8 %log_select_fusion = f32[16,128,256]{2,0,1:T(8,128)} fusion(f32[48,128,256]{2,1,0:T(8,128)S(1)} %pad_maximum_fusion.2, pred[16]{0:T(512)(128)(4,1)S(1)} %compare_and_fusion, f32[16,48]{1,0:T(8,128)S(1)} %reshape.361, s32[16]{0:T(128)S(1)} %iota_add_fusion.1), kind=kOutput, calls=%fused_computation.29 | convolution fusion | flops 302524160 | bytes 8391760 | tf_op jit(solution)/shard_map/wc,cyx->wyx/dot_general | solution.py:66
  426.1 82.3 %all-reduce.5.cloned.1.call-done = f32[16,128,256]{2,0,1:T(8,128)} async-done(((f32[16,128,256]{2,0,1:T(8,128)}), f32[16,128,256]{2,0,1:T(8,128)}) %all-reduce.5.cloned.1.call-update) | async-done | bytes 2097168 | tf_op jit(solution)/shard_map/psum | solution.py:68
  (46 shorter events, 38.0 us)
Async XLA Ops:
  6.5 254.3 %all-reduce.3.cloned.1.call-start = ((), (), s32[]{:S(2)}) async-start(), calls=%async_computation | async-start | bytes 4194304 | tf_op jit(solution)/shard_map/psum | solution.py:68
  6.5 49.6 %collective-permute-start.1 = (f32[16,128,256]{2,1,0:T(8,128)}, f32[16,128,256]{2,1,0:T(8,128)}, u32[]{:S(2)}, u32[]{:S(2)}) collective-permute-start(f32[16,128,256]{2,1,0:T(8,128)} %param.7), channel_id=1, source_target_pairs={{8,0},{16,8},{24,16},{32,24},{40,32},{48,40},{56,48},{64,56},{72,6... | collective-permute-start | bytes 6291464 | tf_op jit(solution)/shard_map/ppermute | solution.py:19
  10.6 47.4 %collective-permute-start = (f32[16,128,256]{2,1,0:T(8,128)}, f32[16,128,256]{2,1,0:T(8,128)}, u32[]{:S(2)}, u32[]{:S(2)}) collective-permute-start(f32[16,128,256]{2,1,0:T(8,128)} %param.7), channel_id=1, source_target_pairs={{0,8},{8,16},{16,24},{24,32},{32,40},{40,48},{48,56},{56,64},{64,7... | collective-permute-start | bytes 6291464 | tf_op jit(solution)/shard_map/ppermute | solution.py:16
  15.2 4.9 copy-start.1
  15.2 42.8 %copy-start = (f32[16,128,256]{2,1,0:T(8,128)S(1)}, f32[16,128,256]{2,1,0:T(8,128)}, u32[]{:S(2)}) copy-start(f32[16,128,256]{2,1,0:T(8,128)} %param.7) | copy-start | bytes 6291460
  81.3 13.1 %copy-start.3 = (f32[1,16,128,256]{3,2,1,0:T(8,128)S(1)}, f32[1,16,128,256]{3,2,1,0:T(8,128)}, u32[]{:S(2)}) copy-start(f32[1,16,128,256]{3,2,1,0:T(8,128)} %param.8) | copy-start | bytes 6291460
  119.9 48.0 %collective-permute-start.3 = (f32[16,128,256]{2,1,0:T(8,128)S(1)}, f32[16,128,256]{2,1,0:T(8,128)}, u32[]{:S(2)}, u32[]{:S(2)}) collective-permute-start(f32[16,128,256]{2,1,0:T(8,128)S(1)} %convolution_bitcast_fusion.1), channel_id=1, source_target_pairs={{8,0},{16,8},{24,16},{32,24},{40,32},{48,40},{56,48},{64,56},{72,6... | collective-permute-start | bytes 6291464 | tf_op jit(solution)/shard_map/ppermute | solution.py:19
  121.8 47.2 %collective-permute-start.2 = (f32[16,128,256]{2,1,0:T(8,128)S(1)}, f32[16,128,256]{2,1,0:T(8,128)}, u32[]{:S(2)}, u32[]{:S(2)}) collective-permute-start(f32[16,128,256]{2,1,0:T(8,128)S(1)} %convolution_bitcast_fusion.1), channel_id=1, source_target_pairs={{0,8},{8,16},{16,24},{24,32},{32,40},{40,48},{48,56},{56,64},{64,7... | collective-permute-start | bytes 6291464 | tf_op jit(solution)/shard_map/ppermute | solution.py:16
  125.9 4.9 copy-start.2
  179.9 328.5 %all-reduce.5.cloned.1.call-start = ((), (), s32[]{:S(2)}) async-start(), calls=%async_computation.1 | async-start | bytes 4194304 | tf_op jit(solution)/shard_map/psum | solution.py:68
  264.4 47.3 %collective-permute-start.5 = (f32[16,128,256]{2,0,1:T(8,128)S(1)}, f32[16,128,256]{2,0,1:T(8,128)S(1)}, u32[]{:S(2)}, u32[]{:S(2)}) collective-permute-start(f32[16,128,256]{2,0,1:T(8,128)S(1)} %copy_multiply_fusion), channel_id=1, source_target_pairs={{8,0},{16,8},{24,16},{32,24},{40,32},{48,40},{56,48},{64,56},{72,6... | collective-permute-start | bytes 6291464 | tf_op jit(solution)/shard_map/ppermute | solution.py:19
  266.9 47.1 %collective-permute-start.4 = (f32[16,128,256]{2,0,1:T(8,128)S(1)}, f32[16,128,256]{2,0,1:T(8,128)S(1)}, u32[]{:S(2)}, u32[]{:S(2)}) collective-permute-start(f32[16,128,256]{2,0,1:T(8,128)S(1)} %copy_multiply_fusion), channel_id=1, source_target_pairs={{0,8},{8,16},{16,24},{24,32},{32,40},{40,48},{48,56},{56,64},{64,7... | collective-permute-start | bytes 6291464 | tf_op jit(solution)/shard_map/ppermute | solution.py:16
  330.8 12.9 %copy-start.4 = (f32[1,16,128,256]{3,2,1,0:T(8,128)S(1)}, f32[1,16,128,256]{3,2,1,0:T(8,128)}, u32[]{:S(2)}) copy-start(f32[1,16,128,256]{3,2,1,0:T(8,128)} %param.8) | copy-start | bytes 6291460
  369.5 46.1 %collective-permute-start.7 = (f32[16,128,256]{2,1,0:T(8,128)S(1)}, f32[16,128,256]{2,1,0:T(8,128)S(1)}, u32[]{:S(2)}, u32[]{:S(2)}) collective-permute-start(f32[16,128,256]{2,1,0:T(8,128)S(1)} %convolution_bitcast_fusion), channel_id=1, source_target_pairs={{8,0},{16,8},{24,16},{32,24},{40,32},{48,40},{56,48},{64,56},{72,6... | collective-permute-start | bytes 6291464 | tf_op jit(solution)/shard_map/ppermute | solution.py:19
  371.4 46.1 %collective-permute-start.6 = (f32[16,128,256]{2,1,0:T(8,128)S(1)}, f32[16,128,256]{2,1,0:T(8,128)S(1)}, u32[]{:S(2)}, u32[]{:S(2)}) collective-permute-start(f32[16,128,256]{2,1,0:T(8,128)S(1)} %convolution_bitcast_fusion), channel_id=1, source_target_pairs={{0,8},{8,16},{16,24},{24,32},{32,40},{40,48},{48,56},{56,64},{64,7... | collective-permute-start | bytes 6291464 | tf_op jit(solution)/shard_map/ppermute | solution.py:16
Sparse Core Ops, SparseCore 0:
  180.0 80.7 all-reduce.2
  426.2 82.1 all-reduce.4
where the time goes:
time: 531 us; the launch traced here: 520 us
  waiting for transfers between devices  320 us (60%)
  matrix products  130 us (24%)
  starting transfers between devices  24 us (5%)
  other arithmetic  18.1 us (3%)
  local copies, waits for them, and re-layouts  14.4 us (3%)
  between operations  13.9 us (3%)
    psum x2, waiting for transfers between devices, local(): total = lax.psum(log_terms, 'view')  163 us
    ppermute x4, waiting for transfers between devices, padded(): lax.ppermute(lax.slice_in_dim(block, 0, width, axis=dim), axis, backward)  149 us
    dot_general x2, matrix products, local(): blurred = jnp.einsum('zyx,wx->zyw', blurred, kx, precision=hi)  27.5 us
    dot_general x2, matrix products, local(): blurred = jnp.einsum('zyx,wy->zwx', blurred, ky, precision=hi)  25.9 us
    dot_general x2, matrix products, local(): back = jnp.einsum('zyx,yw->zwx', back, ky, precision=hi)  25.6 us
    dot_general x2, matrix products, local(): back = jnp.einsum('zyx,xw->zyw', ratio, kx, precision=hi)  25.4 us
    dot_general x2, matrix products, local(): returned = jnp.einsum('wc,cyx->wyx', kz_behind, spread, precision=hi)  15.7 us
    ppermute x4, starting transfers between devices, padded(): lax.ppermute(lax.slice_in_dim(block, block.shape[dim] - width, None, axis...  13.6 us
  transfers between devices with their start and end apart: 10, of which 10 were waited for; matrix products, arithmetic and copies ran while one was open for 3% of the time, Pallas kernels for 0%

commit v1 on v0

v1 whole, which is shorter than its diff:
```python
import functools

import jax
import jax.numpy as jnp
from jax import lax
from jax.experimental import pallas as pl
from jax.experimental.pallas import tpu as pltpu
from jax.sharding import PartitionSpec as P

RAD = 8
RZ = 16
ITERS = 2
YD = 4
XD = 4
F32 = jnp.float32
BF16 = jnp.bfloat16
NLAT = 2 * RAD + 1
NAX = 2 * RZ + 1

DIRS = ((-1, 0), (1, 0), (0, -1), (0, 1), (-1, -1), (-1, 1), (1, -1), (1, 1))
ANY = pl.BlockSpec(memory_space=pl.ANY)
SMEM = pl.BlockSpec(memory_space=pltpu.SMEM)
VMEM = pl.BlockSpec(memory_space=pltpu.VMEM)


def params():
    return pltpu.CompilerParams(vmem_limit_bytes=56 * 1024 * 1024)


def blk_shift(value, dz, dy):
    count = lax.axis_size("blk") // YD
    pairs = [
        (z * YD + y, (z + dz) * YD + y + dy)
        for z in range(count)
        for y in range(YD)
        if 0 <= z + dz < count and 0 <= y + dy < YD
    ]
    return lax.ppermute(value, "blk", pairs)


def y_turn(value, k):
    count = lax.axis_size("blk") // YD
    pairs = [(z * YD + y, z * YD + (y + k) % YD) for z in range(count) for y in range(YD)]
    return lax.ppermute(value, "blk", pairs)


def x_turn(value, k):
    pairs = [(2 * x + c, 2 * ((x + k) % XD) + c) for x in range(XD) for c in range(2)]
    return lax.ppermute(value, "view", pairs)


def core_swap(value):
    return lax.ppermute(value, "view", [(i, i ^ 1) for i in range(2 * XD)])


def split(value):
    high = value.astype(BF16)
    return high, (value - high.astype(F32)).astype(BF16)


def mm(a, b):
    return jnp.dot(a, b, preferred_element_type=F32)


def matrices_kernel(taps, kyh, kyl, kxh, kxl):
    row = lax.broadcasted_iota(jnp.int32, (128, 192), 0)
    col = lax.broadcasted_iota(jnp.int32, (128, 192), 1)
    one = jnp.int32(1)
    zero = jnp.int32(0)
    prow = sum(jnp.where(row >= 32 * n, one, zero) for n in (1, 2, 3))
    pcol = sum(jnp.where(col >= 48 * n, one, zero) for n in (1, 2, 3))
    near = jnp.where(prow == pcol, (col - 48 * pcol) - (row - 32 * prow), -1)
    wide = (
        lax.broadcasted_iota(jnp.int32, (256, 256), 0)
        - lax.broadcasted_iota(jnp.int32, (256, 256), 1)
        + RAD
    )
    for way in range(2):
        ky = jnp.zeros((128, 192), F32)
        kx = jnp.zeros((256, 256), F32)
        for d in range(NLAT):
            e = d if way == 0 else NLAT - 1 - d
            ky = jnp.where(near == d, taps[NAX + e], ky)
            kx = jnp.where(wide == d, taps[NAX + NLAT + e], kx)
        kyh[way], kyl[way] = split(ky)
        kxh[way], kxl[way] = split(kx)


def matrices(taps):
    ky = jax.ShapeDtypeStruct((2, 128, 192), BF16)
    kx = jax.ShapeDtypeStruct((2, 256, 256), BF16)
    return pl.pallas_call(
        matrices_kernel,
        out_shape=(ky, ky, kx, kx),
        in_specs=[SMEM],
        out_specs=(VMEM,) * 4,
        compiler_params=params(),
        name="matrices",
    )(taps)


def lateral(way, wide, kyh, kyl, kxh, kxl, across):
    @pl.loop(0, 24)
    def _(g):
        b = g // 4
        h = (g // 2) % 2
        s = g % 2
        block = wide[b, h, pl.ds(2 * s, 2)].reshape(192, 256)
        high, low = split(block)
        rows = mm(kyh[way], high) + (mm(kyl[way], high) + mm(kyh[way], low))
        high, low = split(rows)
        both = mm(high, kxh[way]) + (mm(low, kxh[way]) + mm(high, kxl[way]))
        across[pl.ds(4 * g, 4)] = both.reshape(4, 32, 256)


def axial(way, taps, across, finish):
    weights = [taps[d if way == 0 else NAX - 1 - d] for d in range(NAX)]

    @pl.loop(0, 16)
    def _(n):
        base = (n // 4) * 16
        rows = pl.ds(pl.multiple_of((n % 4) * 8, 8), 8)
        for half in range(2):
            lanes = pl.ds(half * 128, 128)
            sums = [None] * 16
            for j in range(48):
                value = across[base + j, rows, lanes]
                for o in range(max(0, j - 32), min(16, j + 1)):
                    term = weights[j - o] * value
                    sums[o] = term if sums[o] is None else sums[o] + term
            for o in range(16):
                finish(base + o, n // 4, o, rows, lanes, sums[o])


def halo_slot(wide, direction, halves):
    dz, dy = direction
    b = {1: 0, -1: 5, 0: pl.ds(1, 4)}[dz]
    r = {1: pl.ds(0, 8), -1: pl.ds(40, 8), 0: pl.ds(8, 32)}[dy]
    return wide.at[b, halves, :, :, r, :]


def edge_of(tile, direction):
    dz, dy = direction
    b = {-1: 0, 1: 3, 0: pl.ds(0, 4)}[dz]
    r = {-1: pl.ds(0, 8), 1: pl.ds(24, 8), 0: pl.ds(0, 32)}[dy]
    if len(tile.shape) == 6:
        return tile.at[b, :, :, :, r, :]
    return tile.at[b, :, :, r, :]


def place():
    blk = lax.axis_index("blk")
    view = lax.axis_index("view")
    return blk // YD, blk % YD, view // 2, view % 2


def run(copies):
    for copy in copies:
        copy.start()
    return copies


def forward_kernel(taps, kyh, kyl, kxh, kxl, *refs):
    pieces, halos, shown = refs[:8], refs[8:24], refs[24:28]
    center, edges = refs[28], refs[29:37]
    wide, across, views, ratio, sems = refs[37:]
    z, y, x, c = place()
    copies = []

    def copy(source, target):
        copies.append(pltpu.make_async_copy(source, target, sems.at[len(copies)]))

    for k in range(4):
        s = (x - k + XD) % XD
        for other in range(2):
            half = c if other == 0 else 1 - c
            copy(pieces[4 * other + k], wide.at[pl.ds(1, 4), half, s, :, pl.ds(8, 32), :])
    for n, direction in enumerate(DIRS):
        for other in range(2):
            half = c if other == 0 else 1 - c
            copy(halos[8 * other + n], halo_slot(wide, direction, half))
    for k in range(4):
        b = (y - k + YD) % YD
        copy(shown[k], views.at[pl.ds(pl.multiple_of(16 * b, 16), 16)])
    run(copies)
    for item in copies[:24]:
        item.wait()
    lateral(0, wide, kyh, kyl, kxh, kxl, across)
    for item in copies[24:]:
        item.wait()

    def finish(plane, b, o, rows, lanes, value):
        ratio[b, o // 8, (o % 8) // 2, o % 2, rows, lanes] = views[plane, rows, lanes] / value

    axial(0, taps, across, finish)
    del copies[:]
    copy(ratio, center)
    for n, direction in enumerate(DIRS):
        copy(edge_of(ratio, direction), edges[n])
    for item in run(copies):
        item.wait()


def edge_shape(direction, lead):
    dz, dy = direction
    return ((4,) if dz == 0 else ()) + lead + (4, 2, 32 if dy == 0 else 8, 256)


def forward(taps, mats, pieces, halos, shown):
    outs = [jax.ShapeDtypeStruct((4, 2, 4, 2, 32, 256), F32)]
    outs += [jax.ShapeDtypeStruct(edge_shape(d, (2,)), F32) for d in DIRS]
    got = pl.pallas_call(
        forward_kernel,
        out_shape=tuple(outs),
        in_specs=[SMEM] + [VMEM] * 4 + [ANY] * 28,
        out_specs=(ANY,) * 9,
        scratch_shapes=[
            pltpu.VMEM((6, 2, 4, 2, 48, 256), F32),
            pltpu.VMEM((96, 32, 256), F32),
            pltpu.VMEM((64, 32, 256), F32),
            pltpu.VMEM((4, 2, 4, 2, 32, 256), F32),
            pltpu.SemaphoreType.DMA((28,)),
        ],
        compiler_params=params(),
        name="forward",
    )(taps, *mats, *pieces, *halos, *shown)
    return got[0], got[1:]


def backward_kernel(taps, cover, kyh, kyl, kxh, kxl, *refs):
    center, halos = refs[0], refs[1:9]
    mine, other = refs[9:11]
    wide, across, logs, sems = refs[11:]
    z, y, x, c = place()
    copies = []

    def copy(source, target):
        copies.append(pltpu.make_async_copy(source, target, sems.at[len(copies)]))

    both = pl.ds(0, 2)
    copy(center, wide.at[pl.ds(1, 4), :, :, :, pl.ds(8, 32), :])
    for n, direction in enumerate(DIRS):
        copy(halos[n], halo_slot(wide, direction, both))
    for item in run(copies):
        item.wait()
    lateral(1, wide, kyh, kyl, kxh, kxl, across)
    first = cover[0]
    end = cover[1]

    def finish(plane, b, o, rows, lanes, value):
        at = z * 64 + plane
        inside = jnp.logical_and(at >= first, at < end)
        logs[b, o // 8, (o % 8) // 2, o % 2, rows, lanes] = jnp.where(
            inside, jnp.log(value), jnp.float32(0.0)
        )

    axial(1, taps, across, finish)
    del copies[:]
    copy(logs.at[:, c], mine)
    copy(logs.at[:, 1 - c], other)
    for item in run(copies):
        item.wait()


def backward(taps, cover, mats, center, halos):
    half = jax.ShapeDtypeStruct((4, 4, 2, 32, 256), F32)
    return pl.pallas_call(
        backward_kernel,
        out_shape=(half, half),
        in_specs=[SMEM, SMEM] + [VMEM] * 4 + [ANY] * 9,
        out_specs=(ANY, ANY),
        scratch_shapes=[
            pltpu.VMEM((6, 2, 4, 2, 48, 256), F32),
            pltpu.VMEM((96, 32, 256), F32),
            pltpu.VMEM((4, 2, 4, 2, 32, 256), F32),
            pltpu.SemaphoreType.DMA((9,)),
        ],
        compiler_params=params(),
        name="backward",
    )(taps, cover, *mats, center, *halos)


def shares_kernel(mine, got, *outs):
    z, y, x, c = place()
    for k in range(4):
        s = (x + k) % XD
        outs[k][...] = mine[:, s] + got[:, s]


def shares(mine, got):
    part = jax.ShapeDtypeStruct((4, 2, 32, 256), F32)
    return pl.pallas_call(
        shares_kernel,
        out_shape=(part,) * 4,
        in_specs=[VMEM, VMEM],
        out_specs=(VMEM,) * 4,
        compiler_params=params(),
        name="shares",
    )(mine, got)


def edges_kernel(*refs):
    pieces, outs = refs[:4], refs[4:12]
    tile, sems = refs[12:]
    z, y, x, c = place()
    copies = []

    def copy(source, target):
        copies.append(pltpu.make_async_copy(source, target, sems.at[len(copies)]))

    for k in range(4):
        copy(pieces[k], tile.at[:, (x - k + XD) % XD])
    for item in run(copies):
        item.wait()
    del copies[:]
    for n, direction in enumerate(DIRS):
        copy(edge_of(tile, direction), outs[n])
    for item in run(copies):
        item.wait()


def edges(pieces):
    return pl.pallas_call(
        edges_kernel,
        out_shape=tuple(jax.ShapeDtypeStruct(edge_shape(d, ()), F32) for d in DIRS),
        in_specs=[ANY] * 4,
        out_specs=(ANY,) * 8,
        scratch_shapes=[
            pltpu.VMEM((4, 4, 2, 32, 256), F32),
            pltpu.SemaphoreType.DMA((8,)),
        ],
        compiler_params=params(),
        name="edges",
    )(*pieces)


def slab_kernel(*refs):
    pieces, out = refs[:8], refs[8]
    slab, sems = refs[9:]
    z, y, x, c = place()
    copies = []

    def copy(source, target):
        copies.append(pltpu.make_async_copy(source, target, sems.at[len(copies)]))

    for k in range(4):
        s = (x - k + XD) % XD
        for other in range(2):
            half = c if other == 0 else 1 - c
            copy(pieces[4 * other + k], slab.at[half, s])
    for item in run(copies):
        item.wait()
    del copies[:]
    copy(slab, out)
    for item in run(copies):
        item.wait()


def slab(pieces):
    return pl.pallas_call(
        slab_kernel,
        out_shape=jax.ShapeDtypeStruct((2, 4, 2, 128, 256), F32),
        in_specs=[ANY] * 8,
        out_specs=ANY,
        scratch_shapes=[
            pltpu.VMEM((2, 4, 2, 128, 256), F32),
            pltpu.SemaphoreType.DMA((8,)),
        ],
        compiler_params=params(),
        name="slab",
    )(*pieces)


def by_block(pieces, y):
    order = [pieces[0], pieces[3], pieces[2], pieces[1]]
    stack = jnp.stack(order + order[:3])
    return lax.dynamic_slice_in_dim(stack, (YD - y) % YD, 4, axis=0)


def gathered(share):
    return [share] + [x_turn(share, k) for k in (1, 2, 3)]


def local(estimate, views, axial_taps, lateral_taps, cover):
    z, y, x, c = place()
    taps = jnp.concatenate(
        [
            axial_taps[0] / jnp.sum(axial_taps[0]),
            lateral_taps[0, 0] / jnp.sum(lateral_taps[0, 0]),
            lateral_taps[0, 1] / jnp.sum(lateral_taps[0, 1]),
        ]
    )
    mats = matrices(taps)
    cover = cover[0]

    def rows_for(value, k, axis):
        return lax.dynamic_slice_in_dim(value, 32 * ((y + k) % YD), 32, axis=axis)

    own = lax.dynamic_slice_in_dim(estimate, 8 * c + 2 * x, 2, axis=0)
    parts = [rows_for(own, 0, 1)] + [y_turn(rows_for(own, k, 1), k) for k in (1, 2, 3)]
    share = by_block(parts, y)
    shown = [rows_for(views[0], 0, 1)]
    shown += [y_turn(rows_for(views[0], k, 1), k) for k in (1, 2, 3)]
    for step in range(ITERS):
        pieces = gathered(share)
        swapped = [core_swap(piece) for piece in pieces]
        halos = [blk_shift(e, *d) for e, d in zip(edges(pieces), DIRS)]
        halos += [core_swap(halo) for halo in halos]
        center, rims = forward(taps, mats, pieces + swapped, halos, shown)
        halos = [blk_shift(e, *d) for e, d in zip(rims, DIRS)]
        mine, other = backward(taps, cover, mats, center, halos)
        terms = shares(mine, core_swap(other))
        total = terms[0]
        for k in (1, 2, 3):
            total = total + x_turn(terms[k], k)
        share = share * jnp.exp(total)
    parts = [lax.dynamic_index_in_dim(share, (y + k) % YD, 0, keepdims=False) for k in range(4)]
    parts = [parts[0]] + [y_turn(parts[k], k) for k in (1, 2, 3)]
    strip = by_block(parts, y)
    strip = jnp.transpose(strip, (1, 0, 2, 3)).reshape(2, 128, 256)
    pieces = gathered(strip)
    pieces = pieces + [core_swap(piece) for piece in pieces]
    return slab(pieces).reshape(16, 128, 256)


def solution(mesh):
    in_specs = (
        P("blk", None, None),
        P("view", "blk", None, None),
        P("view", None),
        P("view", None, None),
        P("view", None),
    )
    out_specs = P("blk", None, None)
    return jax.shard_map(local, mesh=mesh, in_specs=in_specs, out_specs=out_specs, check_vma=False)
```

time: 531 us -> 397 us (0.75)
  the two profiles are of different devices: /device:TPU:8 before, /device:TPU:97 now
where the time goes in v1:
time: 397 us; the launch traced here: 391 us
  starting transfers between devices  183 us (46%)
  Pallas kernels  100 us (25%)
  waiting for transfers between devices  85.8 us (22%)
  local copies, waits for them, and re-layouts  14.1 us (4%)
  other arithmetic  5.77 us (1%)
    ppermute x32, starting transfers between devices, blk_shift(): return lax.ppermute(value, 'blk', pairs)  102 us
    ppermute x30, starting transfers between devices, core_swap(): return lax.ppermute(value, 'view', [(i, i ^ 1) for i in range(2 * XD)])  51 us
    pallas_call x2, Pallas kernels, forward(): pl.pallas_call(forward_kernel, out_shape=tuple(outs), in_specs=[SMEM] + [...  43.4 us
    ppermute x15, waiting for transfers between devices, x_turn(): return lax.ppermute(value, 'view', pairs)  42.9 us
    pallas_call x2, Pallas kernels, backward(): pl.pallas_call(backward_kernel, out_shape=(half, half), in_specs=[SMEM, S...  41.6 us
    ppermute x32, waiting for transfers between devices, blk_shift(): return lax.ppermute(value, 'blk', pairs)  28 us
    ppermute x15, starting transfers between devices, x_turn(): return lax.ppermute(value, 'view', pairs)  17.1 us
    ppermute x9, starting transfers between devices, y_turn(): return lax.ppermute(value, 'blk', pairs)  13.2 us
  transfers between devices with their start and end apart: 86, of which 29 were waited for; matrix products, arithmetic and copies ran while one was open for 2% of the time, Pallas kernels for 2%

profile of v1, /device:TPU:97, one launch (start us, length us, event | category | flops | bytes accessed | tf_op | source)
XLA Modules:
  0.0 390.8 jit_solution(5447638286935399932)
XLA Ops:
  21.8 5.7 %collective-permute-done.3.refs_1_ = f32[4,2,32,256]{3,2,1,0:T(8,128)S(1)} collective-permute-done((f32[4,2,32,256]{3,2,1,0:T(8,128)S(1)}, f32[4,2,32,256]{3,2,1,0:T(8,128)S(1)}, u32[]{:S(2)}, u32[]{:S(2)}) %collective-permute-start.3) | collective-permute-done | bytes 262176 | tf_op jit(solution)/shard_map/ppermute | solution.py:49
  39.3 6.0 %collective-permute-start.17 = (f32[4,2,8,256]{3,2,1,0:T(8,128)}, f32[4,2,8,256]{3,2,1,0:T(8,128)S(1)}, u32[]{:S(2)}, u32[]{:S(2)}) collective-permute-start(f32[4,2,8,256]{3,2,1,0:T(8,128)} %get-tuple-element.66), channel_id=1, source_target_pairs={{0,40},{8,48},{16,56},{32,72},{40,80},{48,88},{64,104},{72,112},{8... | collective-permute-start | bytes 196616 | tf_op jit(solution)/shard_map/ppermute | solution.py:38
  61.3 5.7 %collective-permute-start.13 = (f32[4,4,2,8,256]{4,3,2,1,0:T(8,128)}, f32[4,4,2,8,256]{4,3,2,1,0:T(8,128)}, u32[]{:S(2)}, u32[]{:S(2)}) collective-permute-start(f32[4,4,2,8,256]{4,3,2,1,0:T(8,128)} %get-tuple-element.62), channel_id=1, source_target_pairs={{0,8},{8,16},{16,24},{32,40},{40,48},{48,56},{64,72},{72,80},{80,8... | collective-permute-start | bytes 786440 | tf_op jit(solution)/shard_map/ppermute | solution.py:38
  77.6 21.7 %forward.2 = (f32[4,2,4,2,32,256]{5,4,3,2,1,0:T(8,128)}, f32[2,4,2,32,256]{4,3,2,1,0:T(8,128)}, f32[2,4,2,32,256]{4,3,2,1,0:T(8,128)}, f32[4,2,4,2,8,256]{5,4,3,...) custom-call(f32[67]{0:T(128)} %pad_maximum_fusion.taps, ...), custom_call_target="tpu_custom_call" | custom-call | tf_op jit(solution)/shard_map/forward/pallas_call | solution.py:212
  102.5 4.6 %collective-permute-start.30 = (f32[2,4,2,32,256]{4,3,2,1,0:T(8,128)}, f32[2,4,2,32,256]{4,3,2,1,0:T(8,128)S(1)}, u32[]{:S(2)}, u32[]{:S(2)}) collective-permute-start(f32[2,4,2,32,256]{4,3,2,1,0:T(8,128)} %get-tuple-element.69), channel_id=1, source_target_pairs={{0,32},{8,40},{16,48},{24,56},{32,64},{40,72},{48,80},{56,88},{64,... | collective-permute-start | bytes 1572872 | tf_op jit(solution)/shard_map/ppermute | solution.py:38
  108.4 5.4 %collective-permute-start.32 = (f32[4,2,4,2,8,256]{5,4,3,2,1,0:T(8,128)}, f32[4,2,4,2,8,256]{5,4,3,2,1,0:T(8,128)S(1)}, u32[]{:S(2)}, u32[]{:S(2)}) collective-permute-start(f32[4,2,4,2,8,256]{5,4,3,2,1,0:T(8,128)} %get-tuple-element.71), channel_id=1, source_target_pairs={{0,8},{8,16},{16,24},{32,40},{40,48},{48,56},{64,72},{72,80},{80,8... | collective-permute-start | bytes 1572872 | tf_op jit(solution)/shard_map/ppermute | solution.py:38
  119.2 6.4 %collective-permute-done.35.refs_7_ = f32[2,4,2,8,256]{4,3,2,1,0:T(8,128)S(1)} collective-permute-done((f32[2,4,2,8,256]{4,3,2,1,0:T(8,128)}, f32[2,4,2,8,256]{4,3,2,1,0:T(8,128)S(1)}, u32[]{:S(2)}, u32[]{:S(2)}) %collective-permute-start.35) | collective-permute-done | bytes 131104 | tf_op jit(solution)/shard_map/ppermute | solution.py:38
  125.6 7.7 %collective-permute-start.36 = (f32[2,4,2,8,256]{4,3,2,1,0:T(8,128)}, f32[2,4,2,8,256]{4,3,2,1,0:T(8,128)S(1)}, u32[]{:S(2)}, u32[]{:S(2)}) collective-permute-start(f32[2,4,2,8,256]{4,3,2,1,0:T(8,128)} %get-tuple-element.75), channel_id=1, source_target_pairs={{0,40},{8,48},{16,56},{32,72},{40,80},{48,88},{64,104},{72,112},{8... | collective-permute-start | bytes 393224 | tf_op jit(solution)/shard_map/ppermute | solution.py:38
  137.0 20.8 %backward.2 = (f32[4,4,2,32,256]{4,3,2,1,0:T(8,128)}, f32[4,4,2,32,256]{4,3,2,1,0:T(8,128)}) custom-call(f32[67]{0:T(128)} %pad_maximum_fusion.taps, s32[2]{0:T(128)} %bitcast.49, bf16[2,128,192]{2,1,0:T(8,128)(2,1)} %get-tuple-element.55.kyh, bf16[2,128,192]{2,1,0:T(8,128)(2,1)} %get-tuple-element.56.kyl, bf16[2,256,256]{2,1,0:T(8,128)(2,1)} %get-tuple-element.57.kxh, ...), custom_call_target="tpu_custom_call" | custom-call | tf_op jit(solution)/shard_map/backward/pallas_call | solution.py:267
  172.0 5.2 %collective-permute-done.38 = f32[4,2,32,256]{3,2,1,0:T(8,128)S(1)} collective-permute-done((f32[4,2,32,256]{3,2,1,0:T(8,128)}, f32[4,2,32,256]{3,2,1,0:T(8,128)S(1)}, u32[]{:S(2)}, u32[]{:S(2)}) %collective-permute-start.38) | collective-permute-done | bytes 262176 | tf_op jit(solution)/shard_map/ppermute | solution.py:49
  177.2 6.7 %collective-permute-done.39 = f32[4,2,32,256]{3,2,1,0:T(8,128)S(1)} collective-permute-done((f32[4,2,32,256]{3,2,1,0:T(8,128)}, f32[4,2,32,256]{3,2,1,0:T(8,128)S(1)}, u32[]{:S(2)}, u32[]{:S(2)}) %collective-permute-start.39) | collective-permute-done | bytes 262176 | tf_op jit(solution)/shard_map/ppermute | solution.py:49
  189.2 5.0 %collective-permute-done.43.refs_3_ = f32[4,2,32,256]{3,2,1,0:T(8,128)S(1)} collective-permute-done((f32[4,2,32,256]{3,2,1,0:T(8,128)S(1)}, f32[4,2,32,256]{3,2,1,0:T(8,128)S(1)}, u32[]{:S(2)}, u32[]{:S(2)}) %collective-permute-start.43) | collective-permute-done | bytes 262176 | tf_op jit(solution)/shard_map/ppermute | solution.py:49
  194.3 5.4 %collective-permute-start.47 = (f32[4,2,32,256]{3,2,1,0:T(8,128)S(1)}, f32[4,2,32,256]{3,2,1,0:T(8,128)S(1)}, u32[]{:S(2)}, u32[]{:S(2)}) collective-permute-start(f32[4,2,32,256]{3,2,1,0:T(8,128)S(1)} %collective-permute-done.43.refs_3_), channel_id=1, source_target_pairs={{0,1},{1,0},{2,3},{3,2},{4,5},{5,4},{6,7},{7,6},{8,9},{9,8},{10,11... | collective-permute-start | bytes 786440 | tf_op jit(solution)/shard_map/ppermute | solution.py:53
  211.8 7.6 %collective-permute-start.55 = (f32[4,2,8,256]{3,2,1,0:T(8,128)}, f32[4,2,8,256]{3,2,1,0:T(8,128)S(1)}, u32[]{:S(2)}, u32[]{:S(2)}) collective-permute-start(f32[4,2,8,256]{3,2,1,0:T(8,128)} %get-tuple-element.89), channel_id=1, source_target_pairs={{0,40},{8,48},{16,56},{32,72},{40,80},{48,88},{64,104},{72,112},{8... | collective-permute-start | bytes 196616 | tf_op jit(solution)/shard_map/ppermute | solution.py:38
  219.5 10.6 %collective-permute-start.60 = (f32[4,2,8,256]{3,2,1,0:T(8,128)S(1)}, f32[4,2,8,256]{3,2,1,0:T(8,128)S(1)}, u32[]{:S(2)}, u32[]{:S(2)}) collective-permute-start(f32[4,2,8,256]{3,2,1,0:T(8,128)S(1)} %collective-permute-done.52.refs_12_), channel_id=1, source_target_pairs={{0,1},{1,0},{2,3},{3,2},{4,5},{5,4},{6,7},{7,6},{8,9},{9,8},{10,11... | collective-permute-start | bytes 196616 | tf_op jit(solution)/shard_map/ppermute | solution.py:53
  252.7 21.7 %forward.3 = (f32[4,2,4,2,32,256]{5,4,3,2,1,0:T(8,128)}, f32[2,4,2,32,256]{4,3,2,1,0:T(8,128)}, f32[2,4,2,32,256]{4,3,2,1,0:T(8,128)}, f32[4,2,4,2,8,256]{5,4,3,...) custom-call(f32[67]{0:T(128)} %pad_maximum_fusion.taps, ...), custom_call_target="tpu_custom_call" | custom-call | tf_op jit(solution)/shard_map/forward/pallas_call | solution.py:212
  277.6 4.6 %collective-permute-start.65 = (f32[2,4,2,32,256]{4,3,2,1,0:T(8,128)}, f32[2,4,2,32,256]{4,3,2,1,0:T(8,128)S(1)}, u32[]{:S(2)}, u32[]{:S(2)}) collective-permute-start(f32[2,4,2,32,256]{4,3,2,1,0:T(8,128)} %get-tuple-element.92), channel_id=1, source_target_pairs={{0,32},{8,40},{16,48},{24,56},{32,64},{40,72},{48,80},{56,88},{64,... | collective-permute-start | bytes 1572872 | tf_op jit(solution)/shard_map/ppermute | solution.py:38
  283.5 5.3 %collective-permute-start.67 = (f32[4,2,4,2,8,256]{5,4,3,2,1,0:T(8,128)}, f32[4,2,4,2,8,256]{5,4,3,2,1,0:T(8,128)S(1)}, u32[]{:S(2)}, u32[]{:S(2)}) collective-permute-start(f32[4,2,4,2,8,256]{5,4,3,2,1,0:T(8,128)} %get-tuple-element.94), channel_id=1, source_target_pairs={{0,8},{8,16},{16,24},{32,40},{40,48},{48,56},{64,72},{72,80},{80,8... | collective-permute-start | bytes 1572872 | tf_op jit(solution)/shard_map/ppermute | solution.py:38
  294.2 6.0 %collective-permute-done.70.refs_7_ = f32[2,4,2,8,256]{4,3,2,1,0:T(8,128)S(1)} collective-permute-done((f32[2,4,2,8,256]{4,3,2,1,0:T(8,128)}, f32[2,4,2,8,256]{4,3,2,1,0:T(8,128)S(1)}, u32[]{:S(2)}, u32[]{:S(2)}) %collective-permute-start.70) | collective-permute-done | bytes 131104 | tf_op jit(solution)/shard_map/ppermute | solution.py:38
  300.3 8.1 %collective-permute-start.71 = (f32[2,4,2,8,256]{4,3,2,1,0:T(8,128)}, f32[2,4,2,8,256]{4,3,2,1,0:T(8,128)S(1)}, u32[]{:S(2)}, u32[]{:S(2)}) collective-permute-start(f32[2,4,2,8,256]{4,3,2,1,0:T(8,128)} %get-tuple-element.98), channel_id=1, source_target_pairs={{0,40},{8,48},{16,56},{32,72},{40,80},{48,88},{64,104},{72,112},{8... | collective-permute-start | bytes 393224 | tf_op jit(solution)/shard_map/ppermute | solution.py:38
  312.0 20.8 %backward.3 = (f32[4,4,2,32,256]{4,3,2,1,0:T(8,128)}, f32[4,4,2,32,256]{4,3,2,1,0:T(8,128)}) custom-call(f32[67]{0:T(128)} %pad_maximum_fusion.taps, s32[2]{0:T(128)} %bitcast.50, bf16[2,128,192]{2,1,0:T(8,128)(2,1)} %get-tuple-element.55.kyh, bf16[2,128,192]{2,1,0:T(8,128)(2,1)} %get-tuple-element.56.kyl, bf16[2,256,256]{2,1,0:T(8,128)(2,1)} %get-tuple-element.57.kxh, ...), custom_call_target="tpu_custom_call" | custom-call | tf_op jit(solution)/shard_map/backward/pallas_call | solution.py:267
  332.9 4.5 %collective-permute-start.72 = (f32[4,4,2,32,256]{4,3,2,1,0:T(8,128)}, f32[4,4,2,32,256]{4,3,2,1,0:T(8,128)S(1)}, u32[]{:S(2)}, u32[]{:S(2)}) collective-permute-start(f32[4,4,2,32,256]{4,3,2,1,0:T(8,128)} %get-tuple-element.100), channel_id=1, source_target_pairs={{0,1},{1,0},{2,3},{3,2},{4,5},{5,4},{6,7},{7,6},{8,9},{9,8},{10,11... | collective-permute-start | bytes 3145736 | tf_op jit(solution)/shard_map/ppermute | solution.py:53
  346.1 7.0 %collective-permute-done.73 = f32[4,2,32,256]{3,2,1,0:T(8,128)S(1)} collective-permute-done((f32[4,2,32,256]{3,2,1,0:T(8,128)}, f32[4,2,32,256]{3,2,1,0:T(8,128)S(1)}, u32[]{:S(2)}, u32[]{:S(2)}) %collective-permute-start.73) | collective-permute-done | bytes 262176 | tf_op jit(solution)/shard_map/ppermute | solution.py:49
  377.2 5.1 %collective-permute-start.85 = (f32[2,128,256]{2,1,0:T(8,128)S(1)}, f32[2,128,256]{2,1,0:T(8,128)S(1)}, u32[]{:S(2)}, u32[]{:S(2)}) collective-permute-start(f32[2,128,256]{2,1,0:T(8,128)S(1)} %collective-permute-done.81.refs_3_), channel_id=1, source_target_pairs={{0,1},{1,0},{2,3},{3,2},{4,5},{5,4},{6,7},{7,6},{8,9},{9,8},{10,11... | collective-permute-start | bytes 786440 | tf_op jit(solution)/shard_map/ppermute | solution.py:53
  (340 shorter events, 181.5 us)
Async XLA Ops:
  12.6 19.2 %collective-permute-start.6 = (f32[4,2,32,256]{3,2,1,0:T(8,128)S(1)}, f32[4,2,32,256]{3,2,1,0:T(8,128)S(1)}, u32[]{:S(2)}, u32[]{:S(2)}) collective-permute-start(f32[4,2,32,256]{3,2,1,0:T(8,128)S(1)} %constant_dynamic-slice_fusion.refs_0_), channel_id=1, source_target_pairs={{0,1},{1,0},{2,3},{3,2},{4,5},{5,4},{6,7},{7,6},{8,9},{9,8},{10,11... | collective-permute-start | bytes 786440 | tf_op jit(solution)/shard_map/ppermute | solution.py:53
  18.6 37.4 %collective-permute-start.28 = (f32[16,32,256]{2,1,0:T(8,128)S(1)}, f32[16,32,256]{2,1,0:T(8,128)S(1)}, u32[]{:S(2)}, u32[]{:S(2)}) collective-permute-start(f32[16,32,256]{2,1,0:T(8,128)S(1)} %get-tuple-element.107), channel_id=1, source_target_pairs={{0,24},{8,0},{16,8},{24,16},{32,56},{40,32},{48,40},{56,48},{64,88... | collective-permute-start | bytes 1572872 | tf_op jit(solution)/shard_map/ppermute | solution.py:44
  20.1 39.8 %collective-permute-start.26 = (f32[16,32,256]{2,1,0:T(8,128)S(1)}, f32[16,32,256]{2,1,0:T(8,128)S(1)}, u32[]{:S(2)}, u32[]{:S(2)}) collective-permute-start(f32[16,32,256]{2,1,0:T(8,128)S(1)} %get-tuple-element.108), channel_id=1, source_target_pairs={{0,8},{8,16},{16,24},{24,0},{32,40},{40,48},{48,56},{56,32},{64,72... | collective-permute-start | bytes 1572872 | tf_op jit(solution)/shard_map/ppermute | solution.py:44
  20.1 41.1 %collective-permute-start.27 = (f32[16,32,256]{2,1,0:T(8,128)S(1)}, f32[16,32,256]{2,1,0:T(8,128)S(1)}, u32[]{:S(2)}, u32[]{:S(2)}) collective-permute-start(f32[16,32,256]{2,1,0:T(8,128)S(1)} %get-tuple-element.110), channel_id=1, source_target_pairs={{0,16},{8,24},{16,0},{24,8},{32,48},{40,56},{48,32},{56,40},{64,80... | collective-permute-start | bytes 1572872 | tf_op jit(solution)/shard_map/ppermute | solution.py:44
  47.5 19.5 %collective-permute-start.9 = (f32[4,2,32,256]{3,2,1,0:T(8,128)}, f32[4,2,32,256]{3,2,1,0:T(8,128)S(1)}, u32[]{:S(2)}, u32[]{:S(2)}) collective-permute-start(f32[4,2,32,256]{3,2,1,0:T(8,128)} %copy-done.9), channel_id=1, source_target_pairs={{0,1},{1,0},{2,3},{3,2},{4,5},{5,4},{6,7},{7,6},{8,9},{9,8},{10,11... | collective-permute-start | bytes 786440 | tf_op jit(solution)/shard_map/ppermute | solution.py:53
  53.4 17.4 %collective-permute-start.10 = (f32[4,2,32,256]{3,2,1,0:T(8,128)}, f32[4,2,32,256]{3,2,1,0:T(8,128)S(1)}, u32[]{:S(2)}, u32[]{:S(2)}) collective-permute-start(f32[4,2,32,256]{3,2,1,0:T(8,128)} %get-tuple-element.59), channel_id=1, source_target_pairs={{32,0},{40,8},{48,16},{56,24},{64,32},{72,40},{80,48},{88,56},{96,... | collective-permute-start | bytes 786440 | tf_op jit(solution)/shard_map/ppermute | solution.py:38
  56.1 15.5 %collective-permute-start.11 = (f32[4,2,32,256]{3,2,1,0:T(8,128)}, f32[4,2,32,256]{3,2,1,0:T(8,128)S(1)}, u32[]{:S(2)}, u32[]{:S(2)}) collective-permute-start(f32[4,2,32,256]{3,2,1,0:T(8,128)} %get-tuple-element.60), channel_id=1, source_target_pairs={{0,32},{8,40},{16,48},{24,56},{32,64},{40,72},{48,80},{56,88},{64,... | collective-permute-start | bytes 786440 | tf_op jit(solution)/shard_map/ppermute | solution.py:38
  100.6 35.0 %collective-permute-start.29 = (f32[2,4,2,32,256]{4,3,2,1,0:T(8,128)}, f32[2,4,2,32,256]{4,3,2,1,0:T(8,128)S(1)}, u32[]{:S(2)}, u32[]{:S(2)}) collective-permute-start(f32[2,4,2,32,256]{4,3,2,1,0:T(8,128)} %get-tuple-element.68), channel_id=1, source_target_pairs={{32,0},{40,8},{48,16},{56,24},{64,32},{72,40},{80,48},{88,56},{96,... | collective-permute-start | bytes 1572872 | tf_op jit(solution)/shard_map/ppermute | solution.py:38
  102.5 33.1 %collective-permute-start.30 = (f32[2,4,2,32,256]{4,3,2,1,0:T(8,128)}, f32[2,4,2,32,256]{4,3,2,1,0:T(8,128)S(1)}, u32[]{:S(2)}, u32[]{:S(2)}) collective-permute-start(f32[2,4,2,32,256]{4,3,2,1,0:T(8,128)} %get-tuple-element.69), channel_id=1, source_target_pairs={{0,32},{8,40},{16,48},{24,56},{32,64},{40,72},{48,80},{56,88},{64,... | collective-permute-start | bytes 1572872 | tf_op jit(solution)/shard_map/ppermute | solution.py:38
  107.1 28.5 %collective-permute-start.31 = (f32[4,2,4,2,8,256]{5,4,3,2,1,0:T(8,128)}, f32[4,2,4,2,8,256]{5,4,3,2,1,0:T(8,128)S(1)}, u32[]{:S(2)}, u32[]{:S(2)}) collective-permute-start(f32[4,2,4,2,8,256]{5,4,3,2,1,0:T(8,128)} %get-tuple-element.70), channel_id=1, source_target_pairs={{8,0},{16,8},{24,16},{40,32},{48,40},{56,48},{72,64},{80,72},{88,8... | collective-permute-start | bytes 1572872 | tf_op jit(solution)/shard_map/ppermute | solution.py:38
  108.4 27.2 %collective-permute-start.32 = (f32[4,2,4,2,8,256]{5,4,3,2,1,0:T(8,128)}, f32[4,2,4,2,8,256]{5,4,3,2,1,0:T(8,128)S(1)}, u32[]{:S(2)}, u32[]{:S(2)}) collective-permute-start(f32[4,2,4,2,8,256]{5,4,3,2,1,0:T(8,128)} %get-tuple-element.71), channel_id=1, source_target_pairs={{0,8},{8,16},{16,24},{32,40},{40,48},{48,56},{64,72},{72,80},{80,8... | collective-permute-start | bytes 1572872 | tf_op jit(solution)/shard_map/ppermute | solution.py:38
  168.0 15.9 %collective-permute-start.39 = (f32[4,2,32,256]{3,2,1,0:T(8,128)}, f32[4,2,32,256]{3,2,1,0:T(8,128)S(1)}, u32[]{:S(2)}, u32[]{:S(2)}) collective-permute-start(f32[4,2,32,256]{3,2,1,0:T(8,128)} %get-tuple-element.80), channel_id=1, source_target_pairs={{0,4},{1,5},{2,6},{3,7},{4,0},{5,1},{6,2},{7,3},{8,12},{9,13},{10,... | collective-permute-start | bytes 786440 | tf_op jit(solution)/shard_map/ppermute | solution.py:49
  187.5 14.7 %collective-permute-start.41 = (f32[4,2,32,256]{3,2,1,0:T(8,128)S(1)}, f32[4,2,32,256]{3,2,1,0:T(8,128)S(1)}, u32[]{:S(2)}, u32[]{:S(2)}) collective-permute-start(f32[4,2,32,256]{3,2,1,0:T(8,128)S(1)} %exponential_multiply_fusion.1.refs_0_), channel_id=1, source_target_pairs={{0,2},{1,3},{2,4},{3,5},{4,6},{5,7},{6,0},{7,1},{8,10},{9,11},{10,... | collective-permute-start | bytes 786440 | tf_op jit(solution)/shard_map/ppermute | solution.py:49
  188.2 23.6 %collective-permute-start.44 = (f32[4,2,32,256]{3,2,1,0:T(8,128)S(1)}, f32[4,2,32,256]{3,2,1,0:T(8,128)S(1)}, u32[]{:S(2)}, u32[]{:S(2)}) collective-permute-start(f32[4,2,32,256]{3,2,1,0:T(8,128)S(1)} %exponential_multiply_fusion.1.refs_0_), channel_id=1, source_target_pairs={{0,1},{1,0},{2,3},{3,2},{4,5},{5,4},{6,7},{7,6},{8,9},{9,8},{10,11... | collective-permute-start | bytes 786440 | tf_op jit(solution)/shard_map/ppermute | solution.py:53
  194.3 45.3 %collective-permute-start.47 = (f32[4,2,32,256]{3,2,1,0:T(8,128)S(1)}, f32[4,2,32,256]{3,2,1,0:T(8,128)S(1)}, u32[]{:S(2)}, u32[]{:S(2)}) collective-permute-start(f32[4,2,32,256]{3,2,1,0:T(8,128)S(1)} %collective-permute-done.43.refs_3_), channel_id=1, source_target_pairs={{0,1},{1,0},{2,3},{3,2},{4,5},{5,4},{6,7},{7,6},{8,9},{9,8},{10,11... | collective-permute-start | bytes 786440 | tf_op jit(solution)/shard_map/ppermute | solution.py:53
  206.5 23.6 %collective-permute-start.53 = (f32[4,2,8,256]{3,2,1,0:T(8,128)}, f32[4,2,8,256]{3,2,1,0:T(8,128)S(1)}, u32[]{:S(2)}, u32[]{:S(2)}) collective-permute-start(f32[4,2,8,256]{3,2,1,0:T(8,128)} %get-tuple-element.87), channel_id=1, source_target_pairs={{32,8},{40,16},{48,24},{64,40},{72,48},{80,56},{96,72},{104,80},{1... | collective-permute-start | bytes 196616 | tf_op jit(solution)/shard_map/ppermute | solution.py:38
  210.5 19.8 %collective-permute-start.54 = (f32[4,2,8,256]{3,2,1,0:T(8,128)}, f32[4,2,8,256]{3,2,1,0:T(8,128)S(1)}, u32[]{:S(2)}, u32[]{:S(2)}) collective-permute-start(f32[4,2,8,256]{3,2,1,0:T(8,128)} %get-tuple-element.88), channel_id=1, source_target_pairs={{8,32},{16,40},{24,48},{40,64},{48,72},{56,80},{72,96},{80,104},{8... | collective-permute-start | bytes 196616 | tf_op jit(solution)/shard_map/ppermute | solution.py:38
  211.8 18.8 %collective-permute-start.55 = (f32[4,2,8,256]{3,2,1,0:T(8,128)}, f32[4,2,8,256]{3,2,1,0:T(8,128)S(1)}, u32[]{:S(2)}, u32[]{:S(2)}) collective-permute-start(f32[4,2,8,256]{3,2,1,0:T(8,128)} %get-tuple-element.89), channel_id=1, source_target_pairs={{0,40},{8,48},{16,56},{32,72},{40,80},{48,88},{64,104},{72,112},{8... | collective-permute-start | bytes 196616 | tf_op jit(solution)/shard_map/ppermute | solution.py:38
  275.7 34.9 %collective-permute-start.64 = (f32[2,4,2,32,256]{4,3,2,1,0:T(8,128)}, f32[2,4,2,32,256]{4,3,2,1,0:T(8,128)S(1)}, u32[]{:S(2)}, u32[]{:S(2)}) collective-permute-start(f32[2,4,2,32,256]{4,3,2,1,0:T(8,128)} %get-tuple-element.91), channel_id=1, source_target_pairs={{32,0},{40,8},{48,16},{56,24},{64,32},{72,40},{80,48},{88,56},{96,... | collective-permute-start | bytes 1572872 | tf_op jit(solution)/shard_map/ppermute | solution.py:38
  277.6 33.0 %collective-permute-start.65 = (f32[2,4,2,32,256]{4,3,2,1,0:T(8,128)}, f32[2,4,2,32,256]{4,3,2,1,0:T(8,128)S(1)}, u32[]{:S(2)}, u32[]{:S(2)}) collective-permute-start(f32[2,4,2,32,256]{4,3,2,1,0:T(8,128)} %get-tuple-element.92), channel_id=1, source_target_pairs={{0,32},{8,40},{16,48},{24,56},{32,64},{40,72},{48,80},{56,88},{64,... | collective-permute-start | bytes 1572872 | tf_op jit(solution)/shard_map/ppermute | solution.py:38
  282.2 28.4 %collective-permute-start.66 = (f32[4,2,4,2,8,256]{5,4,3,2,1,0:T(8,128)}, f32[4,2,4,2,8,256]{5,4,3,2,1,0:T(8,128)S(1)}, u32[]{:S(2)}, u32[]{:S(2)}) collective-permute-start(f32[4,2,4,2,8,256]{5,4,3,2,1,0:T(8,128)} %get-tuple-element.93), channel_id=1, source_target_pairs={{8,0},{16,8},{24,16},{40,32},{48,40},{56,48},{72,64},{80,72},{88,8... | collective-permute-start | bytes 1572872 | tf_op jit(solution)/shard_map/ppermute | solution.py:38
  283.5 27.1 %collective-permute-start.67 = (f32[4,2,4,2,8,256]{5,4,3,2,1,0:T(8,128)}, f32[4,2,4,2,8,256]{5,4,3,2,1,0:T(8,128)S(1)}, u32[]{:S(2)}, u32[]{:S(2)}) collective-permute-start(f32[4,2,4,2,8,256]{5,4,3,2,1,0:T(8,128)} %get-tuple-element.94), channel_id=1, source_target_pairs={{0,8},{8,16},{16,24},{32,40},{40,48},{48,56},{64,72},{72,80},{80,8... | collective-permute-start | bytes 1572872 | tf_op jit(solution)/shard_map/ppermute | solution.py:38
  370.2 14.8 %collective-permute-start.79 = (f32[2,128,256]{2,1,0:T(8,128)S(1)}, f32[2,128,256]{2,1,0:T(8,128)S(1)}, u32[]{:S(2)}, u32[]{:S(2)}) collective-permute-start(f32[2,128,256]{2,1,0:T(8,128)S(1)} %bitcast.46), channel_id=1, source_target_pairs={{0,2},{1,3},{2,4},{3,5},{4,6},{5,7},{6,0},{7,1},{8,10},{9,11},{10,... | collective-permute-start | bytes 786440 | tf_op jit(solution)/shard_map/ppermute | solution.py:49
  370.8 14.9 %collective-permute-start.82 = (f32[2,128,256]{2,1,0:T(8,128)S(1)}, f32[2,128,256]{2,1,0:T(8,128)S(1)}, u32[]{:S(2)}, u32[]{:S(2)}) collective-permute-start(f32[2,128,256]{2,1,0:T(8,128)S(1)} %bitcast.47), channel_id=1, source_target_pairs={{0,1},{1,0},{2,3},{3,2},{4,5},{5,4},{6,7},{7,6},{8,9},{9,8},{10,11... | collective-permute-start | bytes 786440 | tf_op jit(solution)/shard_map/ppermute | solution.py:53
  (140 other events, 1328.6 us)

commit v2 on v0

v2 whole, which is shorter than its diff:
```python
import jax
import jax.numpy as jnp
from jax import lax
from jax.experimental import pallas as pl
from jax.experimental.pallas import tpu as pltpu
from jax.sharding import PartitionSpec as P

RAD = 8
RZ = 16
ITERS = 2
YD = 4
XD = 4
F32 = jnp.float32
BF16 = jnp.bfloat16
NLAT = 2 * RAD + 1
NAX = 2 * RZ + 1

ANY = pl.BlockSpec(memory_space=pl.ANY)
SMEM = pl.BlockSpec(memory_space=pltpu.SMEM)
VMEM = pl.BlockSpec(memory_space=pltpu.VMEM)
STEPS = (((1, 0), (0, 1)), ((-1, 0), (0, -1)), ((1, 1), (1, -1)), ((-1, -1), (-1, 1)))


def params():
    return pltpu.CompilerParams(vmem_limit_bytes=56 * 1024 * 1024)


def blk_shift(value, dz, dy):
    count = lax.axis_size("blk") // YD
    pairs = [
        (z * YD + y, (z + dz) * YD + y + dy)
        for z in range(count)
        for y in range(YD)
        if 0 <= z + dz < count and 0 <= y + dy < YD
    ]
    return lax.ppermute(value, "blk", pairs)


def core_step(value, steps):
    count = lax.axis_size("blk") // YD
    views = lax.axis_size("view")
    pairs = []
    for z in range(count):
        for y in range(YD):
            for v in range(views):
                dz, dy = steps[v % 2]
                if 0 <= z + dz < count and 0 <= y + dy < YD:
                    target = (z + dz) * YD + y + dy
                    pairs.append(((z * YD + y) * views + v, target * views + v))
    return lax.ppermute(value, ("blk", "view"), pairs)


def y_turn(value, k):
    count = lax.axis_size("blk") // YD
    pairs = [(z * YD + y, z * YD + (y + k) % YD) for z in range(count) for y in range(YD)]
    return lax.ppermute(value, "blk", pairs)


def x_turn(value, k):
    pairs = [(2 * x + c, 2 * ((x + k) % XD) + c) for x in range(XD) for c in range(2)]
    return lax.ppermute(value, "view", pairs)


def core_swap(value):
    return lax.ppermute(value, "view", [(i, i ^ 1) for i in range(2 * XD)])


def split(value):
    high = value.astype(BF16)
    return high, (value - high.astype(F32)).astype(BF16)


def mm(a, b):
    return jnp.dot(a, b, preferred_element_type=F32)


def matrices_kernel(axial_taps, lateral_taps, kyh, kyl, kxh, kxl, kzh, kzl):
    row = lax.broadcasted_iota(jnp.int32, (128, 192), 0)
    col = lax.broadcasted_iota(jnp.int32, (128, 192), 1)
    one = jnp.int32(1)
    zero = jnp.int32(0)
    prow = sum(jnp.where(row >= 32 * n, one, zero) for n in (1, 2, 3))
    pcol = sum(jnp.where(col >= 48 * n, one, zero) for n in (1, 2, 3))
    near = jnp.where(prow == pcol, (col - 48 * pcol) - (row - 32 * prow), -1)

    def offset(shape, sign, shift):
        return shift + sign * (
            lax.broadcasted_iota(jnp.int32, shape, 0) - lax.broadcasted_iota(jnp.int32, shape, 1)
        )

    wide = offset((256, 256), 1, RAD)
    deep = offset((64, 96), -1, 0)

    def total(tap, count):
        return lax.fori_loop(0, count, lambda d, acc: acc + tap(d), jnp.float32(0.0))

    def fill(where, tap, count, high, low):
        norm = total(tap, count)
        for way in range(2):

            def put(d, acc, way=way):
                return jnp.where(where == d, tap(d if way == 0 else count - 1 - d), acc)

            matrix = lax.fori_loop(0, count, put, jnp.zeros(where.shape, F32))
            high[way], low[way] = split(matrix / jnp.full(where.shape, norm))

    fill(near, lambda d: lateral_taps[0, 0, d], NLAT, kyh, kyl)
    fill(wide, lambda d: lateral_taps[0, 1, d], NLAT, kxh, kxl)
    fill(deep, lambda d: axial_taps[0, d], NAX, kzh, kzl)


def matrices(axial_taps, lateral_taps):
    ky = jax.ShapeDtypeStruct((2, 128, 192), BF16)
    kx = jax.ShapeDtypeStruct((2, 256, 256), BF16)
    kz = jax.ShapeDtypeStruct((2, 64, 96), BF16)
    return pl.pallas_call(
        matrices_kernel,
        out_shape=(ky, ky, kx, kx, kz, kz),
        in_specs=[SMEM, SMEM],
        out_specs=(VMEM,) * 6,
        compiler_params=params(),
        name="matrices",
    )(axial_taps, lateral_taps)


def both_halves(ref, group, rows):
    return jnp.concatenate([ref[0, group, rows, :], ref[1, group, rows, :]], axis=1)


def store_halves(ref, group, rows, value):
    ref[0, group, rows, :] = value[:, :128]
    ref[1, group, rows, :] = value[:, 128:]


def blur(way, mats, wide, across, finish):
    kyh, kyl, kxh, kxl, kzh, kzl = [m[way] for m in mats]

    @pl.loop(0, 6)
    def _(b):
        for n in range(4):
            block = wide[b, n // 2, pl.ds(2 * (n % 2), 2)].reshape(192, 256)
            high, low = split(block)
            rows = mm(kyh, high) + (mm(kyl, high) + mm(kyh, low))
            for p in range(4):
                at = pl.ds(pl.multiple_of(128 * b + 32 * n + 8 * p, 8), 8)
                for q in range(4):
                    store_halves(across, q, at, rows[32 * p + 8 * q : 32 * p + 8 * q + 8])

    @pl.loop(0, 8)
    def _(n):
        deep = []
        for r in range(4):
            high, low = split(both_halves(across, n // 2, pl.ds(4 * (n % 2) + r, 96, stride=8)))
            deep.append(mm(kzh, high) + (mm(kzl, high) + mm(kzh, low)))
        high, low = split(jnp.concatenate(deep, axis=0))
        both = mm(high, kxh) + (mm(low, kxh) + mm(high, kxl))
        for r in range(4):
            rows = pl.ds(4 * (n % 2) + r, 64, stride=8)
            finish(n // 2, rows, both[64 * r : 64 * r + 64])


def halo_slot(wide, step):
    dz, dy = step
    b = {1: 0, -1: 5, 0: pl.ds(1, 4)}[dz]
    r = {1: 0, -1: 5, 0: pl.ds(1, 4)}[dy]
    return wide.at[b, :, :, :, r]


def edge_of(tile, step):
    dz, dy = step
    b = {-1: 0, 1: 3, 0: pl.ds(0, 4)}[dz]
    r = {-1: 0, 1: 3, 0: pl.ds(0, 4)}[dy]
    return tile.at[b, :, :, :, r]


def place():
    blk = lax.axis_index("blk")
    view = lax.axis_index("view")
    return blk // YD, blk % YD, view // 2, view % 2


class Copies:
    def __init__(self, sems):
        self.sems = sems
        self.items = []

    def add(self, source, target):
        item = pltpu.make_async_copy(source, target, self.sems.at[len(self.items)])
        item.start()
        self.items.append(item)

    def add_by_core(self, c, pair0, pair1):
        items = [pltpu.make_async_copy(*p, self.sems.at[len(self.items)]) for p in (pair0, pair1)]
        pl.when(c == 0)(items[0].start)
        pl.when(c != 0)(items[1].start)
        self.items.append(items[0])

    def wait(self, first=0, end=None):
        for item in self.items[first:end]:
            item.wait()


TILE = (4, 2, 4, 2, 4, 8, 256)
WIDE = (6, 2, 4, 2, 6, 8, 256)
ZEDGE = (2, 4, 2, 4, 8, 256)
YEDGE = (4, 2, 4, 2, 8, 256)
CORNER = (2, 4, 2, 8, 256)
PART = (4, 2, 4, 8, 256)
RATIO = (4, 4, 2, 4, 2, 8, 256)
RATIO_ZEDGE = (4, 2, 4, 2, 8, 256)
FACES = ((1, 0), (-1, 0), (0, 1), (0, -1))


def grouped(ref, half):
    return ref.at[half].reshape(4, 4, 2, 4, 2, 8, 128)


def put_pieces(copies, pieces, tile, x, c):
    for k in range(4):
        s = (x - k + XD) % XD
        for other in range(2):
            half = c if other == 0 else 1 - c
            copies.add(pieces[4 * other + k], tile(half, s))


def forward_kernel(*refs):
    mats, pieces, halos, shown = refs[:6], refs[6:14], refs[14:26], refs[26:30]
    center, edges = refs[30], refs[31:35]
    wide, across, views, ratio, sems, out_sems = refs[35:]
    z, y, x, c = place()
    copies = Copies(sems)
    put_pieces(copies, pieces, lambda h, s: wide.at[pl.ds(1, 4), h, s, :, pl.ds(1, 4)], x, c)
    for n, steps in enumerate(STEPS):
        if n < 2:
            own, got = halos[4 * n : 4 * n + 2], halos[4 * n + 2 : 4 * n + 4]
        else:
            own, got = (halos[4 + 2 * n],) * 2, (halos[5 + 2 * n],) * 2
        slots = [halo_slot(wide, step) for step in steps]
        copies.add_by_core(c, (own[0], slots[0]), (got[0], slots[0]))
        copies.add_by_core(c, (got[1], slots[1]), (own[1], slots[1]))
    for k in range(4):
        b = (y - k + YD) % YD
        for half in range(2):
            copies.add(shown[k].at[..., pl.ds(128 * half, 128)], grouped(views, half).at[:, b])
    copies.wait()

    def finish(group, rows, value):
        store_halves(ratio, group, rows, both_halves(views, group, rows) / value)

    blur(0, mats, wide, across, finish)
    copies = Copies(out_sems)
    for half in range(2):
        tile = grouped(ratio, half)
        lanes = pl.ds(128 * half, 128)
        for n, edge in enumerate((tile.at[:, 3], tile.at[:, 0], tile.at[3], tile.at[0])):
            copies.add(edge, edges[n].at[..., lanes])
        copies.add(tile, center.at[..., lanes])
    copies.wait()


def forward(mats, pieces, halos, shown):
    shapes = (RATIO, RATIO_ZEDGE, RATIO_ZEDGE, YEDGE, YEDGE)
    got = pl.pallas_call(
        forward_kernel,
        out_shape=tuple(jax.ShapeDtypeStruct(s, F32) for s in shapes),
        in_specs=[VMEM] * 6 + [ANY] * 24,
        out_specs=(ANY,) * 5,
        scratch_shapes=[
            pltpu.VMEM(WIDE, F32),
            pltpu.VMEM((2, 4, 768, 128), F32),
            pltpu.VMEM((2, 4, 512, 128), F32),
            pltpu.VMEM((2, 4, 512, 128), F32),
            pltpu.SemaphoreType.DMA((24,)),
            pltpu.SemaphoreType.DMA((10,)),
        ],
        compiler_params=params(),
        name="forward",
    )(*mats, *pieces, *halos, *shown)
    return got[0], got[1:]


def backward_kernel(cover, *refs):
    mats, center, halos, strips = refs[:6], refs[6], refs[7:11], refs[11:13]
    mine, other = refs[13:15]
    wide, across, logs, sems, out_sems = refs[15:]
    z, y, x, c = place()
    copies = Copies(sems)
    for q in range(4):
        copies.add(center.at[q], wide.at[pl.ds(1, 4), :, :, :, 1 + q])
        for n in range(2):
            copies.add(halos[n].at[q], wide.at[5 * n, :, :, :, 1 + q])
    for n in range(2, 4):
        copies.add(halos[n], halo_slot(wide, FACES[n]))
    for n, dy in enumerate((1, -1)):
        for m, dz in enumerate((1, -1)):
            copies.add(strips[n].at[m], halo_slot(wide, (dz, dy)))
    copies.wait()
    plane = z * 64 + lax.broadcasted_iota(jnp.int32, (64, 256), 0)
    inside = jnp.logical_and(plane >= cover[0, 0], plane < cover[0, 1])

    def finish(group, rows, value):
        store_halves(logs, group, rows, jnp.where(inside, jnp.log(value), jnp.float32(0.0)))

    blur(1, mats, wide, across, finish)
    copies = Copies(out_sems)
    for half in range(2):
        tile = grouped(logs, half)
        lanes = pl.ds(128 * half, 128)
        for q in range(4):
            copies.add(tile.at[q, :, 1 - c], other.at[:, :, :, q, :, lanes])
            copies.add(tile.at[q, :, c], mine.at[:, :, :, q, :, lanes])
    copies.wait()


def backward(cover, mats, center, halos, strips):
    half = jax.ShapeDtypeStruct((4,) + PART, F32)
    return pl.pallas_call(
        backward_kernel,
        out_shape=(half, half),
        in_specs=[SMEM] + [VMEM] * 6 + [ANY] * 7,
        out_specs=(ANY, ANY),
        scratch_shapes=[
            pltpu.VMEM(WIDE, F32),
            pltpu.VMEM((2, 4, 768, 128), F32),
            pltpu.VMEM((2, 4, 512, 128), F32),
            pltpu.SemaphoreType.DMA((18,)),
            pltpu.SemaphoreType.DMA((16,)),
        ],
        compiler_params=params(),
        name="backward",
    )(cover, *mats, center, *halos, *strips)


def shares_kernel(mine, got, *outs):
    z, y, x, c = place()
    for k in range(4):
        s = (x + k) % XD
        outs[k][...] = mine[:, s] + got[:, s]


def shares(mine, got):
    part = jax.ShapeDtypeStruct(PART, F32)
    return pl.pallas_call(
        shares_kernel,
        out_shape=(part,) * 4,
        in_specs=[VMEM, VMEM],
        out_specs=(VMEM,) * 4,
        compiler_params=params(),
        name="shares",
    )(mine, got)


def edges_kernel(*refs):
    pieces, outs = refs[:8], refs[8:12]
    tile, sems, out_sems = refs[12:]
    z, y, x, c = place()
    copies = Copies(sems)
    put_pieces(copies, pieces, lambda h, s: tile.at[:, h, s], x, c)
    copies.wait()
    copies = Copies(out_sems)
    for n, (step0, step1) in enumerate(STEPS):
        out1 = outs[n].reshape(*YEDGE) if n < 2 else outs[n]
        copies.add_by_core(c, (edge_of(tile, step0), outs[n]), (edge_of(tile, step1), out1))
    copies.wait()


def edges(pieces):
    return pl.pallas_call(
        edges_kernel,
        out_shape=tuple(jax.ShapeDtypeStruct(s, F32) for s in (ZEDGE, ZEDGE, CORNER, CORNER)),
        in_specs=[ANY] * 8,
        out_specs=(ANY,) * 4,
        scratch_shapes=[
            pltpu.VMEM(TILE, F32),
            pltpu.SemaphoreType.DMA((8,)),
            pltpu.SemaphoreType.DMA((4,)),
        ],
        compiler_params=params(),
        name="edges",
    )(*pieces)


def slab_kernel(*refs):
    pieces, out = refs[:8], refs[8]
    slab, sems, out_sems = refs[9:]
    z, y, x, c = place()
    copies = Copies(sems)
    put_pieces(copies, pieces, lambda h, s: slab.at[h, s], x, c)
    copies.wait()
    copies = Copies(out_sems)
    copies.add(slab, out)
    copies.wait()


def slab(pieces):
    return pl.pallas_call(
        slab_kernel,
        out_shape=jax.ShapeDtypeStruct((2, 4, 2, 128, 256), F32),
        in_specs=[ANY] * 8,
        out_specs=ANY,
        scratch_shapes=[
            pltpu.VMEM((2, 4, 2, 128, 256), F32),
            pltpu.SemaphoreType.DMA((8,)),
            pltpu.SemaphoreType.DMA((1,)),
        ],
        compiler_params=params(),
        name="slab",
    )(*pieces)


def by_block(pieces, y):
    order = [pieces[0], pieces[3], pieces[2], pieces[1]]
    stack = jnp.stack(order + order[:3])
    return lax.dynamic_slice_in_dim(stack, (YD - y) % YD, 4, axis=0)


def gathered(share):
    return [share] + [x_turn(share, k) for k in (1, 2, 3)]


def local(estimate, views, axial_taps, lateral_taps, cover):
    z, y, x, c = place()

    def rows_for(value, k, axis):
        return lax.dynamic_slice_in_dim(value, 32 * ((y + k) % YD), 32, axis=axis)

    own = lax.dynamic_slice_in_dim(estimate, 8 * c + 2 * x, 2, axis=0)
    parts = [rows_for(own, 0, 1)] + [y_turn(rows_for(own, k, 1), k) for k in (1, 2, 3)]
    share = by_block(parts, y).reshape(PART)
    mats = matrices(axial_taps, lateral_taps)
    def view_rows(k):
        rows = lax.dynamic_slice_in_dim(views[0].reshape(16, 16, 8, 256), 4 * ((y + k) % YD), 4, axis=1)
        return jnp.transpose(rows, (1, 0, 2, 3)).reshape(4, 2, 4, 2, 8, 256)

    shown = [view_rows(k) for k in range(4)]
    share, *rest = lax.optimization_barrier((share, *mats, *shown))
    mats, shown = rest[:6], rest[6:]
    shown = [shown[0]] + [y_turn(shown[k], k) for k in (1, 2, 3)]
    for step in range(ITERS):
        pieces = gathered(share)
        pieces = pieces + [core_swap(piece) for piece in pieces]
        if step == 0:
            pieces, shown = lax.optimization_barrier((pieces, shown))
        halos = []
        rims = [core_step(edge, steps) for edge, steps in zip(edges(pieces), STEPS)]
        rims = lax.optimization_barrier(rims)
        for n, moved in enumerate(rims):
            for value in (moved, core_swap(moved)):
                halos += [value, value.reshape(YEDGE)] if n < 2 else [value]
        center, rims = forward(mats, pieces, halos, shown)
        halos = [blk_shift(e, *d) for e, d in zip(rims, FACES)]
        low, high = halos[0], halos[1]
        strips = [blk_shift(jnp.stack([low[r], high[r]]), 0, dy) for r, dy in ((3, 1), (0, -1))]
        mine, other = backward(cover, mats, center, halos, strips)
        terms = shares(mine, core_swap(other))
        total = terms[0]
        for k in (1, 2, 3):
            total = total + x_turn(terms[k], k)
        share = share * jnp.exp(total)
    share = share.reshape(4, 2, 32, 256)
    parts = [lax.dynamic_index_in_dim(share, (y + k) % YD, 0, keepdims=False) for k in range(4)]
    parts = [parts[0]] + [y_turn(parts[k], k) for k in (1, 2, 3)]
    strip = by_block(parts, y)
    strip = jnp.transpose(strip, (1, 0, 2, 3)).reshape(2, 128, 256)
    pieces = gathered(strip)
    pieces = pieces + [core_swap(piece) for piece in pieces]
    return slab(pieces).reshape(16, 128, 256)


def solution(mesh):
    in_specs = (
        P("blk", None, None),
        P("view", "blk", None, None),
        P("view", None),
        P("view", None, None),
        P("view", None),
    )
    out_specs = P("blk", None, None)
    return jax.shard_map(local, mesh=mesh, in_specs=in_specs, out_specs=out_specs, check_vma=False)
```

time: 531 us -> 333 us (0.63)
  the two profiles are of different devices: /device:TPU:8 before, /device:TPU:97 now
where the time goes in v2:
time: 333 us; the launch traced here: 326 us
  starting transfers between devices  129 us (39%)
  waiting for transfers between devices  115 us (35%)
  Pallas kernels  66.6 us (20%)
  local copies, waits for them, and re-layouts  12.4 us (4%)
    ppermute x22, starting transfers between devices, core_swap(): return lax.ppermute(value, 'view', [(i, i ^ 1) for i in range(2 * XD)])  54.5 us
    ppermute x15, waiting for transfers between devices, x_turn(): return lax.ppermute(value, 'view', pairs)  41 us
    ppermute x12, waiting for transfers between devices, blk_shift(): return lax.ppermute(value, 'blk', pairs)  32.8 us
    ppermute x12, starting transfers between devices, blk_shift(): return lax.ppermute(value, 'blk', pairs)  25.5 us
    pallas_call x2, Pallas kernels, forward(): pl.pallas_call(forward_kernel, out_shape=tuple((jax.ShapeDtypeStruct(s, F...  25.2 us
    pallas_call x2, Pallas kernels, backward(): pl.pallas_call(backward_kernel, out_shape=(half, half), in_specs=[SMEM] +...  22.6 us
    ppermute x8, starting transfers between devices, core_step(): return lax.ppermute(value, ('blk', 'view'), pairs)  20.7 us
    ppermute x9, waiting for transfers between devices, y_turn(): return lax.ppermute(value, 'blk', pairs)  20.7 us
  transfers between devices with their start and end apart: 66, of which 37 were waited for; matrix products, arithmetic and copies ran while one was open for 1% of the time, Pallas kernels for 2%

profile of v2, /device:TPU:97, one launch (start us, length us, event | category | flops | bytes accessed | tf_op | source)
XLA Modules:
  0.0 326.1 jit_solution(10760435933730462653)
XLA Ops:
  8.1 5.2 %matrices.1 = (bf16[2,128,192]{2,1,0:T(8,128)(2,1)}, bf16[2,128,192]{2,1,0:T(8,128)(2,1)}, bf16[2,256,256]{2,1,0:T(8,128)(2,1)}, bf16[2,256,256]{2,1,0:T(8,128)(...) custom-call(f32[1,33]{1,0:T(1,128)} %axial_taps.1, f32[1,2,17]{2,1,0:T(2,128)} %lateral_taps.1), custom_call_target="tpu_custom_call" | custom-call | tf_op jit(solution)/shard_map/matrices/pallas_call | solution.py:116
  22.3 7.7 %collective-permute-start.9 = (f32[4,2,4,8,256]{4,3,2,1,0:T(8,128)S(1)}, f32[4,2,4,8,256]{4,3,2,1,0:T(8,128)S(1)}, u32[]{:S(2)}, u32[]{:S(2)}) collective-permute-start(f32[4,2,4,8,256]{4,3,2,1,0:T(8,128)S(1)} %collective-permute-done.5.refs_3_.refs_9_), channel_id=1, source_target_pairs={{0,1},{1,0},{2,3},{3,2},{4,5},{5,4},{6,7},{7,6},{8,9},{9,8},{10,11... | collective-permute-start | bytes 786440 | tf_op jit(solution)/shard_map/ppermute | solution.py:65
  37.0 8.6 %collective-permute-done.11.refs_28_ = f32[4,2,4,2,8,256]{5,4,3,2,1,0:T(8,128)S(1)} collective-permute-done((f32[4,2,4,2,8,256]{5,4,3,2,1,0:T(8,128)S(1)}, f32[4,2,4,2,8,256]{5,4,3,2,1,0:T(8,128)S(1)}, u32[]{:S(2)}, u32[]{:S(2)}) %collective-permute-start.11) | collective-permute-done | bytes 524320 | tf_op jit(solution)/shard_map/ppermute | solution.py:56
  45.6 8.9 %collective-permute-done.12.refs_29_ = f32[4,2,4,2,8,256]{5,4,3,2,1,0:T(8,128)S(1)} collective-permute-done((f32[4,2,4,2,8,256]{5,4,3,2,1,0:T(8,128)S(1)}, f32[4,2,4,2,8,256]{5,4,3,2,1,0:T(8,128)S(1)}, u32[]{:S(2)}, u32[]{:S(2)}) %collective-permute-start.12) | collective-permute-done | bytes 524320 | tf_op jit(solution)/shard_map/ppermute | solution.py:56
  63.1 4.9 %collective-permute-start.16 = (f32[2,4,2,8,256]{4,3,2,1,0:T(8,128)}, f32[2,4,2,8,256]{4,3,2,1,0:T(8,128)S(1)}, u32[]{:S(2)}, u32[]{:S(2)}) collective-permute-start(f32[2,4,2,8,256]{4,3,2,1,0:T(8,128)} %get-tuple-element.100), channel_id=1, source_target_pairs={{33,9},{35,11},{37,13},{39,15},{40,0},{41,17},{42,2},{43,19},{44,4... | collective-permute-start | bytes 393224 | tf_op jit(solution)/shard_map/ppermute | solution.py:50
  72.4 8.5 %collective-permute-start.17 = (f32[2,4,2,4,8,256]{5,4,3,2,1,0:T(8,128)S(1)}, f32[2,4,2,4,8,256]{5,4,3,2,1,0:T(8,128)S(1)}, u32[]{:S(2)}, u32[]{:S(2)}) collective-permute-start(f32[2,4,2,4,8,256]{5,4,3,2,1,0:T(8,128)S(1)} %collective-permute-done.13.refs_14_), channel_id=1, source_target_pairs={{0,1},{1,0},{2,3},{3,2},{4,5},{5,4},{6,7},{7,6},{8,9},{9,8},{10,11... | collective-permute-start | bytes 1572872 | tf_op jit(solution)/shard_map/ppermute | solution.py:65
  84.5 12.6 %forward.2 = (f32[4,4,2,4,2,8,256]{6,5,4,3,2,1,0:T(8,128)}, f32[4,2,4,2,8,256]{5,4,3,2,1,0:T(8,128)}, f32[4,2,4,2,8,256]{5,4,3,2,1,0:T(8,128)}, f32[4,2,4,2,8,256]{5,4,3,2,1,0:T(8,128)}, f32[4,2,4,2,8,256]{5,4,3,2,1,0:T(8,128)}) custom-call(bf16[2,128,192]{2,1,0:T(8,128)(2,1)} %get-tuple-element.79.refs_0_, bf16[2,128,192]{2,1,0:T(8,128)(2,1)} %get-tuple-element.80.refs_1_, ...), custom_call_target="tpu_custom_call" | custom-call | tf_op jit(solution)/shard_map/forward/pallas_call | solution.py:263
  106.7 5.7 %collective-permute-done.21.refs_7_ = f32[4,2,4,2,8,256]{5,4,3,2,1,0:T(8,128)S(1)} collective-permute-done((f32[4,2,4,2,8,256]{5,4,3,2,1,0:T(8,128)}, f32[4,2,4,2,8,256]{5,4,3,2,1,0:T(8,128)S(1)}, u32[]{:S(2)}, u32[]{:S(2)}) %collective-permute-start.21) | collective-permute-done | bytes 524320 | tf_op jit(solution)/shard_map/ppermute | solution.py:36
  122.9 3.9 %collective-permute-done.26.refs_12_ = f32[2,2,4,2,8,256]{5,4,3,2,1,0:T(8,128)S(1)} collective-permute-done((f32[2,2,4,2,8,256]{5,4,3,2,1,0:T(8,128)S(1)}, f32[2,2,4,2,8,256]{5,4,3,2,1,0:T(8,128)S(1)}, u32[]{:S(2)}, u32[]{:S(2)}) %collective-permute-start.26) | collective-permute-done | bytes 262176 | tf_op jit(solution)/shard_map/ppermute | solution.py:36
  127.5 11.3 %backward.2 = (f32[4,4,2,4,8,256]{5,4,3,2,1,0:T(8,128)}, f32[4,4,2,4,8,256]{5,4,3,2,1,0:T(8,128)}) custom-call(s32[1,2]{1,0:T(1,128)} %cover.3, bf16[2,128,192]{2,1,0:T(8,128)(2,1)} %get-tuple-element.79.refs_0_, bf16[2,128,192]{2,1,0:T(8,128)(2,1)} %get-tuple-element.80.refs_1_, bf16[2,256,256]{2,1,0:T(8,128)(2,1)} %get-tuple-element.81.refs_2_, ...), custom_call_target="tpu_custom_call" | custom-call | tf_op jit(solution)/shard_map/backward/pallas_call | solution.py:317
  147.4 4.6 %collective-permute-start.29 = (f32[4,2,4,8,256]{4,3,2,1,0:T(8,128)}, f32[4,2,4,8,256]{4,3,2,1,0:T(8,128)S(1)}, u32[]{:S(2)}, u32[]{:S(2)}) collective-permute-start(f32[4,2,4,8,256]{4,3,2,1,0:T(8,128)} %get-tuple-element.118), channel_id=1, source_target_pairs={{0,4},{1,5},{2,6},{3,7},{4,0},{5,1},{6,2},{7,3},{8,12},{9,13},{10,... | collective-permute-start | bytes 786440 | tf_op jit(solution)/shard_map/ppermute | solution.py:61
  151.9 5.4 %collective-permute-done.28 = f32[4,2,4,8,256]{4,3,2,1,0:T(8,128)S(1)} collective-permute-done((f32[4,2,4,8,256]{4,3,2,1,0:T(8,128)}, f32[4,2,4,8,256]{4,3,2,1,0:T(8,128)S(1)}, u32[]{:S(2)}, u32[]{:S(2)}) %collective-permute-start.28) | collective-permute-done | bytes 262176 | tf_op jit(solution)/shard_map/ppermute | solution.py:61
  157.3 6.5 %collective-permute-done.29 = f32[4,2,4,8,256]{4,3,2,1,0:T(8,128)S(1)} collective-permute-done((f32[4,2,4,8,256]{4,3,2,1,0:T(8,128)}, f32[4,2,4,8,256]{4,3,2,1,0:T(8,128)S(1)}, u32[]{:S(2)}, u32[]{:S(2)}) %collective-permute-start.29) | collective-permute-done | bytes 262176 | tf_op jit(solution)/shard_map/ppermute | solution.py:61
  169.2 5.0 %collective-permute-done.33.refs_3_.refs_9_ = f32[4,2,4,8,256]{4,3,2,1,0:T(8,128)S(1)} collective-permute-done((f32[4,2,4,8,256]{4,3,2,1,0:T(8,128)S(1)}, f32[4,2,4,8,256]{4,3,2,1,0:T(8,128)S(1)}, u32[]{:S(2)}, u32[]{:S(2)}) %collective-permute-start.33) | collective-permute-done | bytes 262176 | tf_op jit(solution)/shard_map/ppermute | solution.py:61
  174.2 5.4 %collective-permute-start.37 = (f32[4,2,4,8,256]{4,3,2,1,0:T(8,128)S(1)}, f32[4,2,4,8,256]{4,3,2,1,0:T(8,128)S(1)}, u32[]{:S(2)}, u32[]{:S(2)}) collective-permute-start(f32[4,2,4,8,256]{4,3,2,1,0:T(8,128)S(1)} %collective-permute-done.33.refs_3_.refs_9_), channel_id=1, source_target_pairs={{0,1},{1,0},{2,3},{3,2},{4,5},{5,4},{6,7},{7,6},{8,9},{9,8},{10,11... | collective-permute-start | bytes 786440 | tf_op jit(solution)/shard_map/ppermute | solution.py:65
  192.9 4.9 %collective-permute-start.41 = (f32[2,4,2,8,256]{4,3,2,1,0:T(8,128)}, f32[2,4,2,8,256]{4,3,2,1,0:T(8,128)S(1)}, u32[]{:S(2)}, u32[]{:S(2)}) collective-permute-start(f32[2,4,2,8,256]{4,3,2,1,0:T(8,128)} %get-tuple-element.123), channel_id=1, source_target_pairs={{33,9},{35,11},{37,13},{39,15},{40,0},{41,17},{42,2},{43,19},{44,4... | collective-permute-start | bytes 393224 | tf_op jit(solution)/shard_map/ppermute | solution.py:50
  202.1 4.6 %collective-permute-start.42 = (f32[2,4,2,4,8,256]{5,4,3,2,1,0:T(8,128)S(1)}, f32[2,4,2,4,8,256]{5,4,3,2,1,0:T(8,128)S(1)}, u32[]{:S(2)}, u32[]{:S(2)}) collective-permute-start(f32[2,4,2,4,8,256]{5,4,3,2,1,0:T(8,128)S(1)} %collective-permute-done.38.refs_14_), channel_id=1, source_target_pairs={{0,1},{1,0},{2,3},{3,2},{4,5},{5,4},{6,7},{7,6},{8,9},{9,8},{10,11... | collective-permute-start | bytes 1572872 | tf_op jit(solution)/shard_map/ppermute | solution.py:65
  207.2 8.8 %collective-permute-start.45 = (f32[2,4,2,8,256]{4,3,2,1,0:T(8,128)S(1)}, f32[2,4,2,8,256]{4,3,2,1,0:T(8,128)S(1)}, u32[]{:S(2)}, u32[]{:S(2)}) collective-permute-start(f32[2,4,2,8,256]{4,3,2,1,0:T(8,128)S(1)} %collective-permute-done.41.refs_24_), channel_id=1, source_target_pairs={{0,1},{1,0},{2,3},{3,2},{4,5},{5,4},{6,7},{7,6},{8,9},{9,8},{10,11... | collective-permute-start | bytes 393224 | tf_op jit(solution)/shard_map/ppermute | solution.py:65
  218.3 12.6 %forward.3 = (f32[4,4,2,4,2,8,256]{6,5,4,3,2,1,0:T(8,128)}, f32[4,2,4,2,8,256]{5,4,3,2,1,0:T(8,128)}, f32[4,2,4,2,8,256]{5,4,3,2,1,0:T(8,128)}, f32[4,2,4,2,8,256]{5,4,3,2,1,0:T(8,128)}, f32[4,2,4,2,8,256]{5,4,3,2,1,0:T(8,128)}) custom-call(bf16[2,128,192]{2,1,0:T(8,128)(2,1)} %get-tuple-element.79.refs_0_, bf16[2,128,192]{2,1,0:T(8,128)(2,1)} %get-tuple-element.80.refs_1_, ...), custom_call_target="tpu_custom_call" | custom-call | tf_op jit(solution)/shard_map/forward/pallas_call | solution.py:263
  239.4 6.9 %collective-permute-done.46.refs_7_ = f32[4,2,4,2,8,256]{5,4,3,2,1,0:T(8,128)S(1)} collective-permute-done((f32[4,2,4,2,8,256]{5,4,3,2,1,0:T(8,128)}, f32[4,2,4,2,8,256]{5,4,3,2,1,0:T(8,128)S(1)}, u32[]{:S(2)}, u32[]{:S(2)}) %collective-permute-start.46) | collective-permute-done | bytes 524320 | tf_op jit(solution)/shard_map/ppermute | solution.py:36
  260.6 11.3 %backward.3 = (f32[4,4,2,4,8,256]{5,4,3,2,1,0:T(8,128)}, f32[4,4,2,4,8,256]{5,4,3,2,1,0:T(8,128)}) custom-call(s32[1,2]{1,0:T(1,128)} %cover.3, bf16[2,128,192]{2,1,0:T(8,128)(2,1)} %get-tuple-element.79.refs_0_, bf16[2,128,192]{2,1,0:T(8,128)(2,1)} %get-tuple-element.80.refs_1_, bf16[2,256,256]{2,1,0:T(8,128)(2,1)} %get-tuple-element.81.refs_2_, ...), custom_call_target="tpu_custom_call" | custom-call | tf_op jit(solution)/shard_map/backward/pallas_call | solution.py:317
  283.0 6.7 %collective-permute-done.53 = f32[4,2,4,8,256]{4,3,2,1,0:T(8,128)S(1)} collective-permute-done((f32[4,2,4,8,256]{4,3,2,1,0:T(8,128)}, f32[4,2,4,8,256]{4,3,2,1,0:T(8,128)S(1)}, u32[]{:S(2)}, u32[]{:S(2)}) %collective-permute-start.53) | collective-permute-done | bytes 262176 | tf_op jit(solution)/shard_map/ppermute | solution.py:61
  289.7 4.7 %collective-permute-done.54 = f32[4,2,4,8,256]{4,3,2,1,0:T(8,128)S(1)} collective-permute-done((f32[4,2,4,8,256]{4,3,2,1,0:T(8,128)}, f32[4,2,4,8,256]{4,3,2,1,0:T(8,128)S(1)}, u32[]{:S(2)}, u32[]{:S(2)}) %collective-permute-start.54) | collective-permute-done | bytes 262176 | tf_op jit(solution)/shard_map/ppermute | solution.py:61
  312.1 5.3 %collective-permute-start.65 = (f32[2,128,256]{2,1,0:T(8,128)S(1)}, f32[2,128,256]{2,1,0:T(8,128)S(1)}, u32[]{:S(2)}, u32[]{:S(2)}) collective-permute-start(f32[2,128,256]{2,1,0:T(8,128)S(1)} %collective-permute-done.61.refs_3_), channel_id=1, source_target_pairs={{0,1},{1,0},{2,3},{3,2},{4,5},{5,4},{6,7},{7,6},{8,9},{9,8},{10,11... | collective-permute-start | bytes 786440 | tf_op jit(solution)/shard_map/ppermute | solution.py:65
  (269 shorter events, 154.9 us)
Async XLA Ops:
  1.0 13.3 %collective-permute-start.2 = (f32[2,32,256]{2,1,0:T(8,128)S(1)}, f32[2,32,256]{2,1,0:T(8,128)S(1)}, u32[]{:S(2)}, u32[]{:S(2)}) collective-permute-start(f32[2,32,256]{2,1,0:T(8,128)S(1)} %get-tuple-element.143), channel_id=1, source_target_pairs={{0,8},{8,16},{16,24},{24,0},{32,40},{40,48},{48,56},{56,32},{64,72... | collective-permute-start | bytes 196616 | tf_op jit(solution)/shard_map/ppermute | solution.py:56
  20.2 14.9 %collective-permute-start.3 = (f32[4,2,4,8,256]{4,3,2,1,0:T(8,128)S(1)}, f32[4,2,4,8,256]{4,3,2,1,0:T(8,128)S(1)}, u32[]{:S(2)}, u32[]{:S(2)}) collective-permute-start(f32[4,2,4,8,256]{4,3,2,1,0:T(8,128)S(1)} %dynamic-slice_bitcast_fusion.refs_0_.refs_6_), channel_id=1, source_target_pairs={{0,2},{1,3},{2,4},{3,5},{4,6},{5,7},{6,0},{7,1},{8,10},{9,11},{10,... | collective-permute-start | bytes 786440 | tf_op jit(solution)/shard_map/ppermute | solution.py:61
  20.8 16.3 %collective-permute-start.10 = (f32[4,2,4,2,8,256]{5,4,3,2,1,0:T(8,128)S(1)}, f32[4,2,4,2,8,256]{5,4,3,2,1,0:T(8,128)S(1)}, u32[]{:S(2)}, u32[]{:S(2)}) collective-permute-start(f32[4,2,4,2,8,256]{5,4,3,2,1,0:T(8,128)S(1)} %bitcast.75), channel_id=1, source_target_pairs={{0,8},{8,16},{16,24},{24,0},{32,40},{40,48},{48,56},{56,32},{64,72... | collective-permute-start | bytes 1572872 | tf_op jit(solution)/shard_map/ppermute | solution.py:56
  22.3 13.2 %collective-permute-start.9 = (f32[4,2,4,8,256]{4,3,2,1,0:T(8,128)S(1)}, f32[4,2,4,8,256]{4,3,2,1,0:T(8,128)S(1)}, u32[]{:S(2)}, u32[]{:S(2)}) collective-permute-start(f32[4,2,4,8,256]{4,3,2,1,0:T(8,128)S(1)} %collective-permute-done.5.refs_3_.refs_9_), channel_id=1, source_target_pairs={{0,1},{1,0},{2,3},{3,2},{4,5},{5,4},{6,7},{7,6},{8,9},{9,8},{10,11... | collective-permute-start | bytes 786440 | tf_op jit(solution)/shard_map/ppermute | solution.py:65
  30.0 15.6 %collective-permute-start.11 = (f32[4,2,4,2,8,256]{5,4,3,2,1,0:T(8,128)S(1)}, f32[4,2,4,2,8,256]{5,4,3,2,1,0:T(8,128)S(1)}, u32[]{:S(2)}, u32[]{:S(2)}) collective-permute-start(f32[4,2,4,2,8,256]{5,4,3,2,1,0:T(8,128)S(1)} %bitcast.74), channel_id=1, source_target_pairs={{0,16},{8,24},{16,0},{24,8},{32,48},{40,56},{48,32},{56,40},{64,80... | collective-permute-start | bytes 1572872 | tf_op jit(solution)/shard_map/ppermute | solution.py:56
  31.4 23.1 %collective-permute-start.12 = (f32[4,2,4,2,8,256]{5,4,3,2,1,0:T(8,128)S(1)}, f32[4,2,4,2,8,256]{5,4,3,2,1,0:T(8,128)S(1)}, u32[]{:S(2)}, u32[]{:S(2)}) collective-permute-start(f32[4,2,4,2,8,256]{5,4,3,2,1,0:T(8,128)S(1)} %bitcast.73), channel_id=1, source_target_pairs={{0,24},{8,0},{16,8},{24,16},{32,56},{40,32},{48,40},{56,48},{64,88... | collective-permute-start | bytes 1572872 | tf_op jit(solution)/shard_map/ppermute | solution.py:56
  57.4 14.3 %collective-permute-start.13 = (f32[2,4,2,4,8,256]{5,4,3,2,1,0:T(8,128)}, f32[2,4,2,4,8,256]{5,4,3,2,1,0:T(8,128)S(1)}, u32[]{:S(2)}, u32[]{:S(2)}) collective-permute-start(f32[2,4,2,4,8,256]{5,4,3,2,1,0:T(8,128)} %get-tuple-element.97), channel_id=1, source_target_pairs={{0,32},{1,9},{2,34},{3,11},{4,36},{5,13},{6,38},{7,15},{8,40},{9,1... | collective-permute-start | bytes 1572872 | tf_op jit(solution)/shard_map/ppermute | solution.py:50
  97.2 15.2 %collective-permute-start.21 = (f32[4,2,4,2,8,256]{5,4,3,2,1,0:T(8,128)}, f32[4,2,4,2,8,256]{5,4,3,2,1,0:T(8,128)S(1)}, u32[]{:S(2)}, u32[]{:S(2)}) collective-permute-start(f32[4,2,4,2,8,256]{5,4,3,2,1,0:T(8,128)} %get-tuple-element.110), channel_id=1, source_target_pairs={{0,32},{8,40},{16,48},{24,56},{32,64},{40,72},{48,80},{56,88},{64,... | collective-permute-start | bytes 1572872 | tf_op jit(solution)/shard_map/ppermute | solution.py:36
  99.1 16.5 %collective-permute-start.22 = (f32[4,2,4,2,8,256]{5,4,3,2,1,0:T(8,128)}, f32[4,2,4,2,8,256]{5,4,3,2,1,0:T(8,128)S(1)}, u32[]{:S(2)}, u32[]{:S(2)}) collective-permute-start(f32[4,2,4,2,8,256]{5,4,3,2,1,0:T(8,128)} %get-tuple-element.111), channel_id=1, source_target_pairs={{32,0},{40,8},{48,16},{56,24},{64,32},{72,40},{80,48},{88,56},{96,... | collective-permute-start | bytes 1572872 | tf_op jit(solution)/shard_map/ppermute | solution.py:36
  102.5 17.4 %collective-permute-start.23 = (f32[4,2,4,2,8,256]{5,4,3,2,1,0:T(8,128)}, f32[4,2,4,2,8,256]{5,4,3,2,1,0:T(8,128)S(1)}, u32[]{:S(2)}, u32[]{:S(2)}) collective-permute-start(f32[4,2,4,2,8,256]{5,4,3,2,1,0:T(8,128)} %get-tuple-element.112), channel_id=1, source_target_pairs={{0,8},{8,16},{16,24},{32,40},{40,48},{48,56},{64,72},{72,80},{80,8... | collective-permute-start | bytes 1572872 | tf_op jit(solution)/shard_map/ppermute | solution.py:36
  105.4 14.5 %collective-permute-start.24 = (f32[4,2,4,2,8,256]{5,4,3,2,1,0:T(8,128)}, f32[4,2,4,2,8,256]{5,4,3,2,1,0:T(8,128)S(1)}, u32[]{:S(2)}, u32[]{:S(2)}) collective-permute-start(f32[4,2,4,2,8,256]{5,4,3,2,1,0:T(8,128)} %get-tuple-element.113), channel_id=1, source_target_pairs={{8,0},{16,8},{24,16},{40,32},{48,40},{56,48},{72,64},{80,72},{88,8... | collective-permute-start | bytes 1572872 | tf_op jit(solution)/shard_map/ppermute | solution.py:36
  147.4 16.4 %collective-permute-start.29 = (f32[4,2,4,8,256]{4,3,2,1,0:T(8,128)}, f32[4,2,4,8,256]{4,3,2,1,0:T(8,128)S(1)}, u32[]{:S(2)}, u32[]{:S(2)}) collective-permute-start(f32[4,2,4,8,256]{4,3,2,1,0:T(8,128)} %get-tuple-element.118), channel_id=1, source_target_pairs={{0,4},{1,5},{2,6},{3,7},{4,0},{5,1},{6,2},{7,3},{8,12},{9,13},{10,... | collective-permute-start | bytes 786440 | tf_op jit(solution)/shard_map/ppermute | solution.py:61
  167.5 14.7 %collective-permute-start.31 = (f32[4,2,4,8,256]{4,3,2,1,0:T(8,128)S(1)}, f32[4,2,4,8,256]{4,3,2,1,0:T(8,128)S(1)}, u32[]{:S(2)}, u32[]{:S(2)}) collective-permute-start(f32[4,2,4,8,256]{4,3,2,1,0:T(8,128)S(1)} %exponential_multiply_fusion.refs_0_.refs_6_), channel_id=1, source_target_pairs={{0,2},{1,3},{2,4},{3,5},{4,6},{5,7},{6,0},{7,1},{8,10},{9,11},{10,... | collective-permute-start | bytes 786440 | tf_op jit(solution)/shard_map/ppermute | solution.py:61
  168.1 14.9 %collective-permute-start.34 = (f32[4,2,4,8,256]{4,3,2,1,0:T(8,128)S(1)}, f32[4,2,4,8,256]{4,3,2,1,0:T(8,128)S(1)}, u32[]{:S(2)}, u32[]{:S(2)}) collective-permute-start(f32[4,2,4,8,256]{4,3,2,1,0:T(8,128)S(1)} %exponential_multiply_fusion.refs_0_.refs_6_), channel_id=1, source_target_pairs={{0,1},{1,0},{2,3},{3,2},{4,5},{5,4},{6,7},{7,6},{8,9},{9,8},{10,11... | collective-permute-start | bytes 786440 | tf_op jit(solution)/shard_map/ppermute | solution.py:65
  187.6 13.9 %collective-permute-start.38 = (f32[2,4,2,4,8,256]{5,4,3,2,1,0:T(8,128)}, f32[2,4,2,4,8,256]{5,4,3,2,1,0:T(8,128)S(1)}, u32[]{:S(2)}, u32[]{:S(2)}) collective-permute-start(f32[2,4,2,4,8,256]{5,4,3,2,1,0:T(8,128)} %get-tuple-element.120), channel_id=1, source_target_pairs={{0,32},{1,9},{2,34},{3,11},{4,36},{5,13},{6,38},{7,15},{8,40},{9,1... | collective-permute-start | bytes 1572872 | tf_op jit(solution)/shard_map/ppermute | solution.py:50
  202.1 15.1 %collective-permute-start.42 = (f32[2,4,2,4,8,256]{5,4,3,2,1,0:T(8,128)S(1)}, f32[2,4,2,4,8,256]{5,4,3,2,1,0:T(8,128)S(1)}, u32[]{:S(2)}, u32[]{:S(2)}) collective-permute-start(f32[2,4,2,4,8,256]{5,4,3,2,1,0:T(8,128)S(1)} %collective-permute-done.38.refs_14_), channel_id=1, source_target_pairs={{0,1},{1,0},{2,3},{3,2},{4,5},{5,4},{6,7},{7,6},{8,9},{9,8},{10,11... | collective-permute-start | bytes 1572872 | tf_op jit(solution)/shard_map/ppermute | solution.py:65
  230.9 15.5 %collective-permute-start.46 = (f32[4,2,4,2,8,256]{5,4,3,2,1,0:T(8,128)}, f32[4,2,4,2,8,256]{5,4,3,2,1,0:T(8,128)S(1)}, u32[]{:S(2)}, u32[]{:S(2)}) collective-permute-start(f32[4,2,4,2,8,256]{5,4,3,2,1,0:T(8,128)} %get-tuple-element.129), channel_id=1, source_target_pairs={{0,32},{8,40},{16,48},{24,56},{32,64},{40,72},{48,80},{56,88},{64,... | collective-permute-start | bytes 1572872 | tf_op jit(solution)/shard_map/ppermute | solution.py:36
  232.8 16.7 %collective-permute-start.47 = (f32[4,2,4,2,8,256]{5,4,3,2,1,0:T(8,128)}, f32[4,2,4,2,8,256]{5,4,3,2,1,0:T(8,128)S(1)}, u32[]{:S(2)}, u32[]{:S(2)}) collective-permute-start(f32[4,2,4,2,8,256]{5,4,3,2,1,0:T(8,128)} %get-tuple-element.130), channel_id=1, source_target_pairs={{32,0},{40,8},{48,16},{56,24},{64,32},{72,40},{80,48},{88,56},{96,... | collective-permute-start | bytes 1572872 | tf_op jit(solution)/shard_map/ppermute | solution.py:36
  236.2 16.6 %collective-permute-start.48 = (f32[4,2,4,2,8,256]{5,4,3,2,1,0:T(8,128)}, f32[4,2,4,2,8,256]{5,4,3,2,1,0:T(8,128)S(1)}, u32[]{:S(2)}, u32[]{:S(2)}) collective-permute-start(f32[4,2,4,2,8,256]{5,4,3,2,1,0:T(8,128)} %get-tuple-element.131), channel_id=1, source_target_pairs={{0,8},{8,16},{16,24},{32,40},{40,48},{48,56},{64,72},{72,80},{80,8... | collective-permute-start | bytes 1572872 | tf_op jit(solution)/shard_map/ppermute | solution.py:36
  238.1 14.7 %collective-permute-start.49 = (f32[4,2,4,2,8,256]{5,4,3,2,1,0:T(8,128)}, f32[4,2,4,2,8,256]{5,4,3,2,1,0:T(8,128)S(1)}, u32[]{:S(2)}, u32[]{:S(2)}) collective-permute-start(f32[4,2,4,2,8,256]{5,4,3,2,1,0:T(8,128)} %get-tuple-element.132), channel_id=1, source_target_pairs={{8,0},{16,8},{24,16},{40,32},{48,40},{56,48},{72,64},{80,72},{88,8... | collective-permute-start | bytes 1572872 | tf_op jit(solution)/shard_map/ppermute | solution.py:36
  280.3 14.1 %collective-permute-start.54 = (f32[4,2,4,8,256]{4,3,2,1,0:T(8,128)}, f32[4,2,4,8,256]{4,3,2,1,0:T(8,128)S(1)}, u32[]{:S(2)}, u32[]{:S(2)}) collective-permute-start(f32[4,2,4,8,256]{4,3,2,1,0:T(8,128)} %get-tuple-element.137), channel_id=1, source_target_pairs={{0,4},{1,5},{2,6},{3,7},{4,0},{5,1},{6,2},{7,3},{8,12},{9,13},{10,... | collective-permute-start | bytes 786440 | tf_op jit(solution)/shard_map/ppermute | solution.py:61
  282.5 12.7 %collective-permute-start.55 = (f32[4,2,4,8,256]{4,3,2,1,0:T(8,128)}, f32[4,2,4,8,256]{4,3,2,1,0:T(8,128)S(1)}, u32[]{:S(2)}, u32[]{:S(2)}) collective-permute-start(f32[4,2,4,8,256]{4,3,2,1,0:T(8,128)} %get-tuple-element.138), channel_id=1, source_target_pairs={{0,6},{1,7},{2,0},{3,1},{4,2},{5,3},{6,4},{7,5},{8,14},{9,15},{10,... | collective-permute-start | bytes 786440 | tf_op jit(solution)/shard_map/ppermute | solution.py:61
  305.5 15.0 %collective-permute-start.59 = (f32[2,128,256]{2,1,0:T(8,128)S(1)}, f32[2,128,256]{2,1,0:T(8,128)S(1)}, u32[]{:S(2)}, u32[]{:S(2)}) collective-permute-start(f32[2,128,256]{2,1,0:T(8,128)S(1)} %bitcast.70), channel_id=1, source_target_pairs={{0,2},{1,3},{2,4},{3,5},{4,6},{5,7},{6,0},{7,1},{8,10},{9,11},{10,... | collective-permute-start | bytes 786440 | tf_op jit(solution)/shard_map/ppermute | solution.py:61
  305.9 15.2 %collective-permute-start.62 = (f32[2,128,256]{2,1,0:T(8,128)S(1)}, f32[2,128,256]{2,1,0:T(8,128)S(1)}, u32[]{:S(2)}, u32[]{:S(2)}) collective-permute-start(f32[2,128,256]{2,1,0:T(8,128)S(1)} %bitcast.71), channel_id=1, source_target_pairs={{0,1},{1,0},{2,3},{3,2},{4,5},{5,4},{6,7},{7,6},{8,9},{9,8},{10,11... | collective-permute-start | bytes 786440 | tf_op jit(solution)/shard_map/ppermute | solution.py:65
  (101 other events, 967.2 us)

commit v3 on v2

--- a/solution.py
+++ b/solution.py
@@ -1,3 +1,5 @@
+import functools
+
 import jax
 import jax.numpy as jnp
 from jax import lax
@@ -75,34 +77,38 @@
 
 
 def matrices_kernel(axial_taps, lateral_taps, kyh, kyl, kxh, kxl, kzh, kzl):
-    row = lax.broadcasted_iota(jnp.int32, (128, 192), 0)
-    col = lax.broadcasted_iota(jnp.int32, (128, 192), 1)
     one = jnp.int32(1)
     zero = jnp.int32(0)
-    prow = sum(jnp.where(row >= 32 * n, one, zero) for n in (1, 2, 3))
-    pcol = sum(jnp.where(col >= 48 * n, one, zero) for n in (1, 2, 3))
-    near = jnp.where(prow == pcol, (col - 48 * pcol) - (row - 32 * prow), -1)
-
-    def offset(shape, sign, shift):
-        return shift + sign * (
-            lax.broadcasted_iota(jnp.int32, shape, 0) - lax.broadcasted_iota(jnp.int32, shape, 1)
-        )
-
-    wide = offset((256, 256), 1, RAD)
-    deep = offset((64, 96), -1, 0)
-
-    def total(tap, count):
-        return lax.fori_loop(0, count, lambda d, acc: acc + tap(d), jnp.float32(0.0))
+
+    def iota(shape, axis):
+        return lax.broadcasted_iota(jnp.int32, shape, axis)
+
+    def near(shape, start):
+        row, col = iota(shape, 0), iota(shape, 1)
+        pcol = sum(jnp.where(col >= 48 * n, one, zero) for n in (1, 2, 3))
+        return jnp.where(pcol == start // 32, (col - 48 * pcol) - (row + start % 32), -1)
+
+    def wide(shape, start):
+        return iota(shape, 0) + start - iota(shape, 1) + RAD
+
+    def deep(shape, start):
+        return iota(shape, 1) - iota(shape, 0) - start
 
     def fill(where, tap, count, high, low):
-        norm = total(tap, count)
-        for way in range(2):
-
-            def put(d, acc, way=way):
-                return jnp.where(where == d, tap(d if way == 0 else count - 1 - d), acc)
-
-            matrix = lax.fori_loop(0, count, put, jnp.zeros(where.shape, F32))
-            high[way], low[way] = split(matrix / jnp.full(where.shape, norm))
+        taps = [tap(d) for d in range(count)]
+        norm = sum(taps[1:], taps[0])
+        shape = (16, high.shape[2])
+
+        @pl.loop(0, high.shape[1] // 16)
+        def _(n):
+            start = pl.multiple_of(16 * n, 16)
+            offset = where(shape, start)
+            for way in range(2):
+                matrix = jnp.zeros(shape, F32)
+                for d in range(count):
+                    matrix = jnp.where(offset == (d if way == 0 else count - 1 - d), taps[d], matrix)
+                matrix = matrix / jnp.full(shape, norm)
+                high[way, pl.ds(start, 16)], low[way, pl.ds(start, 16)] = split(matrix)
 
     fill(near, lambda d: lateral_taps[0, 0, d], NLAT, kyh, kyl)
     fill(wide, lambda d: lateral_taps[0, 1, d], NLAT, kxh, kxl)
@@ -132,11 +138,10 @@
     ref[1, group, rows, :] = value[:, 128:]
 
 
-def blur(way, mats, wide, across, finish):
+def blur(way, mats, wide, across, inner, outer, ready, finish, done):
     kyh, kyl, kxh, kxl, kzh, kzl = [m[way] for m in mats]
 
-    @pl.loop(0, 6)
-    def _(b):
+    def over_rows(b):
         for n in range(4):
             block = wide[b, n // 2, pl.ds(2 * (n % 2), 2)].reshape(192, 256)
             high, low = split(block)
@@ -146,17 +151,28 @@
                 for q in range(4):
                     store_halves(across, q, at, rows[32 * p + 8 * q : 32 * p + 8 * q + 8])
 
+    inner()
+    pl.loop(1, 5)(over_rows)
+    outer()
+    pl.loop(0, 2)(lambda n: over_rows(5 * n))
+    ready()
+
     @pl.loop(0, 8)
     def _(n):
+        q = n // 2
+        r0 = 4 * (n % 2)
         deep = []
         for r in range(4):
-            high, low = split(both_halves(across, n // 2, pl.ds(4 * (n % 2) + r, 96, stride=8)))
+            high, low = split(both_halves(across, q, pl.ds(r0 + r, 96, stride=8)))
             deep.append(mm(kzh, high) + (mm(kzl, high) + mm(kzh, low)))
         high, low = split(jnp.concatenate(deep, axis=0))
         both = mm(high, kxh) + (mm(low, kxh) + mm(high, kxl))
         for r in range(4):
-            rows = pl.ds(4 * (n % 2) + r, 64, stride=8)
-            finish(n // 2, rows, both[64 * r : 64 * r + 64])
+            finish(q, pl.ds(r0 + r, 64, stride=8), both[64 * r : 64 * r + 64])
+
+        @pl.when(r0 > 0)
+        def _():
+            done(q)
 
 
 def halo_slot(wide, step):
@@ -188,6 +204,7 @@
         item = pltpu.make_async_copy(source, target, self.sems.at[len(self.items)])
         item.start()
         self.items.append(item)
+        return len(self.items)
 
     def add_by_core(self, c, pair0, pair1):
         items = [pltpu.make_async_copy(*p, self.sems.at[len(self.items)]) for p in (pair0, pair1)]
@@ -215,55 +232,83 @@
     return ref.at[half].reshape(4, 4, 2, 4, 2, 8, 128)
 
 
-def put_pieces(copies, pieces, tile, x, c):
+def put_pieces(copies, first, pieces, tile):
+    z, y, x, c = place()
     for k in range(4):
-        s = (x - k + XD) % XD
         for other in range(2):
             half = c if other == 0 else 1 - c
-            copies.add(pieces[4 * other + k], tile(half, s))
-
-
-def forward_kernel(*refs):
-    mats, pieces, halos, shown = refs[:6], refs[6:14], refs[14:26], refs[26:30]
-    center, edges = refs[30], refs[31:35]
-    wide, across, views, ratio, sems, out_sems = refs[35:]
+            if first:
+                slot = tile((y - k + YD) % YD, half, pl.ds(0, 4))
+            else:
+                slot = tile(pl.ds(0, 4), half, (x - k + XD) % XD)
+            copies.add(pieces[4 * other + k], slot)
+
+
+def forward_kernel(first, *refs):
+    mats, pieces, moved, got, shown = refs[:6], refs[6:14], refs[14:18], refs[18], refs[19:23]
+    center, edges = refs[23], refs[24:28]
+    wide, across, views, ratio, sems, group_sems, out_sems = refs[28:]
     z, y, x, c = place()
     copies = Copies(sems)
-    put_pieces(copies, pieces, lambda h, s: wide.at[pl.ds(1, 4), h, s, :, pl.ds(1, 4)], x, c)
-    for n, steps in enumerate(STEPS):
-        if n < 2:
-            own, got = halos[4 * n : 4 * n + 2], halos[4 * n + 2 : 4 * n + 4]
-        else:
-            own, got = (halos[4 + 2 * n],) * 2, (halos[5 + 2 * n],) * 2
-        slots = [halo_slot(wide, step) for step in steps]
-        copies.add_by_core(c, (own[0], slots[0]), (got[0], slots[0]))
-        copies.add_by_core(c, (got[1], slots[1]), (own[1], slots[1]))
+    middle = wide.at[pl.ds(1, 4)]
+    put_pieces(copies, first, pieces, lambda b, h, s: middle.at[b, h, s, :, pl.ds(1, 4)])
+    for n, (step0, step1) in enumerate(STEPS):
+        shapes = (ZEDGE, YEDGE) if n < 2 else (CORNER, CORNER)
+        start, size = ((64 * n, 64) if n < 2 else (96 + 16 * n, 16))
+        theirs = got.at[pl.ds(start, size)]
+        slot0, slot1 = halo_slot(wide, step0), halo_slot(wide, step1)
+        copies.add_by_core(c, (moved[n], slot0), (theirs.reshape(*shapes[0]), slot0))
+        copies.add_by_core(c, (theirs.reshape(*shapes[1]), slot1), (moved[n].reshape(*shapes[1]), slot1))
+    count = len(copies.items)
     for k in range(4):
         b = (y - k + YD) % YD
         for half in range(2):
             copies.add(shown[k].at[..., pl.ds(128 * half, 128)], grouped(views, half).at[:, b])
-    copies.wait()
 
     def finish(group, rows, value):
         store_halves(ratio, group, rows, both_halves(views, group, rows) / value)
 
-    blur(0, mats, wide, across, finish)
+    def group_copies(q):
+        for half in range(2):
+            tile = grouped(ratio, half).at[q]
+            lanes = pl.ds(128 * half, 128)
+            for n, (source, target) in enumerate(((3, edges[0]), (0, edges[1]), (None, center))):
+                source = tile if source is None else tile.at[source]
+                yield pltpu.make_async_copy(source, target.at[q, ..., lanes], group_sems.at[q, half, n])
+
+    def done(q):
+        for item in group_copies(q):
+            item.start()
+
+    blur(
+        0,
+        mats,
+        wide,
+        across,
+        lambda: copies.wait(0, count),
+        lambda: None,
+        lambda: copies.wait(count),
+        finish,
+        done,
+    )
     copies = Copies(out_sems)
     for half in range(2):
         tile = grouped(ratio, half)
         lanes = pl.ds(128 * half, 128)
-        for n, edge in enumerate((tile.at[:, 3], tile.at[:, 0], tile.at[3], tile.at[0])):
+        for n, edge in ((2, tile.at[3]), (3, tile.at[0])):
             copies.add(edge, edges[n].at[..., lanes])
-        copies.add(tile, center.at[..., lanes])
+    for q in range(4):
+        for item in group_copies(q):
+            item.wait()
     copies.wait()
 
 
-def forward(mats, pieces, halos, shown):
+def forward(first, mats, pieces, moved, got, shown):
     shapes = (RATIO, RATIO_ZEDGE, RATIO_ZEDGE, YEDGE, YEDGE)
     got = pl.pallas_call(
-        forward_kernel,
+        functools.partial(forward_kernel, first),
         out_shape=tuple(jax.ShapeDtypeStruct(s, F32) for s in shapes),
-        in_specs=[VMEM] * 6 + [ANY] * 24,
+        in_specs=[VMEM] * 6 + [ANY] * 17,
         out_specs=(ANY,) * 5,
         scratch_shapes=[
             pltpu.VMEM(WIDE, F32),
@@ -271,11 +316,12 @@
             pltpu.VMEM((2, 4, 512, 128), F32),
             pltpu.VMEM((2, 4, 512, 128), F32),
             pltpu.SemaphoreType.DMA((24,)),
-            pltpu.SemaphoreType.DMA((10,)),
+            pltpu.SemaphoreType.DMA((4, 2, 3)),
+            pltpu.SemaphoreType.DMA((4,)),
         ],
         compiler_params=params(),
         name="forward",
-    )(*mats, *pieces, *halos, *shown)
+    )(*mats, *pieces, *moved, got, *shown)
     return got[0], got[1:]
 
 
@@ -285,31 +331,48 @@
     wide, across, logs, sems, out_sems = refs[15:]
     z, y, x, c = place()
     copies = Copies(sems)
+    for n in range(2, 4):
+        copies.add(halos[n], halo_slot(wide, FACES[n]))
     for q in range(4):
-        copies.add(center.at[q], wide.at[pl.ds(1, 4), :, :, :, 1 + q])
+        count = copies.add(center.at[q], wide.at[pl.ds(1, 4), :, :, :, 1 + q])
+    for q in range(4):
         for n in range(2):
             copies.add(halos[n].at[q], wide.at[5 * n, :, :, :, 1 + q])
-    for n in range(2, 4):
-        copies.add(halos[n], halo_slot(wide, FACES[n]))
     for n, dy in enumerate((1, -1)):
         for m, dz in enumerate((1, -1)):
             copies.add(strips[n].at[m], halo_slot(wide, (dz, dy)))
-    copies.wait()
     plane = z * 64 + lax.broadcasted_iota(jnp.int32, (64, 256), 0)
     inside = jnp.logical_and(plane >= cover[0, 0], plane < cover[0, 1])
 
     def finish(group, rows, value):
         store_halves(logs, group, rows, jnp.where(inside, jnp.log(value), jnp.float32(0.0)))
 
-    blur(1, mats, wide, across, finish)
-    copies = Copies(out_sems)
-    for half in range(2):
-        tile = grouped(logs, half)
-        lanes = pl.ds(128 * half, 128)
-        for q in range(4):
-            copies.add(tile.at[q, :, 1 - c], other.at[:, :, :, q, :, lanes])
-            copies.add(tile.at[q, :, c], mine.at[:, :, :, q, :, lanes])
-    copies.wait()
+    def group_copies(q):
+        for half in range(2):
+            tile = grouped(logs, half).at[q]
+            lanes = pl.ds(128 * half, 128)
+            for n, (core, target) in enumerate(((1 - c, other), (c, mine))):
+                target = target.at[:, :, :, q, :, lanes]
+                yield pltpu.make_async_copy(tile.at[:, core], target, out_sems.at[q, half, n])
+
+    def done(q):
+        for item in group_copies(q):
+            item.start()
+
+    blur(
+        1,
+        mats,
+        wide,
+        across,
+        lambda: copies.wait(0, count),
+        lambda: copies.wait(count),
+        lambda: None,
+        finish,
+        done,
+    )
+    for q in range(4):
+        for item in group_copies(q):
+            item.wait()
 
 
 def backward(cover, mats, center, halos, strips):
@@ -324,7 +387,7 @@
             pltpu.VMEM((2, 4, 768, 128), F32),
             pltpu.VMEM((2, 4, 512, 128), F32),
             pltpu.SemaphoreType.DMA((18,)),
-            pltpu.SemaphoreType.DMA((16,)),
+            pltpu.SemaphoreType.DMA((4, 2, 2)),
         ],
         compiler_params=params(),
         name="backward",
@@ -350,12 +413,12 @@
     )(mine, got)
 
 
-def edges_kernel(*refs):
+def edges_kernel(first, *refs):
     pieces, outs = refs[:8], refs[8:12]
     tile, sems, out_sems = refs[12:]
     z, y, x, c = place()
     copies = Copies(sems)
-    put_pieces(copies, pieces, lambda h, s: tile.at[:, h, s], x, c)
+    put_pieces(copies, first, pieces, lambda b, h, s: tile.at[b, h, s])
     copies.wait()
     copies = Copies(out_sems)
     for n, (step0, step1) in enumerate(STEPS):
@@ -364,9 +427,9 @@
     copies.wait()
 
 
-def edges(pieces):
+def edges(first, pieces):
     return pl.pallas_call(
-        edges_kernel,
+        functools.partial(edges_kernel, first),
         out_shape=tuple(jax.ShapeDtypeStruct(s, F32) for s in (ZEDGE, ZEDGE, CORNER, CORNER)),
         in_specs=[ANY] * 8,
         out_specs=(ANY,) * 4,
@@ -385,7 +448,7 @@
     slab, sems, out_sems = refs[9:]
     z, y, x, c = place()
     copies = Copies(sems)
-    put_pieces(copies, pieces, lambda h, s: slab.at[h, s], x, c)
+    put_pieces(copies, False, pieces, lambda b, h, s: slab.at[h, s])
     copies.wait()
     copies = Copies(out_sems)
     copies.add(slab, out)
@@ -421,33 +484,30 @@
 def local(estimate, views, axial_taps, lateral_taps, cover):
     z, y, x, c = place()
 
-    def rows_for(value, k, axis):
-        return lax.dynamic_slice_in_dim(value, 32 * ((y + k) % YD), 32, axis=axis)
-
-    own = lax.dynamic_slice_in_dim(estimate, 8 * c + 2 * x, 2, axis=0)
-    parts = [rows_for(own, 0, 1)] + [y_turn(rows_for(own, k, 1), k) for k in (1, 2, 3)]
-    share = by_block(parts, y).reshape(PART)
-    mats = matrices(axial_taps, lateral_taps)
+    def est_rows(k):
+        half = lax.dynamic_slice_in_dim(estimate, 8 * c, 8, axis=0)
+        rows = lax.dynamic_slice_in_dim(half, 32 * ((y + k) % YD), 32, axis=1)
+        return rows.reshape(PART)
+
     def view_rows(k):
         rows = lax.dynamic_slice_in_dim(views[0].reshape(16, 16, 8, 256), 4 * ((y + k) % YD), 4, axis=1)
         return jnp.transpose(rows, (1, 0, 2, 3)).reshape(4, 2, 4, 2, 8, 256)
 
+    pieces = [est_rows(0)] + [y_turn(est_rows(k), k) for k in (1, 2, 3)]
+    share = by_block([lax.dynamic_index_in_dim(p, x, 0, keepdims=False) for p in pieces], y)
+    mats = matrices(axial_taps, lateral_taps)
     shown = [view_rows(k) for k in range(4)]
-    share, *rest = lax.optimization_barrier((share, *mats, *shown))
-    mats, shown = rest[:6], rest[6:]
+    pieces, mats, shown = lax.optimization_barrier((pieces, mats, shown))
     shown = [shown[0]] + [y_turn(shown[k], k) for k in (1, 2, 3)]
     for step in range(ITERS):
-        pieces = gathered(share)
+        if step > 0:
+            pieces = gathered(share)
         pieces = pieces + [core_swap(piece) for piece in pieces]
+        rims = [core_step(e, steps) for e, steps in zip(edges(step == 0, pieces), STEPS)]
         if step == 0:
-            pieces, shown = lax.optimization_barrier((pieces, shown))
-        halos = []
-        rims = [core_step(edge, steps) for edge, steps in zip(edges(pieces), STEPS)]
-        rims = lax.optimization_barrier(rims)
-        for n, moved in enumerate(rims):
-            for value in (moved, core_swap(moved)):
-                halos += [value, value.reshape(YEDGE)] if n < 2 else [value]
-        center, rims = forward(mats, pieces, halos, shown)
+            rims, shown = lax.optimization_barrier((rims, shown))
+        swapped = core_swap(jnp.concatenate([rim.reshape(-1, 8, 256) for rim in rims]))
+        center, rims = forward(step == 0, mats, pieces, rims, swapped, shown)
         halos = [blk_shift(e, *d) for e, d in zip(rims, FACES)]
         low, high = halos[0], halos[1]
         strips = [blk_shift(jnp.stack([low[r], high[r]]), 0, dy) for r, dy in ((3, 1), (0, -1))]

time: 333 us -> 305 us (0.916); the launches traced: 326 us -> 303 us
  starting transfers between devices: 129 us -> 105 us
  Pallas kernels: 66.6 us -> 60.3 us
  waiting for transfers between devices: 115 us -> 120 us
    ppermute x22 -> x16, starting transfers between devices: 54.5 us -> 24.3 us  [core_swap(): return lax.ppermute(value, 'view', [(i, i ^ 1) for i in range(2 * XD)])]
    ppermute x9, waiting for transfers between devices: 20.7 us -> 33.7 us  [y_turn(): return lax.ppermute(value, 'blk', pairs)]
    ppermute x15 -> x12, waiting for transfers between devices: 41 us -> 34.4 us  [x_turn(): return lax.ppermute(value, 'view', pairs)]
    ppermute x9, starting transfers between devices: 10.4 us -> 15.3 us  [y_turn(): return lax.ppermute(value, 'blk', pairs)]
    ppermute x12, starting transfers between devices: 25.5 us -> 29.7 us  [blk_shift(): return lax.ppermute(value, 'blk', pairs)]
    ppermute x12, waiting for transfers between devices: 32.8 us -> 28.7 us  [blk_shift(): return lax.ppermute(value, 'blk', pairs)]
    ppermute x22 -> x16, waiting for transfers between devices: 11.8 us -> 14.3 us  [core_swap(): return lax.ppermute(value, 'view', [(i, i ^ 1) for i in range(2 * XD)])]
    unnamed x134 -> x128, local copies, waits for them, and re-layouts: 9.59 us -> 12 us
  transfers between devices with their start and end apart: 66 -> 57, of which waited for: 37 -> 41; matrix products, arithmetic and copies ran while one was open for 1% -> 1% of each run, Pallas kernels for 2% -> 1%
where the time goes in v3:
time: 305 us; the launch traced here: 303 us
  waiting for transfers between devices  120 us (39%)
  starting transfers between devices  105 us (34%)
  Pallas kernels  60.3 us (20%)
  local copies, waits for them, and re-layouts  14.7 us (5%)
    ppermute x12, waiting for transfers between devices, x_turn(): return lax.ppermute(value, 'view', pairs)  34.4 us
    ppermute x9, waiting for transfers between devices, y_turn(): return lax.ppermute(value, 'blk', pairs)  33.7 us
    ppermute x12, starting transfers between devices, blk_shift(): return lax.ppermute(value, 'blk', pairs)  29.7 us
    ppermute x12, waiting for transfers between devices, blk_shift(): return lax.ppermute(value, 'blk', pairs)  28.7 us
    ppermute x16, starting transfers between devices, core_swap(): return lax.ppermute(value, 'view', [(i, i ^ 1) for i in range(2 * XD)])  24.3 us
    pallas_call x2, Pallas kernels, forward(): pl.pallas_call(functools.partial(forward_kernel, first), out_shape=tuple(...  22.8 us
    pallas_call x2, Pallas kernels, backward(): pl.pallas_call(backward_kernel, out_shape=(half, half), in_specs=[SMEM] +...  21 us
    ppermute x8, starting transfers between devices, core_step(): return lax.ppermute(value, ('blk', 'view'), pairs)  18 us
  transfers between devices with their start and end apart: 57, of which 41 were waited for; matrix products, arithmetic and copies ran while one was open for 1% of the time, Pallas kernels for 1%

profile of v3, /device:TPU:97, one launch (start us, length us, event | category | flops | bytes accessed | tf_op | source)
XLA Modules:
  0.0 302.9 jit_solution(13264354236607160217)
XLA Ops:
  13.8 6.6 %collective-permute-done.2.refs_1_.refs_7_ = f32[4,2,4,8,256]{4,3,2,1,0:T(8,128)S(1)} collective-permute-done((f32[4,2,4,8,256]{4,3,2,1,0:T(8,128)S(1)}, f32[4,2,4,8,256]{4,3,2,1,0:T(8,128)S(1)}, u32[]{:S(2)}, u32[]{:S(2)}) %collective-permute-start.2) | collective-permute-done | bytes 262176 | tf_op jit(solution)/shard_map/ppermute | solution.py:58
  29.6 4.7 %collective-permute-start.11 = (f32[4,2,4,2,8,256]{5,4,3,2,1,0:T(8,128)S(1)}, f32[4,2,4,2,8,256]{5,4,3,2,1,0:T(8,128)S(1)}, u32[]{:S(2)}, u32[]{:S(2)}) collective-permute-start(f32[4,2,4,2,8,256]{5,4,3,2,1,0:T(8,128)S(1)} %bitcast.67), channel_id=1, source_target_pairs={{0,8},{8,16},{16,24},{24,0},{32,40},{40,48},{48,56},{56,32},{64,72... | collective-permute-start | bytes 1572872 | tf_op jit(solution)/shard_map/ppermute | solution.py:58
  40.9 6.2 %collective-permute-done.11.refs_20_ = f32[4,2,4,2,8,256]{5,4,3,2,1,0:T(8,128)S(1)} collective-permute-done((f32[4,2,4,2,8,256]{5,4,3,2,1,0:T(8,128)S(1)}, f32[4,2,4,2,8,256]{5,4,3,2,1,0:T(8,128)S(1)}, u32[]{:S(2)}, u32[]{:S(2)}) %collective-permute-start.11) | collective-permute-done | bytes 524320 | tf_op jit(solution)/shard_map/ppermute | solution.py:58
  47.1 13.2 %collective-permute-done.12.refs_21_ = f32[4,2,4,2,8,256]{5,4,3,2,1,0:T(8,128)S(1)} collective-permute-done((f32[4,2,4,2,8,256]{5,4,3,2,1,0:T(8,128)S(1)}, f32[4,2,4,2,8,256]{5,4,3,2,1,0:T(8,128)S(1)}, u32[]{:S(2)}, u32[]{:S(2)}) %collective-permute-start.12) | collective-permute-done | bytes 524320 | tf_op jit(solution)/shard_map/ppermute | solution.py:58
  60.3 3.9 %collective-permute-done.7.refs_14_ = f32[2,4,2,4,8,256]{5,4,3,2,1,0:T(8,128)S(1)} collective-permute-done((f32[2,4,2,4,8,256]{5,4,3,2,1,0:T(8,128)}, f32[2,4,2,4,8,256]{5,4,3,2,1,0:T(8,128)S(1)}, u32[]{:S(2)}, u32[]{:S(2)}) %collective-permute-start.7) | collective-permute-done | bytes 524320 | tf_op jit(solution)/shard_map/ppermute | solution.py:52
  69.9 11.4 %forward.2 = (f32[4,4,2,4,2,8,256]{6,5,4,3,2,1,0:T(8,128)}, f32[4,2,4,2,8,256]{5,4,3,2,1,0:T(8,128)}, f32[4,2,4,2,8,256]{5,4,3,2,1,0:T(8,128)}, f32[4,2,4,2,8,256]{5,4,3,2,1,0:T(8,128)}, f32[4,2,4,2,8,256]{5,4,3,2,1,0:T(8,128)}) custom-call(bf16[2,128,192]{2,1,0:T(8,128)(2,1)} %get-tuple-element.69.refs_0_, bf16[2,128,192]{2,1,0:T(8,128)(2,1)} %get-tuple-element.70.refs_1_, ...), custom_call_target="tpu_custom_call" | custom-call | tf_op jit(solution)/shard_map/forward/pallas_call | solution.py:308
  81.2 4.4 %collective-permute-start.15 = (f32[4,2,4,2,8,256]{5,4,3,2,1,0:T(8,128)}, f32[4,2,4,2,8,256]{5,4,3,2,1,0:T(8,128)S(1)}, u32[]{:S(2)}, u32[]{:S(2)}) collective-permute-start(f32[4,2,4,2,8,256]{5,4,3,2,1,0:T(8,128)} %get-tuple-element.96), channel_id=1, source_target_pairs={{0,32},{8,40},{16,48},{24,56},{32,64},{40,72},{48,80},{56,88},{64,... | collective-permute-start | bytes 1572872 | tf_op jit(solution)/shard_map/ppermute | solution.py:38
  91.3 5.9 %collective-permute-done.15.refs_7_ = f32[4,2,4,2,8,256]{5,4,3,2,1,0:T(8,128)S(1)} collective-permute-done((f32[4,2,4,2,8,256]{5,4,3,2,1,0:T(8,128)}, f32[4,2,4,2,8,256]{5,4,3,2,1,0:T(8,128)S(1)}, u32[]{:S(2)}, u32[]{:S(2)}) %collective-permute-start.15) | collective-permute-done | bytes 524320 | tf_op jit(solution)/shard_map/ppermute | solution.py:38
  97.2 4.9 %collective-permute-done.16.refs_8_ = f32[4,2,4,2,8,256]{5,4,3,2,1,0:T(8,128)S(1)} collective-permute-done((f32[4,2,4,2,8,256]{5,4,3,2,1,0:T(8,128)}, f32[4,2,4,2,8,256]{5,4,3,2,1,0:T(8,128)S(1)}, u32[]{:S(2)}, u32[]{:S(2)}) %collective-permute-start.16) | collective-permute-done | bytes 524320 | tf_op jit(solution)/shard_map/ppermute | solution.py:38
  103.4 4.0 %collective-permute-start.19 = (f32[2,2,4,2,8,256]{5,4,3,2,1,0:T(8,128)S(1)}, f32[2,2,4,2,8,256]{5,4,3,2,1,0:T(8,128)S(1)}, u32[]{:S(2)}, u32[]{:S(2)}) collective-permute-start(f32[2,2,4,2,8,256]{5,4,3,2,1,0:T(8,128)S(1)} %pad_maximum_fusion.2), channel_id=1, source_target_pairs={{0,8},{8,16},{16,24},{32,40},{40,48},{48,56},{64,72},{72,80},{80,8... | collective-permute-start | bytes 786440 | tf_op jit(solution)/shard_map/ppermute | solution.py:38
  112.2 10.5 %backward.2 = (f32[4,4,2,4,8,256]{5,4,3,2,1,0:T(8,128)}, f32[4,4,2,4,8,256]{5,4,3,2,1,0:T(8,128)}) custom-call(s32[1,2]{1,0:T(1,128)} %cover.3, bf16[2,128,192]{2,1,0:T(8,128)(2,1)} %get-tuple-element.69.refs_0_, bf16[2,128,192]{2,1,0:T(8,128)(2,1)} %get-tuple-element.70.refs_1_, bf16[2,256,256]{2,1,0:T(8,128)(2,1)} %get-tuple-element.71.refs_2_, ...), custom_call_target="tpu_custom_call" | custom-call | tf_op jit(solution)/shard_map/backward/pallas_call | solution.py:380
  136.4 4.1 %collective-permute-done.22 = f32[4,2,4,8,256]{4,3,2,1,0:T(8,128)S(1)} collective-permute-done((f32[4,2,4,8,256]{4,3,2,1,0:T(8,128)}, f32[4,2,4,8,256]{4,3,2,1,0:T(8,128)S(1)}, u32[]{:S(2)}, u32[]{:S(2)}) %collective-permute-start.22) | collective-permute-done | bytes 262176 | tf_op jit(solution)/shard_map/ppermute | solution.py:63
  140.5 6.6 %collective-permute-done.23 = f32[4,2,4,8,256]{4,3,2,1,0:T(8,128)S(1)} collective-permute-done((f32[4,2,4,8,256]{4,3,2,1,0:T(8,128)}, f32[4,2,4,8,256]{4,3,2,1,0:T(8,128)S(1)}, u32[]{:S(2)}, u32[]{:S(2)}) %collective-permute-start.23) | collective-permute-done | bytes 262176 | tf_op jit(solution)/shard_map/ppermute | solution.py:63
  158.2 5.5 %collective-permute-done.26.refs_2_.refs_8_ = f32[4,2,4,8,256]{4,3,2,1,0:T(8,128)S(1)} collective-permute-done((f32[4,2,4,8,256]{4,3,2,1,0:T(8,128)S(1)}, f32[4,2,4,8,256]{4,3,2,1,0:T(8,128)S(1)}, u32[]{:S(2)}, u32[]{:S(2)}) %collective-permute-start.26) | collective-permute-done | bytes 262176 | tf_op jit(solution)/shard_map/ppermute | solution.py:63
  170.3 4.1 %collective-permute-start.32 = (f32[2,4,2,4,8,256]{5,4,3,2,1,0:T(8,128)}, f32[2,4,2,4,8,256]{5,4,3,2,1,0:T(8,128)S(1)}, u32[]{:S(2)}, u32[]{:S(2)}) collective-permute-start(f32[2,4,2,4,8,256]{5,4,3,2,1,0:T(8,128)} %get-tuple-element.106), channel_id=1, source_target_pairs={{0,32},{1,9},{2,34},{3,11},{4,36},{5,13},{6,38},{7,15},{8,40},{9,1... | collective-permute-start | bytes 1572872 | tf_op jit(solution)/shard_map/ppermute | solution.py:52
  177.0 4.9 %collective-permute-start.35 = (f32[2,4,2,8,256]{4,3,2,1,0:T(8,128)}, f32[2,4,2,8,256]{4,3,2,1,0:T(8,128)S(1)}, u32[]{:S(2)}, u32[]{:S(2)}) collective-permute-start(f32[2,4,2,8,256]{4,3,2,1,0:T(8,128)} %get-tuple-element.109), channel_id=1, source_target_pairs={{33,9},{35,11},{37,13},{39,15},{40,0},{41,17},{42,2},{43,19},{44,4... | collective-permute-start | bytes 393224 | tf_op jit(solution)/shard_map/ppermute | solution.py:52
  187.0 4.8 %collective-permute-start.36 = (f32[160,8,256]{2,1,0:T(8,128)S(1)}, f32[160,8,256]{2,1,0:T(8,128)S(1)}, u32[]{:S(2)}, u32[]{:S(2)}) collective-permute-start(f32[160,8,256]{2,1,0:T(8,128)S(1)} %pad_maximum_fusion.1), channel_id=1, source_target_pairs={{0,1},{1,0},{2,3},{3,2},{4,5},{5,4},{6,7},{7,6},{8,9},{9,8},{10,11... | collective-permute-start | bytes 3932168 | tf_op jit(solution)/shard_map/ppermute | solution.py:67
  195.5 11.4 %forward.3 = (f32[4,4,2,4,2,8,256]{6,5,4,3,2,1,0:T(8,128)}, f32[4,2,4,2,8,256]{5,4,3,2,1,0:T(8,128)}, f32[4,2,4,2,8,256]{5,4,3,2,1,0:T(8,128)}, f32[4,2,4,2,8,256]{5,4,3,2,1,0:T(8,128)}, f32[4,2,4,2,8,256]{5,4,3,2,1,0:T(8,128)}) custom-call(bf16[2,128,192]{2,1,0:T(8,128)(2,1)} %get-tuple-element.69.refs_0_, bf16[2,128,192]{2,1,0:T(8,128)(2,1)} %get-tuple-element.70.refs_1_, ...), custom_call_target="tpu_custom_call" | custom-call | tf_op jit(solution)/shard_map/forward/pallas_call | solution.py:308
  216.1 6.1 %collective-permute-done.37.refs_7_ = f32[4,2,4,2,8,256]{5,4,3,2,1,0:T(8,128)S(1)} collective-permute-done((f32[4,2,4,2,8,256]{5,4,3,2,1,0:T(8,128)}, f32[4,2,4,2,8,256]{5,4,3,2,1,0:T(8,128)S(1)}, u32[]{:S(2)}, u32[]{:S(2)}) %collective-permute-start.37) | collective-permute-done | bytes 524320 | tf_op jit(solution)/shard_map/ppermute | solution.py:38
  226.7 4.0 %collective-permute-start.41 = (f32[2,2,4,2,8,256]{5,4,3,2,1,0:T(8,128)S(1)}, f32[2,2,4,2,8,256]{5,4,3,2,1,0:T(8,128)S(1)}, u32[]{:S(2)}, u32[]{:S(2)}) collective-permute-start(f32[2,2,4,2,8,256]{5,4,3,2,1,0:T(8,128)S(1)} %pad_maximum_fusion.4), channel_id=1, source_target_pairs={{0,8},{8,16},{16,24},{32,40},{40,48},{48,56},{64,72},{72,80},{80,8... | collective-permute-start | bytes 786440 | tf_op jit(solution)/shard_map/ppermute | solution.py:38
  230.7 4.8 %collective-permute-done.42.refs_12_ = f32[2,2,4,2,8,256]{5,4,3,2,1,0:T(8,128)S(1)} collective-permute-done((f32[2,2,4,2,8,256]{5,4,3,2,1,0:T(8,128)S(1)}, f32[2,2,4,2,8,256]{5,4,3,2,1,0:T(8,128)S(1)}, u32[]{:S(2)}, u32[]{:S(2)}) %collective-permute-start.42) | collective-permute-done | bytes 262176 | tf_op jit(solution)/shard_map/ppermute | solution.py:38
  236.4 10.5 %backward.3 = (f32[4,4,2,4,8,256]{5,4,3,2,1,0:T(8,128)}, f32[4,4,2,4,8,256]{5,4,3,2,1,0:T(8,128)}) custom-call(s32[1,2]{1,0:T(1,128)} %cover.3, bf16[2,128,192]{2,1,0:T(8,128)(2,1)} %get-tuple-element.69.refs_0_, bf16[2,128,192]{2,1,0:T(8,128)(2,1)} %get-tuple-element.70.refs_1_, bf16[2,256,256]{2,1,0:T(8,128)(2,1)} %get-tuple-element.71.refs_2_, ...), custom_call_target="tpu_custom_call" | custom-call | tf_op jit(solution)/shard_map/backward/pallas_call | solution.py:380
  257.5 6.3 %collective-permute-done.44 = f32[4,2,4,8,256]{4,3,2,1,0:T(8,128)S(1)} collective-permute-done((f32[4,2,4,8,256]{4,3,2,1,0:T(8,128)}, f32[4,2,4,8,256]{4,3,2,1,0:T(8,128)S(1)}, u32[]{:S(2)}, u32[]{:S(2)}) %collective-permute-start.44) | collective-permute-done | bytes 262176 | tf_op jit(solution)/shard_map/ppermute | solution.py:63
  263.8 5.1 %collective-permute-done.45 = f32[4,2,4,8,256]{4,3,2,1,0:T(8,128)S(1)} collective-permute-done((f32[4,2,4,8,256]{4,3,2,1,0:T(8,128)}, f32[4,2,4,8,256]{4,3,2,1,0:T(8,128)S(1)}, u32[]{:S(2)}, u32[]{:S(2)}) %collective-permute-start.45) | collective-permute-done | bytes 262176 | tf_op jit(solution)/shard_map/ppermute | solution.py:63
  (246 shorter events, 148.1 us)
Async XLA Ops:
  5.5 14.9 %collective-permute-start.2 = (f32[4,2,4,8,256]{4,3,2,1,0:T(8,128)S(1)}, f32[4,2,4,8,256]{4,3,2,1,0:T(8,128)S(1)}, u32[]{:S(2)}, u32[]{:S(2)}) collective-permute-start(f32[4,2,4,8,256]{4,3,2,1,0:T(8,128)S(1)} %bitcast.72), channel_id=1, source_target_pairs={{0,8},{8,16},{16,24},{24,0},{32,40},{40,48},{48,56},{56,32},{64,72... | collective-permute-start | bytes 786440 | tf_op jit(solution)/shard_map/ppermute | solution.py:58
  29.6 17.4 %collective-permute-start.11 = (f32[4,2,4,2,8,256]{5,4,3,2,1,0:T(8,128)S(1)}, f32[4,2,4,2,8,256]{5,4,3,2,1,0:T(8,128)S(1)}, u32[]{:S(2)}, u32[]{:S(2)}) collective-permute-start(f32[4,2,4,2,8,256]{5,4,3,2,1,0:T(8,128)S(1)} %bitcast.67), channel_id=1, source_target_pairs={{0,8},{8,16},{16,24},{24,0},{32,40},{40,48},{48,56},{56,32},{64,72... | collective-permute-start | bytes 1572872 | tf_op jit(solution)/shard_map/ppermute | solution.py:58
  34.4 25.9 %collective-permute-start.12 = (f32[4,2,4,2,8,256]{5,4,3,2,1,0:T(8,128)S(1)}, f32[4,2,4,2,8,256]{5,4,3,2,1,0:T(8,128)S(1)}, u32[]{:S(2)}, u32[]{:S(2)}) collective-permute-start(f32[4,2,4,2,8,256]{5,4,3,2,1,0:T(8,128)S(1)} %bitcast.66), channel_id=1, source_target_pairs={{0,16},{8,24},{16,0},{24,8},{32,48},{40,56},{48,32},{56,40},{64,80... | collective-permute-start | bytes 1572872 | tf_op jit(solution)/shard_map/ppermute | solution.py:58
  36.2 24.1 %collective-permute-start.13 = (f32[4,2,4,2,8,256]{5,4,3,2,1,0:T(8,128)S(1)}, f32[4,2,4,2,8,256]{5,4,3,2,1,0:T(8,128)S(1)}, u32[]{:S(2)}, u32[]{:S(2)}) collective-permute-start(f32[4,2,4,2,8,256]{5,4,3,2,1,0:T(8,128)S(1)} %bitcast.65), channel_id=1, source_target_pairs={{0,24},{8,0},{16,8},{24,16},{32,56},{40,32},{48,40},{56,48},{64,88... | collective-permute-start | bytes 1572872 | tf_op jit(solution)/shard_map/ppermute | solution.py:58
  37.1 27.1 %collective-permute-start.7 = (f32[2,4,2,4,8,256]{5,4,3,2,1,0:T(8,128)}, f32[2,4,2,4,8,256]{5,4,3,2,1,0:T(8,128)S(1)}, u32[]{:S(2)}, u32[]{:S(2)}) collective-permute-start(f32[2,4,2,4,8,256]{5,4,3,2,1,0:T(8,128)} %get-tuple-element.79), channel_id=1, source_target_pairs={{0,32},{1,9},{2,34},{3,11},{4,36},{5,13},{6,38},{7,15},{8,40},{9,1... | collective-permute-start | bytes 1572872 | tf_op jit(solution)/shard_map/ppermute | solution.py:52
  39.6 25.3 %collective-permute-start.8 = (f32[2,4,2,4,8,256]{5,4,3,2,1,0:T(8,128)}, f32[2,4,2,4,8,256]{5,4,3,2,1,0:T(8,128)S(1)}, u32[]{:S(2)}, u32[]{:S(2)}) collective-permute-start(f32[2,4,2,4,8,256]{5,4,3,2,1,0:T(8,128)} %get-tuple-element.80), channel_id=1, source_target_pairs={{9,1},{11,3},{13,5},{15,7},{17,9},{19,11},{21,13},{23,15},{25,17},... | collective-permute-start | bytes 1572872 | tf_op jit(solution)/shard_map/ppermute | solution.py:52
  81.2 15.9 %collective-permute-start.15 = (f32[4,2,4,2,8,256]{5,4,3,2,1,0:T(8,128)}, f32[4,2,4,2,8,256]{5,4,3,2,1,0:T(8,128)S(1)}, u32[]{:S(2)}, u32[]{:S(2)}) collective-permute-start(f32[4,2,4,2,8,256]{5,4,3,2,1,0:T(8,128)} %get-tuple-element.96), channel_id=1, source_target_pairs={{0,32},{8,40},{16,48},{24,56},{32,64},{40,72},{48,80},{56,88},{64,... | collective-permute-start | bytes 1572872 | tf_op jit(solution)/shard_map/ppermute | solution.py:38
  85.7 16.4 %collective-permute-start.16 = (f32[4,2,4,2,8,256]{5,4,3,2,1,0:T(8,128)}, f32[4,2,4,2,8,256]{5,4,3,2,1,0:T(8,128)S(1)}, u32[]{:S(2)}, u32[]{:S(2)}) collective-permute-start(f32[4,2,4,2,8,256]{5,4,3,2,1,0:T(8,128)} %get-tuple-element.97), channel_id=1, source_target_pairs={{32,0},{40,8},{48,16},{56,24},{64,32},{72,40},{80,48},{88,56},{96,... | collective-permute-start | bytes 1572872 | tf_op jit(solution)/shard_map/ppermute | solution.py:38
  87.6 19.8 %collective-permute-start.17 = (f32[4,2,4,2,8,256]{5,4,3,2,1,0:T(8,128)}, f32[4,2,4,2,8,256]{5,4,3,2,1,0:T(8,128)S(1)}, u32[]{:S(2)}, u32[]{:S(2)}) collective-permute-start(f32[4,2,4,2,8,256]{5,4,3,2,1,0:T(8,128)} %get-tuple-element.98), channel_id=1, source_target_pairs={{0,8},{8,16},{16,24},{32,40},{40,48},{48,56},{64,72},{72,80},{80,8... | collective-permute-start | bytes 1572872 | tf_op jit(solution)/shard_map/ppermute | solution.py:38
  90.0 17.5 %collective-permute-start.18 = (f32[4,2,4,2,8,256]{5,4,3,2,1,0:T(8,128)}, f32[4,2,4,2,8,256]{5,4,3,2,1,0:T(8,128)S(1)}, u32[]{:S(2)}, u32[]{:S(2)}) collective-permute-start(f32[4,2,4,2,8,256]{5,4,3,2,1,0:T(8,128)} %get-tuple-element.99), channel_id=1, source_target_pairs={{8,0},{16,8},{24,16},{40,32},{48,40},{56,48},{72,64},{80,72},{88,8... | collective-permute-start | bytes 1572872 | tf_op jit(solution)/shard_map/ppermute | solution.py:38
  132.8 14.3 %collective-permute-start.23 = (f32[4,2,4,8,256]{4,3,2,1,0:T(8,128)}, f32[4,2,4,8,256]{4,3,2,1,0:T(8,128)S(1)}, u32[]{:S(2)}, u32[]{:S(2)}) collective-permute-start(f32[4,2,4,8,256]{4,3,2,1,0:T(8,128)} %get-tuple-element.104), channel_id=1, source_target_pairs={{0,4},{1,5},{2,6},{3,7},{4,0},{5,1},{6,2},{7,3},{8,12},{9,13},{10,... | collective-permute-start | bytes 786440 | tf_op jit(solution)/shard_map/ppermute | solution.py:63
  149.3 14.4 %collective-permute-start.26 = (f32[4,2,4,8,256]{4,3,2,1,0:T(8,128)S(1)}, f32[4,2,4,8,256]{4,3,2,1,0:T(8,128)S(1)}, u32[]{:S(2)}, u32[]{:S(2)}) collective-permute-start(f32[4,2,4,8,256]{4,3,2,1,0:T(8,128)S(1)} %exponential_multiply_fusion.refs_0_.refs_6_), channel_id=1, source_target_pairs={{0,4},{1,5},{2,6},{3,7},{4,0},{5,1},{6,2},{7,3},{8,12},{9,13},{10,... | collective-permute-start | bytes 786440 | tf_op jit(solution)/shard_map/ppermute | solution.py:63
  152.1 12.9 %collective-permute-start.27 = (f32[4,2,4,8,256]{4,3,2,1,0:T(8,128)S(1)}, f32[4,2,4,8,256]{4,3,2,1,0:T(8,128)S(1)}, u32[]{:S(2)}, u32[]{:S(2)}) collective-permute-start(f32[4,2,4,8,256]{4,3,2,1,0:T(8,128)S(1)} %exponential_multiply_fusion.refs_0_.refs_6_), channel_id=1, source_target_pairs={{0,6},{1,7},{2,0},{3,1},{4,2},{5,3},{6,4},{7,5},{8,14},{9,15},{10,... | collective-permute-start | bytes 786440 | tf_op jit(solution)/shard_map/ppermute | solution.py:63
  152.4 12.7 %collective-permute-start.28 = (f32[4,2,4,8,256]{4,3,2,1,0:T(8,128)S(1)}, f32[4,2,4,8,256]{4,3,2,1,0:T(8,128)S(1)}, u32[]{:S(2)}, u32[]{:S(2)}) collective-permute-start(f32[4,2,4,8,256]{4,3,2,1,0:T(8,128)S(1)} %exponential_multiply_fusion.refs_0_.refs_6_), channel_id=1, source_target_pairs={{0,1},{1,0},{2,3},{3,2},{4,5},{5,4},{6,7},{7,6},{8,9},{9,8},{10,11... | collective-permute-start | bytes 786440 | tf_op jit(solution)/shard_map/ppermute | solution.py:67
  170.3 14.2 %collective-permute-start.32 = (f32[2,4,2,4,8,256]{5,4,3,2,1,0:T(8,128)}, f32[2,4,2,4,8,256]{5,4,3,2,1,0:T(8,128)S(1)}, u32[]{:S(2)}, u32[]{:S(2)}) collective-permute-start(f32[2,4,2,4,8,256]{5,4,3,2,1,0:T(8,128)} %get-tuple-element.106), channel_id=1, source_target_pairs={{0,32},{1,9},{2,34},{3,11},{4,36},{5,13},{6,38},{7,15},{8,40},{9,1... | collective-permute-start | bytes 1572872 | tf_op jit(solution)/shard_map/ppermute | solution.py:52
  206.9 15.2 %collective-permute-start.37 = (f32[4,2,4,2,8,256]{5,4,3,2,1,0:T(8,128)}, f32[4,2,4,2,8,256]{5,4,3,2,1,0:T(8,128)S(1)}, u32[]{:S(2)}, u32[]{:S(2)}) collective-permute-start(f32[4,2,4,2,8,256]{5,4,3,2,1,0:T(8,128)} %get-tuple-element.111), channel_id=1, source_target_pairs={{0,32},{8,40},{16,48},{24,56},{32,64},{40,72},{48,80},{56,88},{64,... | collective-permute-start | bytes 1572872 | tf_op jit(solution)/shard_map/ppermute | solution.py:38
  208.9 16.4 %collective-permute-start.38 = (f32[4,2,4,2,8,256]{5,4,3,2,1,0:T(8,128)}, f32[4,2,4,2,8,256]{5,4,3,2,1,0:T(8,128)S(1)}, u32[]{:S(2)}, u32[]{:S(2)}) collective-permute-start(f32[4,2,4,2,8,256]{5,4,3,2,1,0:T(8,128)} %get-tuple-element.112), channel_id=1, source_target_pairs={{32,0},{40,8},{48,16},{56,24},{64,32},{72,40},{80,48},{88,56},{96,... | collective-permute-start | bytes 1572872 | tf_op jit(solution)/shard_map/ppermute | solution.py:38
  212.2 18.5 %collective-permute-start.39 = (f32[4,2,4,2,8,256]{5,4,3,2,1,0:T(8,128)}, f32[4,2,4,2,8,256]{5,4,3,2,1,0:T(8,128)S(1)}, u32[]{:S(2)}, u32[]{:S(2)}) collective-permute-start(f32[4,2,4,2,8,256]{5,4,3,2,1,0:T(8,128)} %get-tuple-element.113), channel_id=1, source_target_pairs={{0,8},{8,16},{16,24},{32,40},{40,48},{48,56},{64,72},{72,80},{80,8... | collective-permute-start | bytes 1572872 | tf_op jit(solution)/shard_map/ppermute | solution.py:38
  214.8 16.0 %collective-permute-start.40 = (f32[4,2,4,2,8,256]{5,4,3,2,1,0:T(8,128)}, f32[4,2,4,2,8,256]{5,4,3,2,1,0:T(8,128)S(1)}, u32[]{:S(2)}, u32[]{:S(2)}) collective-permute-start(f32[4,2,4,2,8,256]{5,4,3,2,1,0:T(8,128)} %get-tuple-element.114), channel_id=1, source_target_pairs={{8,0},{16,8},{24,16},{40,32},{48,40},{56,48},{72,64},{80,72},{88,8... | collective-permute-start | bytes 1572872 | tf_op jit(solution)/shard_map/ppermute | solution.py:38
  254.8 14.1 %collective-permute-start.45 = (f32[4,2,4,8,256]{4,3,2,1,0:T(8,128)}, f32[4,2,4,8,256]{4,3,2,1,0:T(8,128)S(1)}, u32[]{:S(2)}, u32[]{:S(2)}) collective-permute-start(f32[4,2,4,8,256]{4,3,2,1,0:T(8,128)} %get-tuple-element.119), channel_id=1, source_target_pairs={{0,4},{1,5},{2,6},{3,7},{4,0},{5,1},{6,2},{7,3},{8,12},{9,13},{10,... | collective-permute-start | bytes 786440 | tf_op jit(solution)/shard_map/ppermute | solution.py:63
  257.0 12.5 %collective-permute-start.46 = (f32[4,2,4,8,256]{4,3,2,1,0:T(8,128)}, f32[4,2,4,8,256]{4,3,2,1,0:T(8,128)S(1)}, u32[]{:S(2)}, u32[]{:S(2)}) collective-permute-start(f32[4,2,4,8,256]{4,3,2,1,0:T(8,128)} %get-tuple-element.120), channel_id=1, source_target_pairs={{0,6},{1,7},{2,0},{3,1},{4,2},{5,3},{6,4},{7,5},{8,14},{9,15},{10,... | collective-permute-start | bytes 786440 | tf_op jit(solution)/shard_map/ppermute | solution.py:63
  281.1 13.7 %collective-permute-start.51 = (f32[2,128,256]{2,1,0:T(8,128)S(1)}, f32[2,128,256]{2,1,0:T(8,128)S(1)}, u32[]{:S(2)}, u32[]{:S(2)}) collective-permute-start(f32[2,128,256]{2,1,0:T(8,128)S(1)} %bitcast.61), channel_id=1, source_target_pairs={{0,4},{1,5},{2,6},{3,7},{4,0},{5,1},{6,2},{7,3},{8,12},{9,13},{10,... | collective-permute-start | bytes 786440 | tf_op jit(solution)/shard_map/ppermute | solution.py:63
  284.4 12.9 %collective-permute-start.52 = (f32[2,128,256]{2,1,0:T(8,128)S(1)}, f32[2,128,256]{2,1,0:T(8,128)S(1)}, u32[]{:S(2)}, u32[]{:S(2)}) collective-permute-start(f32[2,128,256]{2,1,0:T(8,128)S(1)} %bitcast.62), channel_id=1, source_target_pairs={{0,6},{1,7},{2,0},{3,1},{4,2},{5,3},{6,4},{7,5},{8,14},{9,15},{10,... | collective-permute-start | bytes 786440 | tf_op jit(solution)/shard_map/ppermute | solution.py:63
  284.4 13.0 %collective-permute-start.53 = (f32[2,128,256]{2,1,0:T(8,128)S(1)}, f32[2,128,256]{2,1,0:T(8,128)S(1)}, u32[]{:S(2)}, u32[]{:S(2)}) collective-permute-start(f32[2,128,256]{2,1,0:T(8,128)S(1)} %bitcast.63), channel_id=1, source_target_pairs={{0,1},{1,0},{2,3},{3,2},{4,5},{5,4},{6,7},{7,6},{8,9},{9,8},{10,11... | collective-permute-start | bytes 786440 | tf_op jit(solution)/shard_map/ppermute | solution.py:67
  (89 other events, 577.9 us)

commit v4 on v3

--- a/solution.py
+++ b/solution.py
@@ -76,54 +76,69 @@
     return jnp.dot(a, b, preferred_element_type=F32)
 
 
-def matrices_kernel(axial_taps, lateral_taps, kyh, kyl, kxh, kxl, kzh, kzl):
+def matrices_kernel(axial_taps, lateral_taps, ky, kzh, kzl, kxh, kxl):
     one = jnp.int32(1)
     zero = jnp.int32(0)
 
     def iota(shape, axis):
         return lax.broadcasted_iota(jnp.int32, shape, axis)
 
-    def near(shape, start):
-        row, col = iota(shape, 0), iota(shape, 1)
-        pcol = sum(jnp.where(col >= 48 * n, one, zero) for n in (1, 2, 3))
-        return jnp.where(pcol == start // 32, (col - 48 * pcol) - (row + start % 32), -1)
+    def fill(shape, offset, tap, count, put):
+        taps = [tap(d) for d in range(count)]
+        norm = sum(taps[1:], taps[0])
+
+        @pl.loop(0, shape[0] // 16)
+        def _(n):
+            start = pl.multiple_of(16 * n, 16)
+            where = offset((16, shape[1]), start)
+            for way in range(2):
+                matrix = jnp.zeros((16, shape[1]), F32)
+                for d in range(count):
+                    matrix = jnp.where(where == (d if way == 0 else count - 1 - d), taps[d], matrix)
+                put(way, pl.ds(start, 16), split(matrix / jnp.full((16, shape[1]), norm)))
+
+    def three(depth, out):
+        def part(shape):
+            col = iota(shape, 1)
+            return jnp.where(col >= depth, one, zero) + jnp.where(col >= 2 * depth, one, zero)
+
+        def offset(shape, start):
+            return iota(shape, 1) - depth * part(shape) - iota(shape, 0) - start
+
+        def put(way, rows, parts):
+            high, low = [value.astype(F32) for value in parts]
+            out[way, rows] = jnp.where(part(high.shape) == 1, low, high).astype(BF16)
+
+        return (32, 3 * depth), offset, put
 
     def wide(shape, start):
         return iota(shape, 0) + start - iota(shape, 1) + RAD
 
+    def put_wide(way, rows, parts):
+        kxh[way, rows], kxl[way, rows] = parts
+
+    shape, offset, put = three(32 + 2 * RAD, ky)
+    fill(shape, offset, lambda d: lateral_taps[0, 0, d], NLAT, put)
+    fill((256, 256), wide, lambda d: lateral_taps[0, 1, d], NLAT, put_wide)
+
     def deep(shape, start):
         return iota(shape, 1) - iota(shape, 0) - start
 
-    def fill(where, tap, count, high, low):
-        taps = [tap(d) for d in range(count)]
-        norm = sum(taps[1:], taps[0])
-        shape = (16, high.shape[2])
-
-        @pl.loop(0, high.shape[1] // 16)
-        def _(n):
-            start = pl.multiple_of(16 * n, 16)
-            offset = where(shape, start)
-            for way in range(2):
-                matrix = jnp.zeros(shape, F32)
-                for d in range(count):
-                    matrix = jnp.where(offset == (d if way == 0 else count - 1 - d), taps[d], matrix)
-                matrix = matrix / jnp.full(shape, norm)
-                high[way, pl.ds(start, 16)], low[way, pl.ds(start, 16)] = split(matrix)
-
-    fill(near, lambda d: lateral_taps[0, 0, d], NLAT, kyh, kyl)
-    fill(wide, lambda d: lateral_taps[0, 1, d], NLAT, kxh, kxl)
-    fill(deep, lambda d: axial_taps[0, d], NAX, kzh, kzl)
+    def put_deep(way, rows, parts):
+        kzh[way, rows], kzl[way, rows] = parts
+
+    fill((64, 96), deep, lambda d: axial_taps[0, d], NAX, put_deep)
 
 
 def matrices(axial_taps, lateral_taps):
-    ky = jax.ShapeDtypeStruct((2, 128, 192), BF16)
+    ky = jax.ShapeDtypeStruct((2, 32, 144), BF16)
+    kz = jax.ShapeDtypeStruct((2, 64, 96), BF16)
     kx = jax.ShapeDtypeStruct((2, 256, 256), BF16)
-    kz = jax.ShapeDtypeStruct((2, 64, 96), BF16)
     return pl.pallas_call(
         matrices_kernel,
-        out_shape=(ky, ky, kx, kx, kz, kz),
+        out_shape=(ky, kz, kz, kx, kx),
         in_specs=[SMEM, SMEM],
-        out_specs=(VMEM,) * 6,
+        out_specs=(VMEM,) * 5,
         compiler_params=params(),
         name="matrices",
     )(axial_taps, lateral_taps)
@@ -138,18 +153,20 @@
     ref[1, group, rows, :] = value[:, 128:]
 
 
+def three_products(matrix, high, low):
+    return mm(matrix, jnp.concatenate([high, high, low], axis=0))
+
+
 def blur(way, mats, wide, across, inner, outer, ready, finish, done):
-    kyh, kyl, kxh, kxl, kzh, kzl = [m[way] for m in mats]
+    ky, kzh, kzl, kxh, kxl = [m[way] for m in mats]
 
     def over_rows(b):
-        for n in range(4):
-            block = wide[b, n // 2, pl.ds(2 * (n % 2), 2)].reshape(192, 256)
-            high, low = split(block)
-            rows = mm(kyh, high) + (mm(kyl, high) + mm(kyh, low))
-            for p in range(4):
-                at = pl.ds(pl.multiple_of(128 * b + 32 * n + 8 * p, 8), 8)
-                for q in range(4):
-                    store_halves(across, q, at, rows[32 * p + 8 * q : 32 * p + 8 * q + 8])
+        for n in range(16):
+            block = wide[b, n // 8, (n // 2) % 4, n % 2].reshape(48, 256)
+            rows = three_products(ky, *split(block))
+            at = pl.ds(pl.multiple_of(128 * b + 8 * n, 8), 8)
+            for q in range(4):
+                store_halves(across, q, at, rows[8 * q : 8 * q + 8])
 
     inner()
     pl.loop(1, 5)(over_rows)
@@ -232,33 +249,41 @@
     return ref.at[half].reshape(4, 4, 2, 4, 2, 8, 128)
 
 
-def put_pieces(copies, first, pieces, tile):
+def put_pieces(copies, pieces, tile):
     z, y, x, c = place()
     for k in range(4):
+        s = (x - k + XD) % XD
         for other in range(2):
             half = c if other == 0 else 1 - c
-            if first:
-                slot = tile((y - k + YD) % YD, half, pl.ds(0, 4))
-            else:
-                slot = tile(pl.ds(0, 4), half, (x - k + XD) % XD)
-            copies.add(pieces[4 * other + k], slot)
+            copies.add(pieces[4 * other + k], tile(half, s))
 
 
 def forward_kernel(first, *refs):
-    mats, pieces, moved, got, shown = refs[:6], refs[6:14], refs[14:18], refs[18], refs[19:23]
-    center, edges = refs[23], refs[24:28]
-    wide, across, views, ratio, sems, group_sems, out_sems = refs[28:]
+    inputs = 17 if first else 18
+    mats, tile, refs = refs[:5], refs[5:inputs], refs[inputs:]
+    shown, center, edges = refs[:4], refs[4], refs[5:9]
+    wide, across, views, ratio, sems, group_sems, out_sems = refs[9:]
     z, y, x, c = place()
     copies = Copies(sems)
     middle = wide.at[pl.ds(1, 4)]
-    put_pieces(copies, first, pieces, lambda b, h, s: middle.at[b, h, s, :, pl.ds(1, 4)])
-    for n, (step0, step1) in enumerate(STEPS):
-        shapes = (ZEDGE, YEDGE) if n < 2 else (CORNER, CORNER)
-        start, size = ((64 * n, 64) if n < 2 else (96 + 16 * n, 16))
-        theirs = got.at[pl.ds(start, size)]
-        slot0, slot1 = halo_slot(wide, step0), halo_slot(wide, step1)
-        copies.add_by_core(c, (moved[n], slot0), (theirs.reshape(*shapes[0]), slot0))
-        copies.add_by_core(c, (theirs.reshape(*shapes[1]), slot1), (moved[n].reshape(*shapes[1]), slot1))
+    if first:
+        for other in range(2):
+            half = c if other == 0 else 1 - c
+            for k in range(4):
+                copies.add(tile[4 * other + k], middle.at[(y - k + YD) % YD, half])
+            for n in range(2):
+                copies.add(tile[8 + 2 * other + n], wide.at[5 * n, half])
+    else:
+        pieces, moved, got = tile[:8], tile[8:12], tile[12]
+        put_pieces(copies, pieces, lambda h, s: middle.at[:, h, s, :, pl.ds(1, 4)])
+        for n, (step0, step1) in enumerate(STEPS):
+            shapes = (ZEDGE, YEDGE) if n < 2 else (CORNER, CORNER)
+            start, size = (64 * n, 64) if n < 2 else (96 + 16 * n, 16)
+            theirs = got.at[pl.ds(start, size)]
+            slot0, slot1 = halo_slot(wide, step0), halo_slot(wide, step1)
+            copies.add_by_core(c, (moved[n], slot0), (theirs.reshape(*shapes[0]), slot0))
+            own = moved[n].reshape(*shapes[1])
+            copies.add_by_core(c, (theirs.reshape(*shapes[1]), slot1), (own, slot1))
     count = len(copies.items)
     for k in range(4):
         b = (y - k + YD) % YD
@@ -303,12 +328,12 @@
     copies.wait()
 
 
-def forward(first, mats, pieces, moved, got, shown):
+def forward(first, mats, tile, shown):
     shapes = (RATIO, RATIO_ZEDGE, RATIO_ZEDGE, YEDGE, YEDGE)
     got = pl.pallas_call(
         functools.partial(forward_kernel, first),
         out_shape=tuple(jax.ShapeDtypeStruct(s, F32) for s in shapes),
-        in_specs=[VMEM] * 6 + [ANY] * 17,
+        in_specs=[VMEM] * 5 + [ANY] * (len(tile) + 4),
         out_specs=(ANY,) * 5,
         scratch_shapes=[
             pltpu.VMEM(WIDE, F32),
@@ -321,14 +346,14 @@
         ],
         compiler_params=params(),
         name="forward",
-    )(*mats, *pieces, *moved, got, *shown)
+    )(*mats, *tile, *shown)
     return got[0], got[1:]
 
 
 def backward_kernel(cover, *refs):
-    mats, center, halos, strips = refs[:6], refs[6], refs[7:11], refs[11:13]
-    mine, other = refs[13:15]
-    wide, across, logs, sems, out_sems = refs[15:]
+    mats, center, halos, strips = refs[:5], refs[5], refs[6:10], refs[10:12]
+    mine, other = refs[12:14]
+    wide, across, logs, sems, out_sems = refs[14:]
     z, y, x, c = place()
     copies = Copies(sems)
     for n in range(2, 4):
@@ -380,7 +405,7 @@
     return pl.pallas_call(
         backward_kernel,
         out_shape=(half, half),
-        in_specs=[SMEM] + [VMEM] * 6 + [ANY] * 7,
+        in_specs=[SMEM] + [VMEM] * 5 + [ANY] * 7,
         out_specs=(ANY, ANY),
         scratch_shapes=[
             pltpu.VMEM(WIDE, F32),
@@ -398,7 +423,10 @@
     z, y, x, c = place()
     for k in range(4):
         s = (x + k) % XD
-        outs[k][...] = mine[:, s] + got[:, s]
+
+        @pl.loop(0, 4)
+        def _(b):
+            outs[k][b] = mine[b, s] + got[b, s]
 
 
 def shares(mine, got):
@@ -413,12 +441,12 @@
     )(mine, got)
 
 
-def edges_kernel(first, *refs):
+def edges_kernel(*refs):
     pieces, outs = refs[:8], refs[8:12]
     tile, sems, out_sems = refs[12:]
     z, y, x, c = place()
     copies = Copies(sems)
-    put_pieces(copies, first, pieces, lambda b, h, s: tile.at[b, h, s])
+    put_pieces(copies, pieces, lambda h, s: tile.at[:, h, s])
     copies.wait()
     copies = Copies(out_sems)
     for n, (step0, step1) in enumerate(STEPS):
@@ -427,9 +455,9 @@
     copies.wait()
 
 
-def edges(first, pieces):
+def edges(pieces):
     return pl.pallas_call(
-        functools.partial(edges_kernel, first),
+        edges_kernel,
         out_shape=tuple(jax.ShapeDtypeStruct(s, F32) for s in (ZEDGE, ZEDGE, CORNER, CORNER)),
         in_specs=[ANY] * 8,
         out_specs=(ANY,) * 4,
@@ -448,7 +476,7 @@
     slab, sems, out_sems = refs[9:]
     z, y, x, c = place()
     copies = Copies(sems)
-    put_pieces(copies, False, pieces, lambda b, h, s: slab.at[h, s])
+    put_pieces(copies, pieces, lambda h, s: slab.at[h, s])
     copies.wait()
     copies = Copies(out_sems)
     copies.add(slab, out)
@@ -484,30 +512,37 @@
 def local(estimate, views, axial_taps, lateral_taps, cover):
     z, y, x, c = place()
 
+    half = lax.dynamic_slice_in_dim(estimate, 8 * c, 8, axis=0)
+    half = jnp.pad(half, ((0, 0), (8, 8), (0, 0))).reshape(4, 2, 18, 8, 256)
+
     def est_rows(k):
-        half = lax.dynamic_slice_in_dim(estimate, 8 * c, 8, axis=0)
-        rows = lax.dynamic_slice_in_dim(half, 32 * ((y + k) % YD), 32, axis=1)
-        return rows.reshape(PART)
+        return lax.dynamic_slice_in_dim(half, 4 * ((y + k) % YD), 6, axis=2)
 
     def view_rows(k):
         rows = lax.dynamic_slice_in_dim(views[0].reshape(16, 16, 8, 256), 4 * ((y + k) % YD), 4, axis=1)
         return jnp.transpose(rows, (1, 0, 2, 3)).reshape(4, 2, 4, 2, 8, 256)
 
     pieces = [est_rows(0)] + [y_turn(est_rows(k), k) for k in (1, 2, 3)]
-    share = by_block([lax.dynamic_index_in_dim(p, x, 0, keepdims=False) for p in pieces], y)
     mats = matrices(axial_taps, lateral_taps)
     shown = [view_rows(k) for k in range(4)]
     pieces, mats, shown = lax.optimization_barrier((pieces, mats, shown))
     shown = [shown[0]] + [y_turn(shown[k], k) for k in (1, 2, 3)]
+    share = [lax.dynamic_index_in_dim(p, x, 0, keepdims=False)[:, 1:5] for p in pieces]
+    share = by_block(share, y)
     for step in range(ITERS):
-        if step > 0:
+        if step == 0:
+            top = lax.select_n((y + 1) % YD, *pieces)
+            bottom = lax.select_n(y, *pieces)
+            beside = [blk_shift(top, 1, 0), blk_shift(bottom, -1, 0)]
+            tile = pieces + [core_swap(piece) for piece in pieces]
+            tile += beside + [core_swap(part) for part in beside]
+        else:
             pieces = gathered(share)
-        pieces = pieces + [core_swap(piece) for piece in pieces]
-        rims = [core_step(e, steps) for e, steps in zip(edges(step == 0, pieces), STEPS)]
-        if step == 0:
-            rims, shown = lax.optimization_barrier((rims, shown))
-        swapped = core_swap(jnp.concatenate([rim.reshape(-1, 8, 256) for rim in rims]))
-        center, rims = forward(step == 0, mats, pieces, rims, swapped, shown)
+            pieces = pieces + [core_swap(piece) for piece in pieces]
+            rims = [core_step(e, steps) for e, steps in zip(edges(pieces), STEPS)]
+            swapped = core_swap(jnp.concatenate([rim.reshape(-1, 8, 256) for rim in rims]))
+            tile = pieces + rims + [swapped]
+        center, rims = forward(step == 0, mats, tile, shown)
         halos = [blk_shift(e, *d) for e, d in zip(rims, FACES)]
         low, high = halos[0], halos[1]
         strips = [blk_shift(jnp.stack([low[r], high[r]]), 0, dy) for r, dy in ((3, 1), (0, -1))]

time: 305 us -> 296 us (0.970)
  starting transfers between devices: 105 us -> 99.6 us
  Pallas kernels: 60.3 us -> 54.9 us
  local copies, waits for them, and re-layouts: 14.7 us -> 19 us
    ppermute x12, waiting for transfers between devices: 34.4 us -> 47.5 us  [x_turn(): return lax.ppermute(value, 'view', pairs)]
    ppermute x12 -> x14, starting transfers between devices: 29.7 us -> 41.3 us  [blk_shift(): return lax.ppermute(value, 'blk', pairs)]
    ppermute x8 -> x4, starting transfers between devices: 18 us -> 9.76 us  [core_step(): return lax.ppermute(value, ('blk', 'view'), pairs)]
    ppermute x9, waiting for transfers between devices: 33.7 us -> 26.7 us  [y_turn(): return lax.ppermute(value, 'blk', pairs)]
    ppermute x12, starting transfers between devices: 17.3 us -> 11.3 us  [x_turn(): return lax.ppermute(value, 'view', pairs)]
    ppermute x16 -> x17, waiting for transfers between devices: 14.3 us -> 8.33 us  [core_swap(): return lax.ppermute(value, 'view', [(i, i ^ 1) for i in range(2 * XD)])]
    ppermute x8 -> x4, waiting for transfers between devices: 8.84 us -> 4.33 us  [core_step(): return lax.ppermute(value, ('blk', 'view'), pairs)]
    ppermute x9, starting transfers between devices: 15.3 us -> 11.4 us  [y_turn(): return lax.ppermute(value, 'blk', pairs)]
  transfers between devices with their start and end apart: 57 -> 56, of which waited for: 41 -> 38; matrix products, arithmetic and copies ran while one was open for 1% -> 3% of each run, Pallas kernels for 1% -> 1%
where the time goes in v4:
time: 296 us; the launch traced here: 295 us
  waiting for transfers between devices  117 us (40%)
  starting transfers between devices  99.6 us (34%)
  Pallas kernels  54.9 us (19%)
  local copies, waits for them, and re-layouts  19 us (6%)
  other arithmetic  3.36 us (1%)
    ppermute x12, waiting for transfers between devices, x_turn(): return lax.ppermute(value, 'view', pairs)  47.5 us
    ppermute x14, starting transfers between devices, blk_shift(): return lax.ppermute(value, 'blk', pairs)  41.3 us
    ppermute x14, waiting for transfers between devices, blk_shift(): return lax.ppermute(value, 'blk', pairs)  29.9 us
    ppermute x9, waiting for transfers between devices, y_turn(): return lax.ppermute(value, 'blk', pairs)  26.7 us
    ppermute x17, starting transfers between devices, core_swap(): return lax.ppermute(value, 'view', [(i, i ^ 1) for i in range(2 * XD)])  25.8 us
    pallas_call x2, Pallas kernels, forward(): pl.pallas_call(functools.partial(forward_kernel, first), out_shape=tuple(...  21.6 us
    pallas_call x2, Pallas kernels, backward(): pl.pallas_call(backward_kernel, out_shape=(half, half), in_specs=[SMEM] +...  19.7 us
    unnamed x120, local copies, waits for them, and re-layouts  13.1 us
  transfers between devices with their start and end apart: 56, of which 38 were waited for; matrix products, arithmetic and copies ran while one was open for 3% of the time, Pallas kernels for 1%

profile of v4, /device:TPU:97, one launch (start us, length us, event | category | flops | bytes accessed | tf_op | source)
XLA Modules:
  0.0 294.6 jit_solution(655672717013976117)
XLA Ops:
  15.6 8.4 %collective-permute-done.1.refs_7_ = f32[4,2,6,8,256]{4,3,2,1,0:T(8,128)S(1)} collective-permute-done((f32[4,2,6,8,256]{4,3,2,1,0:T(8,128)}, f32[4,2,6,8,256]{4,3,2,1,0:T(8,128)S(1)}, u32[]{:S(2)}, u32[]{:S(2)}) %collective-permute-start.1) | collective-permute-done | bytes 393248 | tf_op jit(solution)/shard_map/ppermute | solution.py:58
  27.5 4.8 %collective-permute-start.7 = (f32[4,2,6,8,256]{4,3,2,1,0:T(8,128)S(1)}, f32[4,2,6,8,256]{4,3,2,1,0:T(8,128)S(1)}, u32[]{:S(2)}, u32[]{:S(2)}) collective-permute-start(f32[4,2,6,8,256]{4,3,2,1,0:T(8,128)S(1)} %get-tuple-element.98), channel_id=1, source_target_pairs={{0,32},{8,40},{16,48},{24,56},{32,64},{40,72},{48,80},{56,88},{64,... | collective-permute-start | bytes 1179656 | tf_op jit(solution)/shard_map/ppermute | solution.py:38
  41.6 3.8 %collective-permute-done.8.refs_14_ = f32[4,2,6,8,256]{4,3,2,1,0:T(8,128)S(1)} collective-permute-done((f32[4,2,6,8,256]{4,3,2,1,0:T(8,128)S(1)}, f32[4,2,6,8,256]{4,3,2,1,0:T(8,128)S(1)}, u32[]{:S(2)}, u32[]{:S(2)}) %collective-permute-start.8) | collective-permute-done | bytes 393248 | tf_op jit(solution)/shard_map/ppermute | solution.py:38
  48.4 11.5 %collective-permute-done.12.refs_19_.refs_20_ = f32[4,2,4,2,8,256]{5,4,3,2,1,0:T(8,128)S(1)} collective-permute-done((f32[4,2,4,2,8,256]{5,4,3,2,1,0:T(8,128)S(1)}, f32[4,2,4,2,8,256]{5,4,3,2,1,0:T(8,128)S(1)}, u32[]{:S(2)}, u32[]{:S(2)}) %collective-permute-start.12) | collective-permute-done | bytes 524320 | tf_op jit(solution)/shard_map/ppermute | solution.py:58
  61.2 10.8 %forward.2 = (f32[4,4,2,4,2,8,256]{6,5,4,3,2,1,0:T(8,128)}, f32[4,2,4,2,8,256]{5,4,3,2,1,0:T(8,128)}, f32[4,2,4,2,8,256]{5,4,3,2,1,0:T(8,128)}, f32[4,2,4,2,8,256]{5,4,3,2,1,0:T(8,128)}, f32[4,2,4,2,8,256]{5,4,3,2,1,0:T(8,128)}) custom-call(bf16[2,32,144]{2,1,0:T(8,128)(2,1)} %get-tuple-element.58.refs_0_, bf16[2,64,96]{2,1,0:T(8,128)(2,1)} %get-tuple-element.59.refs_1_, ...), custom_call_target="tpu_custom_call" | custom-call | tf_op jit(solution)/shard_map/forward/pallas_call | solution.py:333
  74.0 4.6 %collective-permute-start.14 = (f32[4,2,4,2,8,256]{5,4,3,2,1,0:T(8,128)}, f32[4,2,4,2,8,256]{5,4,3,2,1,0:T(8,128)S(1)}, u32[]{:S(2)}, u32[]{:S(2)}) collective-permute-start(f32[4,2,4,2,8,256]{5,4,3,2,1,0:T(8,128)} %get-tuple-element.68), channel_id=1, source_target_pairs={{0,32},{8,40},{16,48},{24,56},{32,64},{40,72},{48,80},{56,88},{64,... | collective-permute-start | bytes 1572872 | tf_op jit(solution)/shard_map/ppermute | solution.py:38
  78.6 4.4 %collective-permute-start.16 = (f32[4,2,4,2,8,256]{5,4,3,2,1,0:T(8,128)}, f32[4,2,4,2,8,256]{5,4,3,2,1,0:T(8,128)S(1)}, u32[]{:S(2)}, u32[]{:S(2)}) collective-permute-start(f32[4,2,4,2,8,256]{5,4,3,2,1,0:T(8,128)} %get-tuple-element.70), channel_id=1, source_target_pairs={{0,8},{8,16},{16,24},{32,40},{40,48},{48,56},{64,72},{72,80},{80,8... | collective-permute-start | bytes 1572872 | tf_op jit(solution)/shard_map/ppermute | solution.py:38
  88.3 5.3 %collective-permute-start.18 = (f32[2,2,4,2,8,256]{5,4,3,2,1,0:T(8,128)S(1)}, f32[2,2,4,2,8,256]{5,4,3,2,1,0:T(8,128)S(1)}, u32[]{:S(2)}, u32[]{:S(2)}) collective-permute-start(f32[2,2,4,2,8,256]{5,4,3,2,1,0:T(8,128)S(1)} %pad_maximum_fusion.1), channel_id=1, source_target_pairs={{0,8},{8,16},{16,24},{32,40},{40,48},{48,56},{64,72},{72,80},{80,8... | collective-permute-start | bytes 786440 | tf_op jit(solution)/shard_map/ppermute | solution.py:38
  99.0 3.9 %collective-permute-done.19.refs_11_ = f32[2,2,4,2,8,256]{5,4,3,2,1,0:T(8,128)S(1)} collective-permute-done((f32[2,2,4,2,8,256]{5,4,3,2,1,0:T(8,128)S(1)}, f32[2,2,4,2,8,256]{5,4,3,2,1,0:T(8,128)S(1)}, u32[]{:S(2)}, u32[]{:S(2)}) %collective-permute-start.19) | collective-permute-done | bytes 262176 | tf_op jit(solution)/shard_map/ppermute | solution.py:38
  103.6 9.8 %backward.2 = (f32[4,4,2,4,8,256]{5,4,3,2,1,0:T(8,128)}, f32[4,4,2,4,8,256]{5,4,3,2,1,0:T(8,128)}) custom-call(s32[1,2]{1,0:T(1,128)} %cover.3, bf16[2,32,144]{2,1,0:T(8,128)(2,1)} %get-tuple-element.58.refs_0_, bf16[2,64,96]{2,1,0:T(8,128)(2,1)} %get-tuple-element.59.refs_1_, bf16[2,64,96]{2,1,0:T(8,128)(2,1)} %get-tuple-element.60.refs_2_, ...), custom_call_target="tpu_custom_call" | custom-call | tf_op jit(solution)/shard_map/backward/pallas_call | solution.py:405
  125.7 10.0 %collective-permute-done.23 = f32[4,2,4,8,256]{4,3,2,1,0:T(8,128)S(1)} collective-permute-done((f32[4,2,4,8,256]{4,3,2,1,0:T(8,128)}, f32[4,2,4,8,256]{4,3,2,1,0:T(8,128)S(1)}, u32[]{:S(2)}, u32[]{:S(2)}) %collective-permute-start.23) | collective-permute-done | bytes 262176 | tf_op jit(solution)/shard_map/ppermute | solution.py:63
  135.7 4.4 %collective-permute-done.21 = f32[4,2,4,8,256]{4,3,2,1,0:T(8,128)S(1)} collective-permute-done((f32[4,2,4,8,256]{4,3,2,1,0:T(8,128)}, f32[4,2,4,8,256]{4,3,2,1,0:T(8,128)S(1)}, u32[]{:S(2)}, u32[]{:S(2)}) %collective-permute-start.21) | collective-permute-done | bytes 262176 | tf_op jit(solution)/shard_map/ppermute | solution.py:63
  145.2 10.3 %collective-permute-done.24.refs_1_.refs_6_ = f32[4,2,4,8,256]{4,3,2,1,0:T(8,128)S(1)} collective-permute-done((f32[4,2,4,8,256]{4,3,2,1,0:T(8,128)S(1)}, f32[4,2,4,8,256]{4,3,2,1,0:T(8,128)S(1)}, u32[]{:S(2)}, u32[]{:S(2)}) %collective-permute-start.24) | collective-permute-done | bytes 262176 | tf_op jit(solution)/shard_map/ppermute | solution.py:63
  167.3 4.9 %collective-permute-start.34 = (f32[2,4,2,8,256]{4,3,2,1,0:T(8,128)}, f32[2,4,2,8,256]{4,3,2,1,0:T(8,128)S(1)}, u32[]{:S(2)}, u32[]{:S(2)}) collective-permute-start(f32[2,4,2,8,256]{4,3,2,1,0:T(8,128)} %get-tuple-element.81), channel_id=1, source_target_pairs={{33,9},{35,11},{37,13},{39,15},{40,0},{41,17},{42,2},{43,19},{44,4... | collective-permute-start | bytes 393224 | tf_op jit(solution)/shard_map/ppermute | solution.py:52
  177.4 7.7 %collective-permute-start.35 = (f32[160,8,256]{2,1,0:T(8,128)S(1)}, f32[160,8,256]{2,1,0:T(8,128)S(1)}, u32[]{:S(2)}, u32[]{:S(2)}) collective-permute-start(f32[160,8,256]{2,1,0:T(8,128)S(1)} %pad_maximum_fusion), channel_id=1, source_target_pairs={{0,1},{1,0},{2,3},{3,2},{4,5},{5,4},{6,7},{7,6},{8,9},{9,8},{10,11... | collective-permute-start | bytes 3932168 | tf_op jit(solution)/shard_map/ppermute | solution.py:67
  188.8 10.8 %forward.3 = (f32[4,4,2,4,2,8,256]{6,5,4,3,2,1,0:T(8,128)}, f32[4,2,4,2,8,256]{5,4,3,2,1,0:T(8,128)}, f32[4,2,4,2,8,256]{5,4,3,2,1,0:T(8,128)}, f32[4,2,4,2,8,256]{5,4,3,2,1,0:T(8,128)}, f32[4,2,4,2,8,256]{5,4,3,2,1,0:T(8,128)}) custom-call(bf16[2,32,144]{2,1,0:T(8,128)(2,1)} %get-tuple-element.58.refs_0_, bf16[2,64,96]{2,1,0:T(8,128)(2,1)} %get-tuple-element.59.refs_1_, ...), custom_call_target="tpu_custom_call" | custom-call | tf_op jit(solution)/shard_map/forward/pallas_call | solution.py:333
  201.6 4.6 %collective-permute-start.36 = (f32[4,2,4,2,8,256]{5,4,3,2,1,0:T(8,128)}, f32[4,2,4,2,8,256]{5,4,3,2,1,0:T(8,128)S(1)}, u32[]{:S(2)}, u32[]{:S(2)}) collective-permute-start(f32[4,2,4,2,8,256]{5,4,3,2,1,0:T(8,128)} %get-tuple-element.83), channel_id=1, source_target_pairs={{0,32},{8,40},{16,48},{24,56},{32,64},{40,72},{48,80},{56,88},{64,... | collective-permute-start | bytes 1572872 | tf_op jit(solution)/shard_map/ppermute | solution.py:38
  206.2 3.4 %collective-permute-start.38 = (f32[4,2,4,2,8,256]{5,4,3,2,1,0:T(8,128)}, f32[4,2,4,2,8,256]{5,4,3,2,1,0:T(8,128)S(1)}, u32[]{:S(2)}, u32[]{:S(2)}) collective-permute-start(f32[4,2,4,2,8,256]{5,4,3,2,1,0:T(8,128)} %get-tuple-element.85), channel_id=1, source_target_pairs={{0,8},{8,16},{16,24},{32,40},{40,48},{48,56},{64,72},{72,80},{80,8... | collective-permute-start | bytes 1572872 | tf_op jit(solution)/shard_map/ppermute | solution.py:38
  210.8 5.3 %collective-permute-done.37.refs_7_ = f32[4,2,4,2,8,256]{5,4,3,2,1,0:T(8,128)S(1)} collective-permute-done((f32[4,2,4,2,8,256]{5,4,3,2,1,0:T(8,128)}, f32[4,2,4,2,8,256]{5,4,3,2,1,0:T(8,128)S(1)}, u32[]{:S(2)}, u32[]{:S(2)}) %collective-permute-start.37) | collective-permute-done | bytes 524320 | tf_op jit(solution)/shard_map/ppermute | solution.py:38
  225.5 3.9 %collective-permute-done.41.refs_11_ = f32[2,2,4,2,8,256]{5,4,3,2,1,0:T(8,128)S(1)} collective-permute-done((f32[2,2,4,2,8,256]{5,4,3,2,1,0:T(8,128)S(1)}, f32[2,2,4,2,8,256]{5,4,3,2,1,0:T(8,128)S(1)}, u32[]{:S(2)}, u32[]{:S(2)}) %collective-permute-start.41) | collective-permute-done | bytes 262176 | tf_op jit(solution)/shard_map/ppermute | solution.py:38
  230.1 9.8 %backward.3 = (f32[4,4,2,4,8,256]{5,4,3,2,1,0:T(8,128)}, f32[4,4,2,4,8,256]{5,4,3,2,1,0:T(8,128)}) custom-call(s32[1,2]{1,0:T(1,128)} %cover.3, bf16[2,32,144]{2,1,0:T(8,128)(2,1)} %get-tuple-element.58.refs_0_, bf16[2,64,96]{2,1,0:T(8,128)(2,1)} %get-tuple-element.59.refs_1_, bf16[2,64,96]{2,1,0:T(8,128)(2,1)} %get-tuple-element.60.refs_2_, ...), custom_call_target="tpu_custom_call" | custom-call | tf_op jit(solution)/shard_map/backward/pallas_call | solution.py:405
  250.6 5.5 %collective-permute-done.45 = f32[4,2,4,8,256]{4,3,2,1,0:T(8,128)S(1)} collective-permute-done((f32[4,2,4,8,256]{4,3,2,1,0:T(8,128)}, f32[4,2,4,8,256]{4,3,2,1,0:T(8,128)S(1)}, u32[]{:S(2)}, u32[]{:S(2)}) %collective-permute-start.45) | collective-permute-done | bytes 262176 | tf_op jit(solution)/shard_map/ppermute | solution.py:63
  259.0 6.0 %collective-permute-done.43 = f32[4,2,4,8,256]{4,3,2,1,0:T(8,128)S(1)} collective-permute-done((f32[4,2,4,8,256]{4,3,2,1,0:T(8,128)}, f32[4,2,4,8,256]{4,3,2,1,0:T(8,128)S(1)}, u32[]{:S(2)}, u32[]{:S(2)}) %collective-permute-start.43) | collective-permute-done | bytes 262176 | tf_op jit(solution)/shard_map/ppermute | solution.py:63
  278.2 8.4 %collective-permute-done.49.refs_1_ = f32[2,128,256]{2,1,0:T(8,128)S(1)} collective-permute-done((f32[2,128,256]{2,1,0:T(8,128)S(1)}, f32[2,128,256]{2,1,0:T(8,128)S(1)}, u32[]{:S(2)}, u32[]{:S(2)}) %collective-permute-start.49) | collective-permute-done | bytes 262176 | tf_op jit(solution)/shard_map/ppermute | solution.py:63
  (240 shorter events, 131.5 us)
Async XLA Ops:
  4.3 19.8 %collective-permute-start.1 = (f32[4,2,6,8,256]{4,3,2,1,0:T(8,128)}, f32[4,2,6,8,256]{4,3,2,1,0:T(8,128)S(1)}, u32[]{:S(2)}, u32[]{:S(2)}) collective-permute-start(f32[4,2,6,8,256]{4,3,2,1,0:T(8,128)} %get-tuple-element.100), channel_id=1, source_target_pairs={{0,16},{8,24},{16,0},{24,8},{32,48},{40,56},{48,32},{56,40},{64,80... | collective-permute-start | bytes 1179656 | tf_op jit(solution)/shard_map/ppermute | solution.py:58
  6.9 17.2 %collective-permute-start.2 = (f32[4,2,6,8,256]{4,3,2,1,0:T(8,128)}, f32[4,2,6,8,256]{4,3,2,1,0:T(8,128)}, u32[]{:S(2)}, u32[]{:S(2)}) collective-permute-start(f32[4,2,6,8,256]{4,3,2,1,0:T(8,128)} %get-tuple-element.99), channel_id=1, source_target_pairs={{0,24},{8,0},{16,8},{24,16},{32,56},{40,32},{48,40},{56,48},{64,88... | collective-permute-start | bytes 1179656 | tf_op jit(solution)/shard_map/ppermute | solution.py:58
  34.2 14.1 %collective-permute-start.11 = (f32[4,2,4,2,8,256]{5,4,3,2,1,0:T(8,128)S(1)}, f32[4,2,4,2,8,256]{5,4,3,2,1,0:T(8,128)S(1)}, u32[]{:S(2)}, u32[]{:S(2)}) collective-permute-start(f32[4,2,4,2,8,256]{5,4,3,2,1,0:T(8,128)S(1)} %bitcast.86), channel_id=1, source_target_pairs={{0,8},{8,16},{16,24},{24,0},{32,40},{40,48},{48,56},{56,32},{64,72... | collective-permute-start | bytes 1572872 | tf_op jit(solution)/shard_map/ppermute | solution.py:58
  35.2 24.6 %collective-permute-start.12 = (f32[4,2,4,2,8,256]{5,4,3,2,1,0:T(8,128)S(1)}, f32[4,2,4,2,8,256]{5,4,3,2,1,0:T(8,128)S(1)}, u32[]{:S(2)}, u32[]{:S(2)}) collective-permute-start(f32[4,2,4,2,8,256]{5,4,3,2,1,0:T(8,128)S(1)} %bitcast.85), channel_id=1, source_target_pairs={{0,16},{8,24},{16,0},{24,8},{32,48},{40,56},{48,32},{56,40},{64,80... | collective-permute-start | bytes 1572872 | tf_op jit(solution)/shard_map/ppermute | solution.py:58
  37.4 22.9 %collective-permute-start.13 = (f32[4,2,4,2,8,256]{5,4,3,2,1,0:T(8,128)S(1)}, f32[4,2,4,2,8,256]{5,4,3,2,1,0:T(8,128)S(1)}, u32[]{:S(2)}, u32[]{:S(2)}) collective-permute-start(f32[4,2,4,2,8,256]{5,4,3,2,1,0:T(8,128)S(1)} %bitcast.84), channel_id=1, source_target_pairs={{0,24},{8,0},{16,8},{24,16},{32,56},{40,32},{48,40},{56,48},{64,88... | collective-permute-start | bytes 1572872 | tf_op jit(solution)/shard_map/ppermute | solution.py:58
  40.4 19.9 %collective-permute-start.9 = (f32[4,2,6,8,256]{4,3,2,1,0:T(8,128)S(1)}, f32[4,2,6,8,256]{4,3,2,1,0:T(8,128)S(1)}, u32[]{:S(2)}, u32[]{:S(2)}) collective-permute-start(f32[4,2,6,8,256]{4,3,2,1,0:T(8,128)S(1)} %collective-permute-done.7.refs_13_), channel_id=1, source_target_pairs={{0,1},{1,0},{2,3},{3,2},{4,5},{5,4},{6,7},{7,6},{8,9},{9,8},{10,11... | collective-permute-start | bytes 1179656 | tf_op jit(solution)/shard_map/ppermute | solution.py:67
  45.4 14.9 %collective-permute-start.10 = (f32[4,2,6,8,256]{4,3,2,1,0:T(8,128)S(1)}, f32[4,2,6,8,256]{4,3,2,1,0:T(8,128)}, u32[]{:S(2)}, u32[]{:S(2)}) collective-permute-start(f32[4,2,6,8,256]{4,3,2,1,0:T(8,128)S(1)} %collective-permute-done.8.refs_14_), channel_id=1, source_target_pairs={{0,1},{1,0},{2,3},{3,2},{4,5},{5,4},{6,7},{7,6},{8,9},{9,8},{10,11... | collective-permute-start | bytes 1179656 | tf_op jit(solution)/shard_map/ppermute | solution.py:67
  72.1 15.2 %collective-permute-start.15 = (f32[4,2,4,2,8,256]{5,4,3,2,1,0:T(8,128)}, f32[4,2,4,2,8,256]{5,4,3,2,1,0:T(8,128)S(1)}, u32[]{:S(2)}, u32[]{:S(2)}) collective-permute-start(f32[4,2,4,2,8,256]{5,4,3,2,1,0:T(8,128)} %get-tuple-element.69), channel_id=1, source_target_pairs={{32,0},{40,8},{48,16},{56,24},{64,32},{72,40},{80,48},{88,56},{96,... | collective-permute-start | bytes 1572872 | tf_op jit(solution)/shard_map/ppermute | solution.py:38
  74.0 14.3 %collective-permute-start.14 = (f32[4,2,4,2,8,256]{5,4,3,2,1,0:T(8,128)}, f32[4,2,4,2,8,256]{5,4,3,2,1,0:T(8,128)S(1)}, u32[]{:S(2)}, u32[]{:S(2)}) collective-permute-start(f32[4,2,4,2,8,256]{5,4,3,2,1,0:T(8,128)} %get-tuple-element.68), channel_id=1, source_target_pairs={{0,32},{8,40},{16,48},{24,56},{32,64},{40,72},{48,80},{56,88},{64,... | collective-permute-start | bytes 1572872 | tf_op jit(solution)/shard_map/ppermute | solution.py:38
  78.6 17.3 %collective-permute-start.16 = (f32[4,2,4,2,8,256]{5,4,3,2,1,0:T(8,128)}, f32[4,2,4,2,8,256]{5,4,3,2,1,0:T(8,128)S(1)}, u32[]{:S(2)}, u32[]{:S(2)}) collective-permute-start(f32[4,2,4,2,8,256]{5,4,3,2,1,0:T(8,128)} %get-tuple-element.70), channel_id=1, source_target_pairs={{0,8},{8,16},{16,24},{32,40},{40,48},{48,56},{64,72},{72,80},{80,8... | collective-permute-start | bytes 1572872 | tf_op jit(solution)/shard_map/ppermute | solution.py:38
  83.0 14.1 %collective-permute-start.17 = (f32[4,2,4,2,8,256]{5,4,3,2,1,0:T(8,128)}, f32[4,2,4,2,8,256]{5,4,3,2,1,0:T(8,128)S(1)}, u32[]{:S(2)}, u32[]{:S(2)}) collective-permute-start(f32[4,2,4,2,8,256]{5,4,3,2,1,0:T(8,128)} %get-tuple-element.71), channel_id=1, source_target_pairs={{8,0},{16,8},{24,16},{40,32},{48,40},{56,48},{72,64},{80,72},{88,8... | collective-permute-start | bytes 1572872 | tf_op jit(solution)/shard_map/ppermute | solution.py:38
  122.1 13.6 %collective-permute-start.23 = (f32[4,2,4,8,256]{4,3,2,1,0:T(8,128)}, f32[4,2,4,8,256]{4,3,2,1,0:T(8,128)S(1)}, u32[]{:S(2)}, u32[]{:S(2)}) collective-permute-start(f32[4,2,4,8,256]{4,3,2,1,0:T(8,128)} %get-tuple-element.77), channel_id=1, source_target_pairs={{0,6},{1,7},{2,0},{3,1},{4,2},{5,3},{6,4},{7,5},{8,14},{9,15},{10,... | collective-permute-start | bytes 786440 | tf_op jit(solution)/shard_map/ppermute | solution.py:63
  125.1 15.0 %collective-permute-start.21 = (f32[4,2,4,8,256]{4,3,2,1,0:T(8,128)}, f32[4,2,4,8,256]{4,3,2,1,0:T(8,128)S(1)}, u32[]{:S(2)}, u32[]{:S(2)}) collective-permute-start(f32[4,2,4,8,256]{4,3,2,1,0:T(8,128)} %get-tuple-element.75), channel_id=1, source_target_pairs={{0,2},{1,3},{2,4},{3,5},{4,6},{5,7},{6,0},{7,1},{8,10},{9,11},{10,... | collective-permute-start | bytes 786440 | tf_op jit(solution)/shard_map/ppermute | solution.py:63
  141.2 14.3 %collective-permute-start.24 = (f32[4,2,4,8,256]{4,3,2,1,0:T(8,128)S(1)}, f32[4,2,4,8,256]{4,3,2,1,0:T(8,128)S(1)}, u32[]{:S(2)}, u32[]{:S(2)}) collective-permute-start(f32[4,2,4,8,256]{4,3,2,1,0:T(8,128)S(1)} %exponential_multiply_fusion.refs_0_.refs_5_), channel_id=1, source_target_pairs={{0,2},{1,3},{2,4},{3,5},{4,6},{5,7},{6,0},{7,1},{8,10},{9,11},{10,... | collective-permute-start | bytes 786440 | tf_op jit(solution)/shard_map/ppermute | solution.py:63
  141.3 15.5 %collective-permute-start.25 = (f32[4,2,4,8,256]{4,3,2,1,0:T(8,128)S(1)}, f32[4,2,4,8,256]{4,3,2,1,0:T(8,128)S(1)}, u32[]{:S(2)}, u32[]{:S(2)}) collective-permute-start(f32[4,2,4,8,256]{4,3,2,1,0:T(8,128)S(1)} %exponential_multiply_fusion.refs_0_.refs_5_), channel_id=1, source_target_pairs={{0,4},{1,5},{2,6},{3,7},{4,0},{5,1},{6,2},{7,3},{8,12},{9,13},{10,... | collective-permute-start | bytes 786440 | tf_op jit(solution)/shard_map/ppermute | solution.py:63
  141.9 15.0 %collective-permute-start.26 = (f32[4,2,4,8,256]{4,3,2,1,0:T(8,128)S(1)}, f32[4,2,4,8,256]{4,3,2,1,0:T(8,128)S(1)}, u32[]{:S(2)}, u32[]{:S(2)}) collective-permute-start(f32[4,2,4,8,256]{4,3,2,1,0:T(8,128)S(1)} %exponential_multiply_fusion.refs_0_.refs_5_), channel_id=1, source_target_pairs={{0,6},{1,7},{2,0},{3,1},{4,2},{5,3},{6,4},{7,5},{8,14},{9,15},{10,... | collective-permute-start | bytes 786440 | tf_op jit(solution)/shard_map/ppermute | solution.py:63
  199.6 16.5 %collective-permute-start.37 = (f32[4,2,4,2,8,256]{5,4,3,2,1,0:T(8,128)}, f32[4,2,4,2,8,256]{5,4,3,2,1,0:T(8,128)S(1)}, u32[]{:S(2)}, u32[]{:S(2)}) collective-permute-start(f32[4,2,4,2,8,256]{5,4,3,2,1,0:T(8,128)} %get-tuple-element.84), channel_id=1, source_target_pairs={{32,0},{40,8},{48,16},{56,24},{64,32},{72,40},{80,48},{88,56},{96,... | collective-permute-start | bytes 1572872 | tf_op jit(solution)/shard_map/ppermute | solution.py:38
  201.6 15.5 %collective-permute-start.36 = (f32[4,2,4,2,8,256]{5,4,3,2,1,0:T(8,128)}, f32[4,2,4,2,8,256]{5,4,3,2,1,0:T(8,128)S(1)}, u32[]{:S(2)}, u32[]{:S(2)}) collective-permute-start(f32[4,2,4,2,8,256]{5,4,3,2,1,0:T(8,128)} %get-tuple-element.83), channel_id=1, source_target_pairs={{0,32},{8,40},{16,48},{24,56},{32,64},{40,72},{48,80},{56,88},{64,... | collective-permute-start | bytes 1572872 | tf_op jit(solution)/shard_map/ppermute | solution.py:38
  206.2 15.7 %collective-permute-start.38 = (f32[4,2,4,2,8,256]{5,4,3,2,1,0:T(8,128)}, f32[4,2,4,2,8,256]{5,4,3,2,1,0:T(8,128)S(1)}, u32[]{:S(2)}, u32[]{:S(2)}) collective-permute-start(f32[4,2,4,2,8,256]{5,4,3,2,1,0:T(8,128)} %get-tuple-element.85), channel_id=1, source_target_pairs={{0,8},{8,16},{16,24},{32,40},{40,48},{48,56},{64,72},{72,80},{80,8... | collective-permute-start | bytes 1572872 | tf_op jit(solution)/shard_map/ppermute | solution.py:38
  209.5 14.3 %collective-permute-start.39 = (f32[4,2,4,2,8,256]{5,4,3,2,1,0:T(8,128)}, f32[4,2,4,2,8,256]{5,4,3,2,1,0:T(8,128)S(1)}, u32[]{:S(2)}, u32[]{:S(2)}) collective-permute-start(f32[4,2,4,2,8,256]{5,4,3,2,1,0:T(8,128)} %get-tuple-element.86), channel_id=1, source_target_pairs={{8,0},{16,8},{24,16},{40,32},{48,40},{56,48},{72,64},{80,72},{88,8... | collective-permute-start | bytes 1572872 | tf_op jit(solution)/shard_map/ppermute | solution.py:38
  250.0 15.0 %collective-permute-start.43 = (f32[4,2,4,8,256]{4,3,2,1,0:T(8,128)}, f32[4,2,4,8,256]{4,3,2,1,0:T(8,128)S(1)}, u32[]{:S(2)}, u32[]{:S(2)}) collective-permute-start(f32[4,2,4,8,256]{4,3,2,1,0:T(8,128)} %get-tuple-element.90), channel_id=1, source_target_pairs={{0,2},{1,3},{2,4},{3,5},{4,6},{5,7},{6,0},{7,1},{8,10},{9,11},{10,... | collective-permute-start | bytes 786440 | tf_op jit(solution)/shard_map/ppermute | solution.py:63
  272.9 13.6 %collective-permute-start.49 = (f32[2,128,256]{2,1,0:T(8,128)S(1)}, f32[2,128,256]{2,1,0:T(8,128)S(1)}, u32[]{:S(2)}, u32[]{:S(2)}) collective-permute-start(f32[2,128,256]{2,1,0:T(8,128)S(1)} %bitcast.77), channel_id=1, source_target_pairs={{0,2},{1,3},{2,4},{3,5},{4,6},{5,7},{6,0},{7,1},{8,10},{9,11},{10,... | collective-permute-start | bytes 786440 | tf_op jit(solution)/shard_map/ppermute | solution.py:63
  273.0 15.5 %collective-permute-start.50 = (f32[2,128,256]{2,1,0:T(8,128)S(1)}, f32[2,128,256]{2,1,0:T(8,128)S(1)}, u32[]{:S(2)}, u32[]{:S(2)}) collective-permute-start(f32[2,128,256]{2,1,0:T(8,128)S(1)} %bitcast.78), channel_id=1, source_target_pairs={{0,4},{1,5},{2,6},{3,7},{4,0},{5,1},{6,2},{7,3},{8,12},{9,13},{10,... | collective-permute-start | bytes 786440 | tf_op jit(solution)/shard_map/ppermute | solution.py:63
  274.0 14.7 %collective-permute-start.51 = (f32[2,128,256]{2,1,0:T(8,128)S(1)}, f32[2,128,256]{2,1,0:T(8,128)S(1)}, u32[]{:S(2)}, u32[]{:S(2)}) collective-permute-start(f32[2,128,256]{2,1,0:T(8,128)S(1)} %bitcast.79), channel_id=1, source_target_pairs={{0,6},{1,7},{2,0},{3,1},{4,2},{5,3},{6,4},{7,5},{8,14},{9,15},{10,... | collective-permute-start | bytes 786440 | tf_op jit(solution)/shard_map/ppermute | solution.py:63
  (84 other events, 632.8 us)

commit v5 on v4

--- a/solution.py
+++ b/solution.py
@@ -23,8 +23,8 @@
 STEPS = (((1, 0), (0, 1)), ((-1, 0), (0, -1)), ((1, 1), (1, -1)), ((-1, -1), (-1, 1)))
 
 
-def params():
-    return pltpu.CompilerParams(vmem_limit_bytes=56 * 1024 * 1024)
+def params(mebibytes):
+    return pltpu.CompilerParams(vmem_limit_bytes=mebibytes * 1024 * 1024)
 
 
 def blk_shift(value, dz, dy):
@@ -139,7 +139,7 @@
         out_shape=(ky, kz, kz, kx, kx),
         in_specs=[SMEM, SMEM],
         out_specs=(VMEM,) * 5,
-        compiler_params=params(),
+        compiler_params=params(8),
         name="matrices",
     )(axial_taps, lateral_taps)
 
@@ -169,9 +169,12 @@
                 store_halves(across, q, at, rows[8 * q : 8 * q + 8])
 
     inner()
-    pl.loop(1, 5)(over_rows)
-    outer()
-    pl.loop(0, 2)(lambda n: over_rows(5 * n))
+
+    @pl.loop(0, 6)
+    def _(n):
+        pl.when(n == 4)(outer)
+        over_rows(jnp.where(n < 4, n + 1, 5 * (n - 4)))
+
     ready()
 
     @pl.loop(0, 8)
@@ -344,7 +347,7 @@
             pltpu.SemaphoreType.DMA((4, 2, 3)),
             pltpu.SemaphoreType.DMA((4,)),
         ],
-        compiler_params=params(),
+        compiler_params=params(18),
         name="forward",
     )(*mats, *tile, *shown)
     return got[0], got[1:]
@@ -414,7 +417,7 @@
             pltpu.SemaphoreType.DMA((18,)),
             pltpu.SemaphoreType.DMA((4, 2, 2)),
         ],
-        compiler_params=params(),
+        compiler_params=params(16),
         name="backward",
     )(cover, *mats, center, *halos, *strips)
 
@@ -436,7 +439,7 @@
         out_shape=(part,) * 4,
         in_specs=[VMEM, VMEM],
         out_specs=(VMEM,) * 4,
-        compiler_params=params(),
+        compiler_params=params(8),
         name="shares",
     )(mine, got)
 
@@ -466,7 +469,7 @@
             pltpu.SemaphoreType.DMA((8,)),
             pltpu.SemaphoreType.DMA((4,)),
         ],
-        compiler_params=params(),
+        compiler_params=params(6),
         name="edges",
     )(*pieces)
 
@@ -494,7 +497,7 @@
             pltpu.SemaphoreType.DMA((8,)),
             pltpu.SemaphoreType.DMA((1,)),
         ],
-        compiler_params=params(),
+        compiler_params=params(6),
         name="slab",
     )(*pieces)
 

time: 296 us -> 274 us (0.926)
  Pallas kernels: 54.9 us -> 35.1 us
  waiting for transfers between devices: 117 us -> 114 us
    pallas_call x2, Pallas kernels: 21.6 us -> 16.1 us  [forward(): pl.pallas_call(functools.partial(forward_kernel, first), out_shape=tuple(...]
    pallas_call x2, Pallas kernels: 5.44 us -> 0.35 us  [shares(): pl.pallas_call(shares_kernel, out_shape=(part,) * 4, in_specs=[VMEM, VMEM...]
    pallas_call x2, Pallas kernels: 19.7 us -> 14.9 us  [backward(): pl.pallas_call(backward_kernel, out_shape=(half, half), in_specs=[SMEM] +...]
    unnamed x120 -> x68, local copies, waits for them, and re-layouts: 13.1 us -> 9.04 us
  transfers between devices with their start and end apart: 56 -> 56, of which waited for: 38 -> 37; matrix products, arithmetic and copies ran while one was open for 3% -> 4% of each run, Pallas kernels for 1% -> 1%
where the time goes in v5:
time: 274 us; the launch traced here: 273 us
  waiting for transfers between devices  114 us (42%)
  starting transfers between devices  102 us (37%)
  Pallas kernels  35.1 us (13%)
  local copies, waits for them, and re-layouts  18.3 us (7%)
  other arithmetic  2.82 us (1%)
    ppermute x12, waiting for transfers between devices, x_turn(): return lax.ppermute(value, 'view', pairs)  46.8 us
    ppermute x14, starting transfers between devices, blk_shift(): return lax.ppermute(value, 'blk', pairs)  41 us
    ppermute x14, waiting for transfers between devices, blk_shift(): return lax.ppermute(value, 'blk', pairs)  28.4 us
    ppermute x17, starting transfers between devices, core_swap(): return lax.ppermute(value, 'view', [(i, i ^ 1) for i in range(2 * XD)])  27.2 us
    ppermute x9, waiting for transfers between devices, y_turn(): return lax.ppermute(value, 'blk', pairs)  26.6 us
    pallas_call x2, Pallas kernels, forward(): pl.pallas_call(functools.partial(forward_kernel, first), out_shape=tuple(...  16.1 us
    pallas_call x2, Pallas kernels, backward(): pl.pallas_call(backward_kernel, out_shape=(half, half), in_specs=[SMEM] +...  14.9 us
    ppermute x12, starting transfers between devices, x_turn(): return lax.ppermute(value, 'view', pairs)  12 us
  transfers between devices with their start and end apart: 56, of which 37 were waited for; matrix products, arithmetic and copies ran while one was open for 4% of the time, Pallas kernels for 1%

profile of v5, /device:TPU:97, one launch (start us, length us, event | category | flops | bytes accessed | tf_op | source)
XLA Modules:
  0.0 272.8 jit_solution(6237831354309640988)
XLA Ops:
  18.0 8.5 %collective-permute-done.1.refs_7_ = f32[4,2,6,8,256]{4,3,2,1,0:T(8,128)} collective-permute-done((f32[4,2,6,8,256]{4,3,2,1,0:T(8,128)}, f32[4,2,6,8,256]{4,3,2,1,0:T(8,128)}, u32[]{:S(2)}, u32[]{:S(2)}) %collective-permute-start.1) | collective-permute-done | bytes 393248 | tf_op jit(solution)/shard_map/ppermute | solution.py:58
  30.1 4.8 %collective-permute-start.7 = (f32[4,2,6,8,256]{4,3,2,1,0:T(8,128)S(1)}, f32[4,2,6,8,256]{4,3,2,1,0:T(8,128)S(1)}, u32[]{:S(2)}, u32[]{:S(2)}) collective-permute-start(f32[4,2,6,8,256]{4,3,2,1,0:T(8,128)S(1)} %get-tuple-element.98), channel_id=1, source_target_pairs={{0,32},{8,40},{16,48},{24,56},{32,64},{40,72},{48,80},{56,88},{64,... | collective-permute-start | bytes 1179656 | tf_op jit(solution)/shard_map/ppermute | solution.py:38
  44.1 3.8 %collective-permute-done.8.refs_14_ = f32[4,2,6,8,256]{4,3,2,1,0:T(8,128)S(1)} collective-permute-done((f32[4,2,6,8,256]{4,3,2,1,0:T(8,128)S(1)}, f32[4,2,6,8,256]{4,3,2,1,0:T(8,128)S(1)}, u32[]{:S(2)}, u32[]{:S(2)}) %collective-permute-start.8) | collective-permute-done | bytes 393248 | tf_op jit(solution)/shard_map/ppermute | solution.py:38
  50.9 11.5 %collective-permute-done.12.refs_19_.refs_20_ = f32[4,2,4,2,8,256]{5,4,3,2,1,0:T(8,128)S(1)} collective-permute-done((f32[4,2,4,2,8,256]{5,4,3,2,1,0:T(8,128)S(1)}, f32[4,2,4,2,8,256]{5,4,3,2,1,0:T(8,128)S(1)}, u32[]{:S(2)}, u32[]{:S(2)}) %collective-permute-start.12) | collective-permute-done | bytes 524320 | tf_op jit(solution)/shard_map/ppermute | solution.py:58
  62.8 8.8 %forward.2 = (f32[4,4,2,4,2,8,256]{6,5,4,3,2,1,0:T(8,128)S(1)}, f32[4,2,4,2,8,256]{5,4,3,2,1,0:T(8,128)}, f32[4,2,4,2,8,256]{5,4,3,2,1,0:T(8,128)}, f32[4,2,4,2,...) custom-call(bf16[2,32,144]{2,1,0:T(8,128)(2,1)S(1)} %copy-done.10, bf16[2,64,96]{2,1,0:T(8,128)(2,1)S(1)} %copy-done.13, ...), custom_call_target="tpu_custom_call" | custom-call | tf_op jit(solution)/shard_map/forward/pallas_call | solution.py:336
  76.6 4.6 %collective-permute-start.14 = (f32[4,2,4,2,8,256]{5,4,3,2,1,0:T(8,128)}, f32[4,2,4,2,8,256]{5,4,3,2,1,0:T(8,128)}, u32[]{:S(2)}, u32[]{:S(2)}) collective-permute-start(f32[4,2,4,2,8,256]{5,4,3,2,1,0:T(8,128)} %get-tuple-element.68), channel_id=1, source_target_pairs={{0,32},{8,40},{16,48},{24,56},{32,64},{40,72},{48,80},{56,88},{64,... | collective-permute-start | bytes 1572872 | tf_op jit(solution)/shard_map/ppermute | solution.py:38
  81.3 4.3 %collective-permute-start.16 = (f32[4,2,4,2,8,256]{5,4,3,2,1,0:T(8,128)}, f32[4,2,4,2,8,256]{5,4,3,2,1,0:T(8,128)S(1)}, u32[]{:S(2)}, u32[]{:S(2)}) collective-permute-start(f32[4,2,4,2,8,256]{5,4,3,2,1,0:T(8,128)} %copy-done.20), channel_id=1, source_target_pairs={{0,8},{8,16},{16,24},{32,40},{40,48},{48,56},{64,72},{72,80},{80,8... | collective-permute-start | bytes 1572872 | tf_op jit(solution)/shard_map/ppermute | solution.py:38
  92.0 5.0 %collective-permute-start.18 = (f32[2,2,4,2,8,256]{5,4,3,2,1,0:T(8,128)S(1)}, f32[2,2,4,2,8,256]{5,4,3,2,1,0:T(8,128)S(1)}, u32[]{:S(2)}, u32[]{:S(2)}) collective-permute-start(f32[2,2,4,2,8,256]{5,4,3,2,1,0:T(8,128)S(1)} %pad_maximum_fusion.1), channel_id=1, source_target_pairs={{0,8},{8,16},{16,24},{32,40},{40,48},{48,56},{64,72},{72,80},{80,8... | collective-permute-start | bytes 786440 | tf_op jit(solution)/shard_map/ppermute | solution.py:38
  100.8 3.9 %collective-permute-done.19.refs_11_ = f32[2,2,4,2,8,256]{5,4,3,2,1,0:T(8,128)S(1)} collective-permute-done((f32[2,2,4,2,8,256]{5,4,3,2,1,0:T(8,128)S(1)}, f32[2,2,4,2,8,256]{5,4,3,2,1,0:T(8,128)S(1)}, u32[]{:S(2)}, u32[]{:S(2)}) %collective-permute-start.19) | collective-permute-done | bytes 262176 | tf_op jit(solution)/shard_map/ppermute | solution.py:38
  104.7 7.4 %backward.2 = (f32[4,4,2,4,8,256]{5,4,3,2,1,0:T(8,128)S(1)}, f32[4,4,2,4,8,256]{5,4,3,2,1,0:T(8,128)S(1)}) custom-call(s32[1,2]{1,0:T(1,128)S(1)} %copy-done.18, bf16[2,32,144]{2,1,0:T(8,128)(2,1)S(1)} %copy-done.11, bf16[2,64,96]{2,1,0:T(8,128)(2,1)S(1)} %copy-done.14, bf16[2,64,96]{2,1,0:T(8,128)(2,1)S(1)} %copy-done.17, ...), custom_call_target="tpu_custom_call" | custom-call | tf_op jit(solution)/shard_map/backward/pallas_call | solution.py:408
  121.7 9.5 %collective-permute-done.23 = f32[4,2,4,8,256]{4,3,2,1,0:T(8,128)S(1)} collective-permute-done((f32[4,2,4,8,256]{4,3,2,1,0:T(8,128)S(1)}, f32[4,2,4,8,256]{4,3,2,1,0:T(8,128)S(1)}, u32[]{:S(2)}, u32[]{:S(2)}) %collective-permute-start.23) | collective-permute-done | bytes 262176 | tf_op jit(solution)/shard_map/ppermute | solution.py:63
  131.2 4.6 %collective-permute-done.21 = f32[4,2,4,8,256]{4,3,2,1,0:T(8,128)S(1)} collective-permute-done((f32[4,2,4,8,256]{4,3,2,1,0:T(8,128)S(1)}, f32[4,2,4,8,256]{4,3,2,1,0:T(8,128)S(1)}, u32[]{:S(2)}, u32[]{:S(2)}) %collective-permute-start.21) | collective-permute-done | bytes 262176 | tf_op jit(solution)/shard_map/ppermute | solution.py:63
  139.9 10.2 %collective-permute-done.24.refs_1_.refs_6_ = f32[4,2,4,8,256]{4,3,2,1,0:T(8,128)S(1)} collective-permute-done((f32[4,2,4,8,256]{4,3,2,1,0:T(8,128)S(1)}, f32[4,2,4,8,256]{4,3,2,1,0:T(8,128)S(1)}, u32[]{:S(2)}, u32[]{:S(2)}) %collective-permute-start.24) | collective-permute-done | bytes 262176 | tf_op jit(solution)/shard_map/ppermute | solution.py:63
  159.4 4.9 %collective-permute-start.34 = (f32[2,4,2,8,256]{4,3,2,1,0:T(8,128)S(1)}, f32[2,4,2,8,256]{4,3,2,1,0:T(8,128)S(1)}, u32[]{:S(2)}, u32[]{:S(2)}) collective-permute-start(f32[2,4,2,8,256]{4,3,2,1,0:T(8,128)S(1)} %get-tuple-element.81), channel_id=1, source_target_pairs={{33,9},{35,11},{37,13},{39,15},{40,0},{41,17},{42,2},{43,19},{44,4... | collective-permute-start | bytes 393224 | tf_op jit(solution)/shard_map/ppermute | solution.py:52
  168.5 8.1 %collective-permute-start.35 = (f32[160,8,256]{2,1,0:T(8,128)S(1)}, f32[160,8,256]{2,1,0:T(8,128)S(1)}, u32[]{:S(2)}, u32[]{:S(2)}) collective-permute-start(f32[160,8,256]{2,1,0:T(8,128)S(1)} %pad_maximum_fusion), channel_id=1, source_target_pairs={{0,1},{1,0},{2,3},{3,2},{4,5},{5,4},{6,7},{7,6},{8,9},{9,8},{10,11... | collective-permute-start | bytes 3932168 | tf_op jit(solution)/shard_map/ppermute | solution.py:67
  179.2 7.3 %forward.3 = (f32[4,4,2,4,2,8,256]{6,5,4,3,2,1,0:T(8,128)S(1)}, f32[4,2,4,2,8,256]{5,4,3,2,1,0:T(8,128)S(1)}, f32[4,2,4,2,8,256]{5,4,3,2,1,0:T(8,128)S(1)}, f32[...) custom-call(bf16[2,32,144]{2,1,0:T(8,128)(2,1)S(1)} %copy-done.11, bf16[2,64,96]{2,1,0:T(8,128)(2,1)S(1)} %copy-done.14, ...), custom_call_target="tpu_custom_call" | custom-call | tf_op jit(solution)/shard_map/forward/pallas_call | solution.py:336
  188.4 4.6 %collective-permute-start.36 = (f32[4,2,4,2,8,256]{5,4,3,2,1,0:T(8,128)S(1)}, f32[4,2,4,2,8,256]{5,4,3,2,1,0:T(8,128)S(1)}, u32[]{:S(2)}, u32[]{:S(2)}) collective-permute-start(f32[4,2,4,2,8,256]{5,4,3,2,1,0:T(8,128)S(1)} %get-tuple-element.83), channel_id=1, source_target_pairs={{0,32},{8,40},{16,48},{24,56},{32,64},{40,72},{48,80},{56,88},{64,... | collective-permute-start | bytes 1572872 | tf_op jit(solution)/shard_map/ppermute | solution.py:38
  193.0 3.4 %collective-permute-start.38 = (f32[4,2,4,2,8,256]{5,4,3,2,1,0:T(8,128)S(1)}, f32[4,2,4,2,8,256]{5,4,3,2,1,0:T(8,128)S(1)}, u32[]{:S(2)}, u32[]{:S(2)}) collective-permute-start(f32[4,2,4,2,8,256]{5,4,3,2,1,0:T(8,128)S(1)} %get-tuple-element.85), channel_id=1, source_target_pairs={{0,8},{8,16},{16,24},{32,40},{40,48},{48,56},{64,72},{72,80},{80,8... | collective-permute-start | bytes 1572872 | tf_op jit(solution)/shard_map/ppermute | solution.py:38
  197.7 5.0 %collective-permute-done.37.refs_7_ = f32[4,2,4,2,8,256]{5,4,3,2,1,0:T(8,128)S(1)} collective-permute-done((f32[4,2,4,2,8,256]{5,4,3,2,1,0:T(8,128)S(1)}, f32[4,2,4,2,8,256]{5,4,3,2,1,0:T(8,128)S(1)}, u32[]{:S(2)}, u32[]{:S(2)}) %collective-permute-start.37) | collective-permute-done | bytes 524320 | tf_op jit(solution)/shard_map/ppermute | solution.py:38
  212.2 3.9 %collective-permute-done.41.refs_11_ = f32[2,2,4,2,8,256]{5,4,3,2,1,0:T(8,128)S(1)} collective-permute-done((f32[2,2,4,2,8,256]{5,4,3,2,1,0:T(8,128)S(1)}, f32[2,2,4,2,8,256]{5,4,3,2,1,0:T(8,128)S(1)}, u32[]{:S(2)}, u32[]{:S(2)}) %collective-permute-start.41) | collective-permute-done | bytes 262176 | tf_op jit(solution)/shard_map/ppermute | solution.py:38
  216.1 7.5 %backward.3 = (f32[4,4,2,4,8,256]{5,4,3,2,1,0:T(8,128)S(1)}, f32[4,4,2,4,8,256]{5,4,3,2,1,0:T(8,128)S(1)}) custom-call(s32[1,2]{1,0:T(1,128)S(1)} %copy-done.18, bf16[2,32,144]{2,1,0:T(8,128)(2,1)S(1)} %copy-done.11, bf16[2,64,96]{2,1,0:T(8,128)(2,1)S(1)} %copy-done.14, bf16[2,64,96]{2,1,0:T(8,128)(2,1)S(1)} %copy-done.17, ...), custom_call_target="tpu_custom_call" | custom-call | tf_op jit(solution)/shard_map/backward/pallas_call | solution.py:408
  231.3 5.0 %collective-permute-done.45 = f32[4,2,4,8,256]{4,3,2,1,0:T(8,128)} collective-permute-done((f32[4,2,4,8,256]{4,3,2,1,0:T(8,128)S(1)}, f32[4,2,4,8,256]{4,3,2,1,0:T(8,128)}, u32[]{:S(2)}, u32[]{:S(2)}) %collective-permute-start.45) | collective-permute-done | bytes 262176 | tf_op jit(solution)/shard_map/ppermute | solution.py:63
  239.5 6.0 %collective-permute-done.43 = f32[4,2,4,8,256]{4,3,2,1,0:T(8,128)} collective-permute-done((f32[4,2,4,8,256]{4,3,2,1,0:T(8,128)S(1)}, f32[4,2,4,8,256]{4,3,2,1,0:T(8,128)}, u32[]{:S(2)}, u32[]{:S(2)}) %collective-permute-start.43) | collective-permute-done | bytes 262176 | tf_op jit(solution)/shard_map/ppermute | solution.py:63
  258.8 8.4 %collective-permute-done.49.refs_1_ = f32[2,128,256]{2,1,0:T(8,128)S(1)} collective-permute-done((f32[2,128,256]{2,1,0:T(8,128)S(1)}, f32[2,128,256]{2,1,0:T(8,128)S(1)}, u32[]{:S(2)}, u32[]{:S(2)}) %collective-permute-start.49) | collective-permute-done | bytes 262176 | tf_op jit(solution)/shard_map/ppermute | solution.py:63
  (188 shorter events, 121.4 us)
Async XLA Ops:
  6.6 19.9 %collective-permute-start.1 = (f32[4,2,6,8,256]{4,3,2,1,0:T(8,128)}, f32[4,2,6,8,256]{4,3,2,1,0:T(8,128)}, u32[]{:S(2)}, u32[]{:S(2)}) collective-permute-start(f32[4,2,6,8,256]{4,3,2,1,0:T(8,128)} %get-tuple-element.100), channel_id=1, source_target_pairs={{0,16},{8,24},{16,0},{24,8},{32,48},{40,56},{48,32},{56,40},{64,80... | collective-permute-start | bytes 1179656 | tf_op jit(solution)/shard_map/ppermute | solution.py:58
  9.2 17.3 %collective-permute-start.2 = (f32[4,2,6,8,256]{4,3,2,1,0:T(8,128)}, f32[4,2,6,8,256]{4,3,2,1,0:T(8,128)}, u32[]{:S(2)}, u32[]{:S(2)}) collective-permute-start(f32[4,2,6,8,256]{4,3,2,1,0:T(8,128)} %get-tuple-element.99), channel_id=1, source_target_pairs={{0,24},{8,0},{16,8},{24,16},{32,56},{40,32},{48,40},{56,48},{64,88... | collective-permute-start | bytes 1179656 | tf_op jit(solution)/shard_map/ppermute | solution.py:58
  36.8 14.1 %collective-permute-start.11 = (f32[4,2,4,2,8,256]{5,4,3,2,1,0:T(8,128)S(1)}, f32[4,2,4,2,8,256]{5,4,3,2,1,0:T(8,128)S(1)}, u32[]{:S(2)}, u32[]{:S(2)}) collective-permute-start(f32[4,2,4,2,8,256]{5,4,3,2,1,0:T(8,128)S(1)} %bitcast.86), channel_id=1, source_target_pairs={{0,8},{8,16},{16,24},{24,0},{32,40},{40,48},{48,56},{56,32},{64,72... | collective-permute-start | bytes 1572872 | tf_op jit(solution)/shard_map/ppermute | solution.py:58
  37.7 24.6 %collective-permute-start.12 = (f32[4,2,4,2,8,256]{5,4,3,2,1,0:T(8,128)S(1)}, f32[4,2,4,2,8,256]{5,4,3,2,1,0:T(8,128)S(1)}, u32[]{:S(2)}, u32[]{:S(2)}) collective-permute-start(f32[4,2,4,2,8,256]{5,4,3,2,1,0:T(8,128)S(1)} %bitcast.85), channel_id=1, source_target_pairs={{0,16},{8,24},{16,0},{24,8},{32,48},{40,56},{48,32},{56,40},{64,80... | collective-permute-start | bytes 1572872 | tf_op jit(solution)/shard_map/ppermute | solution.py:58
  39.9 22.9 %collective-permute-start.13 = (f32[4,2,4,2,8,256]{5,4,3,2,1,0:T(8,128)S(1)}, f32[4,2,4,2,8,256]{5,4,3,2,1,0:T(8,128)S(1)}, u32[]{:S(2)}, u32[]{:S(2)}) collective-permute-start(f32[4,2,4,2,8,256]{5,4,3,2,1,0:T(8,128)S(1)} %bitcast.84), channel_id=1, source_target_pairs={{0,24},{8,0},{16,8},{24,16},{32,56},{40,32},{48,40},{56,48},{64,88... | collective-permute-start | bytes 1572872 | tf_op jit(solution)/shard_map/ppermute | solution.py:58
  42.9 19.8 %collective-permute-start.9 = (f32[4,2,6,8,256]{4,3,2,1,0:T(8,128)S(1)}, f32[4,2,6,8,256]{4,3,2,1,0:T(8,128)S(1)}, u32[]{:S(2)}, u32[]{:S(2)}) collective-permute-start(f32[4,2,6,8,256]{4,3,2,1,0:T(8,128)S(1)} %collective-permute-done.7.refs_13_), channel_id=1, source_target_pairs={{0,1},{1,0},{2,3},{3,2},{4,5},{5,4},{6,7},{7,6},{8,9},{9,8},{10,11... | collective-permute-start | bytes 1179656 | tf_op jit(solution)/shard_map/ppermute | solution.py:67
  47.9 14.8 %collective-permute-start.10 = (f32[4,2,6,8,256]{4,3,2,1,0:T(8,128)S(1)}, f32[4,2,6,8,256]{4,3,2,1,0:T(8,128)S(1)}, u32[]{:S(2)}, u32[]{:S(2)}) collective-permute-start(f32[4,2,6,8,256]{4,3,2,1,0:T(8,128)S(1)} %collective-permute-done.8.refs_14_), channel_id=1, source_target_pairs={{0,1},{1,0},{2,3},{3,2},{4,5},{5,4},{6,7},{7,6},{8,9},{9,8},{10,11... | collective-permute-start | bytes 1179656 | tf_op jit(solution)/shard_map/ppermute | solution.py:67
  74.6 15.4 %collective-permute-start.15 = (f32[4,2,4,2,8,256]{5,4,3,2,1,0:T(8,128)}, f32[4,2,4,2,8,256]{5,4,3,2,1,0:T(8,128)}, u32[]{:S(2)}, u32[]{:S(2)}) collective-permute-start(f32[4,2,4,2,8,256]{5,4,3,2,1,0:T(8,128)} %get-tuple-element.69), channel_id=1, source_target_pairs={{32,0},{40,8},{48,16},{56,24},{64,32},{72,40},{80,48},{88,56},{96,... | collective-permute-start | bytes 1572872 | tf_op jit(solution)/shard_map/ppermute | solution.py:38
  76.6 14.3 %collective-permute-start.14 = (f32[4,2,4,2,8,256]{5,4,3,2,1,0:T(8,128)}, f32[4,2,4,2,8,256]{5,4,3,2,1,0:T(8,128)}, u32[]{:S(2)}, u32[]{:S(2)}) collective-permute-start(f32[4,2,4,2,8,256]{5,4,3,2,1,0:T(8,128)} %get-tuple-element.68), channel_id=1, source_target_pairs={{0,32},{8,40},{16,48},{24,56},{32,64},{40,72},{48,80},{56,88},{64,... | collective-permute-start | bytes 1572872 | tf_op jit(solution)/shard_map/ppermute | solution.py:38
  81.3 17.1 %collective-permute-start.16 = (f32[4,2,4,2,8,256]{5,4,3,2,1,0:T(8,128)}, f32[4,2,4,2,8,256]{5,4,3,2,1,0:T(8,128)S(1)}, u32[]{:S(2)}, u32[]{:S(2)}) collective-permute-start(f32[4,2,4,2,8,256]{5,4,3,2,1,0:T(8,128)} %copy-done.20), channel_id=1, source_target_pairs={{0,8},{8,16},{16,24},{32,40},{40,48},{48,56},{64,72},{72,80},{80,8... | collective-permute-start | bytes 1572872 | tf_op jit(solution)/shard_map/ppermute | solution.py:38
  85.6 13.9 %collective-permute-start.17 = (f32[4,2,4,2,8,256]{5,4,3,2,1,0:T(8,128)}, f32[4,2,4,2,8,256]{5,4,3,2,1,0:T(8,128)S(1)}, u32[]{:S(2)}, u32[]{:S(2)}) collective-permute-start(f32[4,2,4,2,8,256]{5,4,3,2,1,0:T(8,128)} %copy-done.19), channel_id=1, source_target_pairs={{8,0},{16,8},{24,16},{40,32},{48,40},{56,48},{72,64},{80,72},{88,8... | collective-permute-start | bytes 1572872 | tf_op jit(solution)/shard_map/ppermute | solution.py:38
  121.0 14.7 %collective-permute-start.21 = (f32[4,2,4,8,256]{4,3,2,1,0:T(8,128)S(1)}, f32[4,2,4,8,256]{4,3,2,1,0:T(8,128)S(1)}, u32[]{:S(2)}, u32[]{:S(2)}) collective-permute-start(f32[4,2,4,8,256]{4,3,2,1,0:T(8,128)S(1)} %get-tuple-element.75), channel_id=1, source_target_pairs={{0,2},{1,3},{2,4},{3,5},{4,6},{5,7},{6,0},{7,1},{8,10},{9,11},{10,... | collective-permute-start | bytes 786440 | tf_op jit(solution)/shard_map/ppermute | solution.py:63
  135.8 14.3 %collective-permute-start.24 = (f32[4,2,4,8,256]{4,3,2,1,0:T(8,128)S(1)}, f32[4,2,4,8,256]{4,3,2,1,0:T(8,128)S(1)}, u32[]{:S(2)}, u32[]{:S(2)}) collective-permute-start(f32[4,2,4,8,256]{4,3,2,1,0:T(8,128)S(1)} %exponential_multiply_fusion.refs_0_.refs_5_), channel_id=1, source_target_pairs={{0,2},{1,3},{2,4},{3,5},{4,6},{5,7},{6,0},{7,1},{8,10},{9,11},{10,... | collective-permute-start | bytes 786440 | tf_op jit(solution)/shard_map/ppermute | solution.py:63
  135.9 15.5 %collective-permute-start.25 = (f32[4,2,4,8,256]{4,3,2,1,0:T(8,128)S(1)}, f32[4,2,4,8,256]{4,3,2,1,0:T(8,128)S(1)}, u32[]{:S(2)}, u32[]{:S(2)}) collective-permute-start(f32[4,2,4,8,256]{4,3,2,1,0:T(8,128)S(1)} %exponential_multiply_fusion.refs_0_.refs_5_), channel_id=1, source_target_pairs={{0,4},{1,5},{2,6},{3,7},{4,0},{5,1},{6,2},{7,3},{8,12},{9,13},{10,... | collective-permute-start | bytes 786440 | tf_op jit(solution)/shard_map/ppermute | solution.py:63
  136.6 14.9 %collective-permute-start.26 = (f32[4,2,4,8,256]{4,3,2,1,0:T(8,128)S(1)}, f32[4,2,4,8,256]{4,3,2,1,0:T(8,128)S(1)}, u32[]{:S(2)}, u32[]{:S(2)}) collective-permute-start(f32[4,2,4,8,256]{4,3,2,1,0:T(8,128)S(1)} %exponential_multiply_fusion.refs_0_.refs_5_), channel_id=1, source_target_pairs={{0,6},{1,7},{2,0},{3,1},{4,2},{5,3},{6,4},{7,5},{8,14},{9,15},{10,... | collective-permute-start | bytes 786440 | tf_op jit(solution)/shard_map/ppermute | solution.py:63
  153.9 13.7 %collective-permute-start.31 = (f32[2,4,2,4,8,256]{5,4,3,2,1,0:T(8,128)S(1)}, f32[2,4,2,4,8,256]{5,4,3,2,1,0:T(8,128)S(1)}, u32[]{:S(2)}, u32[]{:S(2)}) collective-permute-start(f32[2,4,2,4,8,256]{5,4,3,2,1,0:T(8,128)S(1)} %get-tuple-element.78), channel_id=1, source_target_pairs={{0,32},{1,9},{2,34},{3,11},{4,36},{5,13},{6,38},{7,15},{8,40},{9,1... | collective-permute-start | bytes 1572872 | tf_op jit(solution)/shard_map/ppermute | solution.py:52
  186.5 16.2 %collective-permute-start.37 = (f32[4,2,4,2,8,256]{5,4,3,2,1,0:T(8,128)S(1)}, f32[4,2,4,2,8,256]{5,4,3,2,1,0:T(8,128)S(1)}, u32[]{:S(2)}, u32[]{:S(2)}) collective-permute-start(f32[4,2,4,2,8,256]{5,4,3,2,1,0:T(8,128)S(1)} %get-tuple-element.84), channel_id=1, source_target_pairs={{32,0},{40,8},{48,16},{56,24},{64,32},{72,40},{80,48},{88,56},{96,... | collective-permute-start | bytes 1572872 | tf_op jit(solution)/shard_map/ppermute | solution.py:38
  188.4 15.1 %collective-permute-start.36 = (f32[4,2,4,2,8,256]{5,4,3,2,1,0:T(8,128)S(1)}, f32[4,2,4,2,8,256]{5,4,3,2,1,0:T(8,128)S(1)}, u32[]{:S(2)}, u32[]{:S(2)}) collective-permute-start(f32[4,2,4,2,8,256]{5,4,3,2,1,0:T(8,128)S(1)} %get-tuple-element.83), channel_id=1, source_target_pairs={{0,32},{8,40},{16,48},{24,56},{32,64},{40,72},{48,80},{56,88},{64,... | collective-permute-start | bytes 1572872 | tf_op jit(solution)/shard_map/ppermute | solution.py:38
  193.0 15.3 %collective-permute-start.38 = (f32[4,2,4,2,8,256]{5,4,3,2,1,0:T(8,128)S(1)}, f32[4,2,4,2,8,256]{5,4,3,2,1,0:T(8,128)S(1)}, u32[]{:S(2)}, u32[]{:S(2)}) collective-permute-start(f32[4,2,4,2,8,256]{5,4,3,2,1,0:T(8,128)S(1)} %get-tuple-element.85), channel_id=1, source_target_pairs={{0,8},{8,16},{16,24},{32,40},{40,48},{48,56},{64,72},{72,80},{80,8... | collective-permute-start | bytes 1572872 | tf_op jit(solution)/shard_map/ppermute | solution.py:38
  196.4 14.1 %collective-permute-start.39 = (f32[4,2,4,2,8,256]{5,4,3,2,1,0:T(8,128)S(1)}, f32[4,2,4,2,8,256]{5,4,3,2,1,0:T(8,128)S(1)}, u32[]{:S(2)}, u32[]{:S(2)}) collective-permute-start(f32[4,2,4,2,8,256]{5,4,3,2,1,0:T(8,128)S(1)} %get-tuple-element.86), channel_id=1, source_target_pairs={{8,0},{16,8},{24,16},{40,32},{48,40},{56,48},{72,64},{80,72},{88,8... | collective-permute-start | bytes 1572872 | tf_op jit(solution)/shard_map/ppermute | solution.py:38
  230.6 14.9 %collective-permute-start.43 = (f32[4,2,4,8,256]{4,3,2,1,0:T(8,128)S(1)}, f32[4,2,4,8,256]{4,3,2,1,0:T(8,128)}, u32[]{:S(2)}, u32[]{:S(2)}) collective-permute-start(f32[4,2,4,8,256]{4,3,2,1,0:T(8,128)S(1)} %get-tuple-element.90), channel_id=1, source_target_pairs={{0,2},{1,3},{2,4},{3,5},{4,6},{5,7},{6,0},{7,1},{8,10},{9,11},{10,... | collective-permute-start | bytes 786440 | tf_op jit(solution)/shard_map/ppermute | solution.py:63
  253.5 13.6 %collective-permute-start.49 = (f32[2,128,256]{2,1,0:T(8,128)S(1)}, f32[2,128,256]{2,1,0:T(8,128)S(1)}, u32[]{:S(2)}, u32[]{:S(2)}) collective-permute-start(f32[2,128,256]{2,1,0:T(8,128)S(1)} %bitcast.75), channel_id=1, source_target_pairs={{0,2},{1,3},{2,4},{3,5},{4,6},{5,7},{6,0},{7,1},{8,10},{9,11},{10,... | collective-permute-start | bytes 786440 | tf_op jit(solution)/shard_map/ppermute | solution.py:63
  253.6 15.5 %collective-permute-start.50 = (f32[2,128,256]{2,1,0:T(8,128)S(1)}, f32[2,128,256]{2,1,0:T(8,128)S(1)}, u32[]{:S(2)}, u32[]{:S(2)}) collective-permute-start(f32[2,128,256]{2,1,0:T(8,128)S(1)} %bitcast.76), channel_id=1, source_target_pairs={{0,4},{1,5},{2,6},{3,7},{4,0},{5,1},{6,2},{7,3},{8,12},{9,13},{10,... | collective-permute-start | bytes 786440 | tf_op jit(solution)/shard_map/ppermute | solution.py:63
  254.6 14.6 %collective-permute-start.51 = (f32[2,128,256]{2,1,0:T(8,128)S(1)}, f32[2,128,256]{2,1,0:T(8,128)S(1)}, u32[]{:S(2)}, u32[]{:S(2)}) collective-permute-start(f32[2,128,256]{2,1,0:T(8,128)S(1)} %bitcast.77), channel_id=1, source_target_pairs={{0,6},{1,7},{2,0},{3,1},{4,2},{5,3},{6,4},{7,5},{8,14},{9,15},{10,... | collective-permute-start | bytes 786440 | tf_op jit(solution)/shard_map/ppermute | solution.py:63
  (58 other events, 592.4 us)

commit v6 on v5

--- a/solution.py
+++ b/solution.py
@@ -528,7 +528,7 @@
     pieces = [est_rows(0)] + [y_turn(est_rows(k), k) for k in (1, 2, 3)]
     mats = matrices(axial_taps, lateral_taps)
     shown = [view_rows(k) for k in range(4)]
-    pieces, mats, shown = lax.optimization_barrier((pieces, mats, shown))
+    pieces, mats = lax.optimization_barrier((pieces, mats))
     shown = [shown[0]] + [y_turn(shown[k], k) for k in (1, 2, 3)]
     share = [lax.dynamic_index_in_dim(p, x, 0, keepdims=False)[:, 1:5] for p in pieces]
     share = by_block(share, y)
@@ -538,6 +538,7 @@
             bottom = lax.select_n(y, *pieces)
             beside = [blk_shift(top, 1, 0), blk_shift(bottom, -1, 0)]
             tile = pieces + [core_swap(piece) for piece in pieces]
+            beside, shown = lax.optimization_barrier((beside, shown))
             tile += beside + [core_swap(part) for part in beside]
         else:
             pieces = gathered(share)

time: 274 us -> 265 us (0.967)
  starting transfers between devices: 102 us -> 96.3 us
    ppermute x14, waiting for transfers between devices: 28.4 us -> 24.8 us  [blk_shift(): return lax.ppermute(value, 'blk', pairs)]
    unnamed x68 -> x56, local copies, waits for them, and re-layouts: 9.04 us -> 7.19 us
  transfers between devices with their start and end apart: 56 -> 56, of which waited for: 37 -> 39; matrix products, arithmetic and copies ran while one was open for 4% -> 4% of each run, Pallas kernels for 1% -> 1%
where the time goes in v6:
time: 265 us; the launch traced here: 264 us
  waiting for transfers between devices  112 us (42%)
  starting transfers between devices  96.3 us (36%)
  Pallas kernels  35.3 us (13%)
  local copies, waits for them, and re-layouts  17.3 us (7%)
  other arithmetic  2.82 us (1%)
    ppermute x12, waiting for transfers between devices, x_turn(): return lax.ppermute(value, 'view', pairs)  47.6 us
    ppermute x14, starting transfers between devices, blk_shift(): return lax.ppermute(value, 'blk', pairs)  40.4 us
    ppermute x17, starting transfers between devices, core_swap(): return lax.ppermute(value, 'view', [(i, i ^ 1) for i in range(2 * XD)])  24.9 us
    ppermute x14, waiting for transfers between devices, blk_shift(): return lax.ppermute(value, 'blk', pairs)  24.8 us
    ppermute x9, waiting for transfers between devices, y_turn(): return lax.ppermute(value, 'blk', pairs)  24.6 us
    pallas_call x2, Pallas kernels, forward(): pl.pallas_call(functools.partial(forward_kernel, first), out_shape=tuple(...  16.3 us
    pallas_call x2, Pallas kernels, backward(): pl.pallas_call(backward_kernel, out_shape=(half, half), in_specs=[SMEM] +...  14.9 us
    ppermute x12, starting transfers between devices, x_turn(): return lax.ppermute(value, 'view', pairs)  12 us
  transfers between devices with their start and end apart: 56, of which 39 were waited for; matrix products, arithmetic and copies ran while one was open for 4% of the time, Pallas kernels for 1%

profile of v6, /device:TPU:97, one launch (start us, length us, event | category | flops | bytes accessed | tf_op | source)
XLA Modules:
  0.0 264.1 jit_solution(12571655213174235054)
XLA Ops:
  19.1 7.4 %collective-permute-done.1.refs_7_ = f32[4,2,6,8,256]{4,3,2,1,0:T(8,128)} collective-permute-done((f32[4,2,6,8,256]{4,3,2,1,0:T(8,128)}, f32[4,2,6,8,256]{4,3,2,1,0:T(8,128)}, u32[]{:S(2)}, u32[]{:S(2)}) %collective-permute-start.1) | collective-permute-done | bytes 393248 | tf_op jit(solution)/shard_map/ppermute | solution.py:58
  28.0 4.8 %collective-permute-start.7 = (f32[4,2,6,8,256]{4,3,2,1,0:T(8,128)S(1)}, f32[4,2,6,8,256]{4,3,2,1,0:T(8,128)S(1)}, u32[]{:S(2)}, u32[]{:S(2)}) collective-permute-start(f32[4,2,6,8,256]{4,3,2,1,0:T(8,128)S(1)} %get-tuple-element.102), channel_id=1, source_target_pairs={{0,32},{8,40},{16,48},{24,56},{32,64},{40,72},{48,80},{56,88},{64,... | collective-permute-start | bytes 1179656 | tf_op jit(solution)/shard_map/ppermute | solution.py:38
  38.8 10.2 %collective-permute-done.10.refs_19_.refs_20_ = f32[4,2,4,2,8,256]{5,4,3,2,1,0:T(8,128)} collective-permute-done((f32[4,2,4,2,8,256]{5,4,3,2,1,0:T(8,128)}, f32[4,2,4,2,8,256]{5,4,3,2,1,0:T(8,128)}, u32[]{:S(2)}, u32[]{:S(2)}) %collective-permute-start.10) | collective-permute-done | bytes 524320 | tf_op jit(solution)/shard_map/ppermute | solution.py:58
  54.1 9.0 %forward.2 = (f32[4,4,2,4,2,8,256]{6,5,4,3,2,1,0:T(8,128)S(1)}, f32[4,2,4,2,8,256]{5,4,3,2,1,0:T(8,128)}, f32[4,2,4,2,8,256]{5,4,3,2,1,0:T(8,128)}, f32[4,2,4,2,...) custom-call(bf16[2,32,144]{2,1,0:T(8,128)(2,1)S(1)} %get-tuple-element.60.refs_0_, ...), custom_call_target="tpu_custom_call" | custom-call | tf_op jit(solution)/shard_map/forward/pallas_call | solution.py:336
  68.2 4.8 %collective-permute-start.14 = (f32[4,2,4,2,8,256]{5,4,3,2,1,0:T(8,128)}, f32[4,2,4,2,8,256]{5,4,3,2,1,0:T(8,128)}, u32[]{:S(2)}, u32[]{:S(2)}) collective-permute-start(f32[4,2,4,2,8,256]{5,4,3,2,1,0:T(8,128)} %get-tuple-element.72), channel_id=1, source_target_pairs={{0,32},{8,40},{16,48},{24,56},{32,64},{40,72},{48,80},{56,88},{64,... | collective-permute-start | bytes 1572872 | tf_op jit(solution)/shard_map/ppermute | solution.py:38
  73.0 6.6 %collective-permute-start.16 = (f32[4,2,4,2,8,256]{5,4,3,2,1,0:T(8,128)}, f32[4,2,4,2,8,256]{5,4,3,2,1,0:T(8,128)S(1)}, u32[]{:S(2)}, u32[]{:S(2)}) collective-permute-start(f32[4,2,4,2,8,256]{5,4,3,2,1,0:T(8,128)} %copy-done.16), channel_id=1, source_target_pairs={{0,8},{8,16},{16,24},{32,40},{40,48},{48,56},{64,72},{72,80},{80,8... | collective-permute-start | bytes 1572872 | tf_op jit(solution)/shard_map/ppermute | solution.py:38
  85.3 6.1 %collective-permute-start.18 = (f32[2,2,4,2,8,256]{5,4,3,2,1,0:T(8,128)S(1)}, f32[2,2,4,2,8,256]{5,4,3,2,1,0:T(8,128)S(1)}, u32[]{:S(2)}, u32[]{:S(2)}) collective-permute-start(f32[2,2,4,2,8,256]{5,4,3,2,1,0:T(8,128)S(1)} %pad_maximum_fusion.1), channel_id=1, source_target_pairs={{0,8},{8,16},{16,24},{32,40},{40,48},{48,56},{64,72},{72,80},{80,8... | collective-permute-start | bytes 786440 | tf_op jit(solution)/shard_map/ppermute | solution.py:38
  95.4 3.9 %collective-permute-done.19.refs_11_ = f32[2,2,4,2,8,256]{5,4,3,2,1,0:T(8,128)S(1)} collective-permute-done((f32[2,2,4,2,8,256]{5,4,3,2,1,0:T(8,128)S(1)}, f32[2,2,4,2,8,256]{5,4,3,2,1,0:T(8,128)S(1)}, u32[]{:S(2)}, u32[]{:S(2)}) %collective-permute-start.19) | collective-permute-done | bytes 262176 | tf_op jit(solution)/shard_map/ppermute | solution.py:38
  99.3 7.4 %backward.2 = (f32[4,4,2,4,8,256]{5,4,3,2,1,0:T(8,128)S(1)}, f32[4,4,2,4,8,256]{5,4,3,2,1,0:T(8,128)S(1)}) custom-call(s32[1,2]{1,0:T(1,128)S(1)} %copy-done.14, bf16[2,32,144]{2,1,0:T(8,128)(2,1)S(1)} %copy-done.9, bf16[2,64,96]{2,1,0:T(8,128)(2,1)S(1)} %copy-done.11, bf16[2,64,96]{2,1,0:T(8,128)(2,1)S(1)} %copy-done.13, ...), custom_call_target="tpu_custom_call" | custom-call | tf_op jit(solution)/shard_map/backward/pallas_call | solution.py:408
  106.8 2.9 %collective-permute-start.20 = (f32[4,4,2,4,8,256]{5,4,3,2,1,0:T(8,128)S(1)}, f32[4,4,2,4,8,256]{5,4,3,2,1,0:T(8,128)S(1)}, u32[]{:S(2)}, u32[]{:S(2)}) collective-permute-start(f32[4,4,2,4,8,256]{5,4,3,2,1,0:T(8,128)S(1)} %get-tuple-element.77), channel_id=1, source_target_pairs={{0,1},{1,0},{2,3},{3,2},{4,5},{5,4},{6,7},{7,6},{8,9},{9,8},{10,11... | collective-permute-start | bytes 3145736 | tf_op jit(solution)/shard_map/ppermute | solution.py:67
  116.0 9.5 %collective-permute-done.23 = f32[4,2,4,8,256]{4,3,2,1,0:T(8,128)S(1)} collective-permute-done((f32[4,2,4,8,256]{4,3,2,1,0:T(8,128)S(1)}, f32[4,2,4,8,256]{4,3,2,1,0:T(8,128)S(1)}, u32[]{:S(2)}, u32[]{:S(2)}) %collective-permute-start.23) | collective-permute-done | bytes 262176 | tf_op jit(solution)/shard_map/ppermute | solution.py:63
  125.5 4.6 %collective-permute-done.21 = f32[4,2,4,8,256]{4,3,2,1,0:T(8,128)S(1)} collective-permute-done((f32[4,2,4,8,256]{4,3,2,1,0:T(8,128)S(1)}, f32[4,2,4,8,256]{4,3,2,1,0:T(8,128)S(1)}, u32[]{:S(2)}, u32[]{:S(2)}) %collective-permute-start.21) | collective-permute-done | bytes 262176 | tf_op jit(solution)/shard_map/ppermute | solution.py:63
  134.3 10.2 %collective-permute-done.24.refs_1_.refs_6_ = f32[4,2,4,8,256]{4,3,2,1,0:T(8,128)S(1)} collective-permute-done((f32[4,2,4,8,256]{4,3,2,1,0:T(8,128)S(1)}, f32[4,2,4,8,256]{4,3,2,1,0:T(8,128)S(1)}, u32[]{:S(2)}, u32[]{:S(2)}) %collective-permute-start.24) | collective-permute-done | bytes 262176 | tf_op jit(solution)/shard_map/ppermute | solution.py:63
  152.8 4.9 %collective-permute-start.34 = (f32[2,4,2,8,256]{4,3,2,1,0:T(8,128)S(1)}, f32[2,4,2,8,256]{4,3,2,1,0:T(8,128)S(1)}, u32[]{:S(2)}, u32[]{:S(2)}) collective-permute-start(f32[2,4,2,8,256]{4,3,2,1,0:T(8,128)S(1)} %get-tuple-element.85), channel_id=1, source_target_pairs={{33,9},{35,11},{37,13},{39,15},{40,0},{41,17},{42,2},{43,19},{44,4... | collective-permute-start | bytes 393224 | tf_op jit(solution)/shard_map/ppermute | solution.py:52
  161.9 8.1 %collective-permute-start.35 = (f32[160,8,256]{2,1,0:T(8,128)S(1)}, f32[160,8,256]{2,1,0:T(8,128)S(1)}, u32[]{:S(2)}, u32[]{:S(2)}) collective-permute-start(f32[160,8,256]{2,1,0:T(8,128)S(1)} %pad_maximum_fusion), channel_id=1, source_target_pairs={{0,1},{1,0},{2,3},{3,2},{4,5},{5,4},{6,7},{7,6},{8,9},{9,8},{10,11... | collective-permute-start | bytes 3932168 | tf_op jit(solution)/shard_map/ppermute | solution.py:67
  172.6 7.2 %forward.3 = (f32[4,4,2,4,2,8,256]{6,5,4,3,2,1,0:T(8,128)S(1)}, f32[4,2,4,2,8,256]{5,4,3,2,1,0:T(8,128)S(1)}, f32[4,2,4,2,8,256]{5,4,3,2,1,0:T(8,128)S(1)}, f32[...) custom-call(bf16[2,32,144]{2,1,0:T(8,128)(2,1)S(1)} %copy-done.9, bf16[2,64,96]{2,1,0:T(8,128)(2,1)S(1)} %copy-done.11, ...), custom_call_target="tpu_custom_call" | custom-call | tf_op jit(solution)/shard_map/forward/pallas_call | solution.py:336
  181.8 4.6 %collective-permute-start.36 = (f32[4,2,4,2,8,256]{5,4,3,2,1,0:T(8,128)S(1)}, f32[4,2,4,2,8,256]{5,4,3,2,1,0:T(8,128)S(1)}, u32[]{:S(2)}, u32[]{:S(2)}) collective-permute-start(f32[4,2,4,2,8,256]{5,4,3,2,1,0:T(8,128)S(1)} %get-tuple-element.87), channel_id=1, source_target_pairs={{0,32},{8,40},{16,48},{24,56},{32,64},{40,72},{48,80},{56,88},{64,... | collective-permute-start | bytes 1572872 | tf_op jit(solution)/shard_map/ppermute | solution.py:38
  189.0 7.1 %collective-permute-done.37.refs_7_ = f32[4,2,4,2,8,256]{5,4,3,2,1,0:T(8,128)S(1)} collective-permute-done((f32[4,2,4,2,8,256]{5,4,3,2,1,0:T(8,128)S(1)}, f32[4,2,4,2,8,256]{5,4,3,2,1,0:T(8,128)S(1)}, u32[]{:S(2)}, u32[]{:S(2)}) %collective-permute-start.37) | collective-permute-done | bytes 524320 | tf_op jit(solution)/shard_map/ppermute | solution.py:38
  203.7 3.9 %collective-permute-done.41.refs_11_ = f32[2,2,4,2,8,256]{5,4,3,2,1,0:T(8,128)S(1)} collective-permute-done((f32[2,2,4,2,8,256]{5,4,3,2,1,0:T(8,128)S(1)}, f32[2,2,4,2,8,256]{5,4,3,2,1,0:T(8,128)S(1)}, u32[]{:S(2)}, u32[]{:S(2)}) %collective-permute-start.41) | collective-permute-done | bytes 262176 | tf_op jit(solution)/shard_map/ppermute | solution.py:38
  207.5 7.5 %backward.3 = (f32[4,4,2,4,8,256]{5,4,3,2,1,0:T(8,128)S(1)}, f32[4,4,2,4,8,256]{5,4,3,2,1,0:T(8,128)S(1)}) custom-call(s32[1,2]{1,0:T(1,128)S(1)} %copy-done.14, bf16[2,32,144]{2,1,0:T(8,128)(2,1)S(1)} %copy-done.9, bf16[2,64,96]{2,1,0:T(8,128)(2,1)S(1)} %copy-done.11, bf16[2,64,96]{2,1,0:T(8,128)(2,1)S(1)} %copy-done.13, ...), custom_call_target="tpu_custom_call" | custom-call | tf_op jit(solution)/shard_map/backward/pallas_call | solution.py:408
  222.6 5.0 %collective-permute-done.45 = f32[4,2,4,8,256]{4,3,2,1,0:T(8,128)} collective-permute-done((f32[4,2,4,8,256]{4,3,2,1,0:T(8,128)S(1)}, f32[4,2,4,8,256]{4,3,2,1,0:T(8,128)}, u32[]{:S(2)}, u32[]{:S(2)}) %collective-permute-start.45) | collective-permute-done | bytes 262176 | tf_op jit(solution)/shard_map/ppermute | solution.py:63
  227.6 3.2 %collective-permute-done.44 = f32[4,2,4,8,256]{4,3,2,1,0:T(8,128)} collective-permute-done((f32[4,2,4,8,256]{4,3,2,1,0:T(8,128)S(1)}, f32[4,2,4,8,256]{4,3,2,1,0:T(8,128)}, u32[]{:S(2)}, u32[]{:S(2)}) %collective-permute-start.44) | collective-permute-done | bytes 262176 | tf_op jit(solution)/shard_map/ppermute | solution.py:63
  230.8 6.0 %collective-permute-done.43 = f32[4,2,4,8,256]{4,3,2,1,0:T(8,128)} collective-permute-done((f32[4,2,4,8,256]{4,3,2,1,0:T(8,128)S(1)}, f32[4,2,4,8,256]{4,3,2,1,0:T(8,128)}, u32[]{:S(2)}, u32[]{:S(2)}) %collective-permute-start.43) | collective-permute-done | bytes 262176 | tf_op jit(solution)/shard_map/ppermute | solution.py:63
  249.9 9.1 %collective-permute-done.49.refs_1_ = f32[2,128,256]{2,1,0:T(8,128)S(1)} collective-permute-done((f32[2,128,256]{2,1,0:T(8,128)S(1)}, f32[2,128,256]{2,1,0:T(8,128)S(1)}, u32[]{:S(2)}, u32[]{:S(2)}) %collective-permute-start.49) | collective-permute-done | bytes 262176 | tf_op jit(solution)/shard_map/ppermute | solution.py:63
  (176 shorter events, 109.4 us)
Async XLA Ops:
  6.6 19.9 %collective-permute-start.1 = (f32[4,2,6,8,256]{4,3,2,1,0:T(8,128)}, f32[4,2,6,8,256]{4,3,2,1,0:T(8,128)}, u32[]{:S(2)}, u32[]{:S(2)}) collective-permute-start(f32[4,2,6,8,256]{4,3,2,1,0:T(8,128)} %get-tuple-element.104), channel_id=1, source_target_pairs={{0,16},{8,24},{16,0},{24,8},{32,48},{40,56},{48,32},{56,40},{64,80... | collective-permute-start | bytes 1179656 | tf_op jit(solution)/shard_map/ppermute | solution.py:58
  9.2 17.4 %collective-permute-start.2 = (f32[4,2,6,8,256]{4,3,2,1,0:T(8,128)}, f32[4,2,6,8,256]{4,3,2,1,0:T(8,128)}, u32[]{:S(2)}, u32[]{:S(2)}) collective-permute-start(f32[4,2,6,8,256]{4,3,2,1,0:T(8,128)} %get-tuple-element.103), channel_id=1, source_target_pairs={{0,24},{8,0},{16,8},{24,16},{32,56},{40,32},{48,40},{56,48},{64,88... | collective-permute-start | bytes 1179656 | tf_op jit(solution)/shard_map/ppermute | solution.py:58
  13.6 23.0 %collective-permute-start.9 = (f32[4,2,4,2,8,256]{5,4,3,2,1,0:T(8,128)}, f32[4,2,4,2,8,256]{5,4,3,2,1,0:T(8,128)S(1)}, u32[]{:S(2)}, u32[]{:S(2)}) collective-permute-start(f32[4,2,4,2,8,256]{5,4,3,2,1,0:T(8,128)} %bitcast.13), channel_id=1, source_target_pairs={{0,8},{8,16},{16,24},{24,0},{32,40},{40,48},{48,56},{56,32},{64,72... | collective-permute-start | bytes 1572872 | tf_op jit(solution)/shard_map/ppermute | solution.py:58
  14.8 34.1 %collective-permute-start.10 = (f32[4,2,4,2,8,256]{5,4,3,2,1,0:T(8,128)}, f32[4,2,4,2,8,256]{5,4,3,2,1,0:T(8,128)}, u32[]{:S(2)}, u32[]{:S(2)}) collective-permute-start(f32[4,2,4,2,8,256]{5,4,3,2,1,0:T(8,128)} %bitcast.15), channel_id=1, source_target_pairs={{0,16},{8,24},{16,0},{24,8},{32,48},{40,56},{48,32},{56,40},{64,80... | collective-permute-start | bytes 1572872 | tf_op jit(solution)/shard_map/ppermute | solution.py:58
  17.4 33.1 %collective-permute-start.11 = (f32[4,2,4,2,8,256]{5,4,3,2,1,0:T(8,128)S(1)}, f32[4,2,4,2,8,256]{5,4,3,2,1,0:T(8,128)S(1)}, u32[]{:S(2)}, u32[]{:S(2)}) collective-permute-start(f32[4,2,4,2,8,256]{5,4,3,2,1,0:T(8,128)S(1)} %bitcast.84), channel_id=1, source_target_pairs={{0,24},{8,0},{16,8},{24,16},{32,56},{40,32},{48,40},{56,48},{64,88... | collective-permute-start | bytes 1572872 | tf_op jit(solution)/shard_map/ppermute | solution.py:58
  28.0 22.6 %collective-permute-start.7 = (f32[4,2,6,8,256]{4,3,2,1,0:T(8,128)S(1)}, f32[4,2,6,8,256]{4,3,2,1,0:T(8,128)S(1)}, u32[]{:S(2)}, u32[]{:S(2)}) collective-permute-start(f32[4,2,6,8,256]{4,3,2,1,0:T(8,128)S(1)} %get-tuple-element.102), channel_id=1, source_target_pairs={{0,32},{8,40},{16,48},{24,56},{32,64},{40,72},{48,80},{56,88},{64,... | collective-permute-start | bytes 1179656 | tf_op jit(solution)/shard_map/ppermute | solution.py:38
  32.7 18.3 %collective-permute-start.8 = (f32[4,2,6,8,256]{4,3,2,1,0:T(8,128)S(1)}, f32[4,2,6,8,256]{4,3,2,1,0:T(8,128)S(1)}, u32[]{:S(2)}, u32[]{:S(2)}) collective-permute-start(f32[4,2,6,8,256]{4,3,2,1,0:T(8,128)S(1)} %get-tuple-element.101), channel_id=1, source_target_pairs={{32,0},{40,8},{48,16},{56,24},{64,32},{72,40},{80,48},{88,56},{96,... | collective-permute-start | bytes 1179656 | tf_op jit(solution)/shard_map/ppermute | solution.py:38
  37.3 13.8 %collective-permute-start.3 = (f32[4,2,6,8,256]{4,3,2,1,0:T(8,128)S(1)}, f32[4,2,6,8,256]{4,3,2,1,0:T(8,128)S(1)}, u32[]{:S(2)}, u32[]{:S(2)}) collective-permute-start(f32[4,2,6,8,256]{4,3,2,1,0:T(8,128)S(1)} %get-tuple-element.56.refs_5_), channel_id=1, source_target_pairs={{0,1},{1,0},{2,3},{3,2},{4,5},{5,4},{6,7},{7,6},{8,9},{9,8},{10,11... | collective-permute-start | bytes 1179656 | tf_op jit(solution)/shard_map/ppermute | solution.py:67
  66.1 17.1 %collective-permute-start.15 = (f32[4,2,4,2,8,256]{5,4,3,2,1,0:T(8,128)}, f32[4,2,4,2,8,256]{5,4,3,2,1,0:T(8,128)}, u32[]{:S(2)}, u32[]{:S(2)}) collective-permute-start(f32[4,2,4,2,8,256]{5,4,3,2,1,0:T(8,128)} %get-tuple-element.73), channel_id=1, source_target_pairs={{32,0},{40,8},{48,16},{56,24},{64,32},{72,40},{80,48},{88,56},{96,... | collective-permute-start | bytes 1572872 | tf_op jit(solution)/shard_map/ppermute | solution.py:38
  68.2 16.1 %collective-permute-start.14 = (f32[4,2,4,2,8,256]{5,4,3,2,1,0:T(8,128)}, f32[4,2,4,2,8,256]{5,4,3,2,1,0:T(8,128)}, u32[]{:S(2)}, u32[]{:S(2)}) collective-permute-start(f32[4,2,4,2,8,256]{5,4,3,2,1,0:T(8,128)} %get-tuple-element.72), channel_id=1, source_target_pairs={{0,32},{8,40},{16,48},{24,56},{32,64},{40,72},{48,80},{56,88},{64,... | collective-permute-start | bytes 1572872 | tf_op jit(solution)/shard_map/ppermute | solution.py:38
  73.0 19.7 %collective-permute-start.16 = (f32[4,2,4,2,8,256]{5,4,3,2,1,0:T(8,128)}, f32[4,2,4,2,8,256]{5,4,3,2,1,0:T(8,128)S(1)}, u32[]{:S(2)}, u32[]{:S(2)}) collective-permute-start(f32[4,2,4,2,8,256]{5,4,3,2,1,0:T(8,128)} %copy-done.16), channel_id=1, source_target_pairs={{0,8},{8,16},{16,24},{32,40},{40,48},{48,56},{64,72},{72,80},{80,8... | collective-permute-start | bytes 1572872 | tf_op jit(solution)/shard_map/ppermute | solution.py:38
  79.6 14.2 %collective-permute-start.17 = (f32[4,2,4,2,8,256]{5,4,3,2,1,0:T(8,128)}, f32[4,2,4,2,8,256]{5,4,3,2,1,0:T(8,128)S(1)}, u32[]{:S(2)}, u32[]{:S(2)}) collective-permute-start(f32[4,2,4,2,8,256]{5,4,3,2,1,0:T(8,128)} %copy-done.15), channel_id=1, source_target_pairs={{8,0},{16,8},{24,16},{40,32},{48,40},{56,48},{72,64},{80,72},{88,8... | collective-permute-start | bytes 1572872 | tf_op jit(solution)/shard_map/ppermute | solution.py:38
  115.3 14.8 %collective-permute-start.21 = (f32[4,2,4,8,256]{4,3,2,1,0:T(8,128)S(1)}, f32[4,2,4,8,256]{4,3,2,1,0:T(8,128)S(1)}, u32[]{:S(2)}, u32[]{:S(2)}) collective-permute-start(f32[4,2,4,8,256]{4,3,2,1,0:T(8,128)S(1)} %get-tuple-element.79), channel_id=1, source_target_pairs={{0,2},{1,3},{2,4},{3,5},{4,6},{5,7},{6,0},{7,1},{8,10},{9,11},{10,... | collective-permute-start | bytes 786440 | tf_op jit(solution)/shard_map/ppermute | solution.py:63
  130.2 14.3 %collective-permute-start.24 = (f32[4,2,4,8,256]{4,3,2,1,0:T(8,128)S(1)}, f32[4,2,4,8,256]{4,3,2,1,0:T(8,128)S(1)}, u32[]{:S(2)}, u32[]{:S(2)}) collective-permute-start(f32[4,2,4,8,256]{4,3,2,1,0:T(8,128)S(1)} %exponential_multiply_fusion.refs_0_.refs_5_), channel_id=1, source_target_pairs={{0,2},{1,3},{2,4},{3,5},{4,6},{5,7},{6,0},{7,1},{8,10},{9,11},{10,... | collective-permute-start | bytes 786440 | tf_op jit(solution)/shard_map/ppermute | solution.py:63
  130.3 15.5 %collective-permute-start.25 = (f32[4,2,4,8,256]{4,3,2,1,0:T(8,128)S(1)}, f32[4,2,4,8,256]{4,3,2,1,0:T(8,128)S(1)}, u32[]{:S(2)}, u32[]{:S(2)}) collective-permute-start(f32[4,2,4,8,256]{4,3,2,1,0:T(8,128)S(1)} %exponential_multiply_fusion.refs_0_.refs_5_), channel_id=1, source_target_pairs={{0,4},{1,5},{2,6},{3,7},{4,0},{5,1},{6,2},{7,3},{8,12},{9,13},{10,... | collective-permute-start | bytes 786440 | tf_op jit(solution)/shard_map/ppermute | solution.py:63
  130.9 14.9 %collective-permute-start.26 = (f32[4,2,4,8,256]{4,3,2,1,0:T(8,128)S(1)}, f32[4,2,4,8,256]{4,3,2,1,0:T(8,128)S(1)}, u32[]{:S(2)}, u32[]{:S(2)}) collective-permute-start(f32[4,2,4,8,256]{4,3,2,1,0:T(8,128)S(1)} %exponential_multiply_fusion.refs_0_.refs_5_), channel_id=1, source_target_pairs={{0,6},{1,7},{2,0},{3,1},{4,2},{5,3},{6,4},{7,5},{8,14},{9,15},{10,... | collective-permute-start | bytes 786440 | tf_op jit(solution)/shard_map/ppermute | solution.py:63
  132.9 13.5 %collective-permute-start.27 = (f32[4,2,4,8,256]{4,3,2,1,0:T(8,128)S(1)}, f32[4,2,4,8,256]{4,3,2,1,0:T(8,128)S(1)}, u32[]{:S(2)}, u32[]{:S(2)}) collective-permute-start(f32[4,2,4,8,256]{4,3,2,1,0:T(8,128)S(1)} %exponential_multiply_fusion.refs_0_.refs_5_), channel_id=1, source_target_pairs={{0,1},{1,0},{2,3},{3,2},{4,5},{5,4},{6,7},{7,6},{8,9},{9,8},{10,11... | collective-permute-start | bytes 786440 | tf_op jit(solution)/shard_map/ppermute | solution.py:67
  179.9 16.2 %collective-permute-start.37 = (f32[4,2,4,2,8,256]{5,4,3,2,1,0:T(8,128)S(1)}, f32[4,2,4,2,8,256]{5,4,3,2,1,0:T(8,128)S(1)}, u32[]{:S(2)}, u32[]{:S(2)}) collective-permute-start(f32[4,2,4,2,8,256]{5,4,3,2,1,0:T(8,128)S(1)} %get-tuple-element.88), channel_id=1, source_target_pairs={{32,0},{40,8},{48,16},{56,24},{64,32},{72,40},{80,48},{88,56},{96,... | collective-permute-start | bytes 1572872 | tf_op jit(solution)/shard_map/ppermute | solution.py:38
  181.8 15.2 %collective-permute-start.36 = (f32[4,2,4,2,8,256]{5,4,3,2,1,0:T(8,128)S(1)}, f32[4,2,4,2,8,256]{5,4,3,2,1,0:T(8,128)S(1)}, u32[]{:S(2)}, u32[]{:S(2)}) collective-permute-start(f32[4,2,4,2,8,256]{5,4,3,2,1,0:T(8,128)S(1)} %get-tuple-element.87), channel_id=1, source_target_pairs={{0,32},{8,40},{16,48},{24,56},{32,64},{40,72},{48,80},{56,88},{64,... | collective-permute-start | bytes 1572872 | tf_op jit(solution)/shard_map/ppermute | solution.py:38
  187.7 14.2 %collective-permute-start.39 = (f32[4,2,4,2,8,256]{5,4,3,2,1,0:T(8,128)S(1)}, f32[4,2,4,2,8,256]{5,4,3,2,1,0:T(8,128)S(1)}, u32[]{:S(2)}, u32[]{:S(2)}) collective-permute-start(f32[4,2,4,2,8,256]{5,4,3,2,1,0:T(8,128)S(1)} %get-tuple-element.90), channel_id=1, source_target_pairs={{8,0},{16,8},{24,16},{40,32},{48,40},{56,48},{72,64},{80,72},{88,8... | collective-permute-start | bytes 1572872 | tf_op jit(solution)/shard_map/ppermute | solution.py:38
  221.9 14.9 %collective-permute-start.43 = (f32[4,2,4,8,256]{4,3,2,1,0:T(8,128)S(1)}, f32[4,2,4,8,256]{4,3,2,1,0:T(8,128)}, u32[]{:S(2)}, u32[]{:S(2)}) collective-permute-start(f32[4,2,4,8,256]{4,3,2,1,0:T(8,128)S(1)} %get-tuple-element.94), channel_id=1, source_target_pairs={{0,2},{1,3},{2,4},{3,5},{4,6},{5,7},{6,0},{7,1},{8,10},{9,11},{10,... | collective-permute-start | bytes 786440 | tf_op jit(solution)/shard_map/ppermute | solution.py:63
  244.8 14.2 %collective-permute-start.49 = (f32[2,128,256]{2,1,0:T(8,128)S(1)}, f32[2,128,256]{2,1,0:T(8,128)S(1)}, u32[]{:S(2)}, u32[]{:S(2)}) collective-permute-start(f32[2,128,256]{2,1,0:T(8,128)S(1)} %bitcast.75), channel_id=1, source_target_pairs={{0,2},{1,3},{2,4},{3,5},{4,6},{5,7},{6,0},{7,1},{8,10},{9,11},{10,... | collective-permute-start | bytes 786440 | tf_op jit(solution)/shard_map/ppermute | solution.py:63
  244.9 15.5 %collective-permute-start.50 = (f32[2,128,256]{2,1,0:T(8,128)S(1)}, f32[2,128,256]{2,1,0:T(8,128)S(1)}, u32[]{:S(2)}, u32[]{:S(2)}) collective-permute-start(f32[2,128,256]{2,1,0:T(8,128)S(1)} %bitcast.76), channel_id=1, source_target_pairs={{0,4},{1,5},{2,6},{3,7},{4,0},{5,1},{6,2},{7,3},{8,12},{9,13},{10,... | collective-permute-start | bytes 786440 | tf_op jit(solution)/shard_map/ppermute | solution.py:63
  245.3 15.1 %collective-permute-start.51 = (f32[2,128,256]{2,1,0:T(8,128)S(1)}, f32[2,128,256]{2,1,0:T(8,128)S(1)}, u32[]{:S(2)}, u32[]{:S(2)}) collective-permute-start(f32[2,128,256]{2,1,0:T(8,128)S(1)} %bitcast.77), channel_id=1, source_target_pairs={{0,6},{1,7},{2,0},{3,1},{4,2},{5,3},{6,4},{7,5},{8,14},{9,15},{10,... | collective-permute-start | bytes 786440 | tf_op jit(solution)/shard_map/ppermute | solution.py:63
  (52 other events, 545.0 us)

commit v7 on v6

--- a/solution.py
+++ b/solution.py
@@ -525,7 +525,8 @@
         rows = lax.dynamic_slice_in_dim(views[0].reshape(16, 16, 8, 256), 4 * ((y + k) % YD), 4, axis=1)
         return jnp.transpose(rows, (1, 0, 2, 3)).reshape(4, 2, 4, 2, 8, 256)
 
-    pieces = [est_rows(0)] + [y_turn(est_rows(k), k) for k in (1, 2, 3)]
+    parts, views = lax.optimization_barrier(([est_rows(k) for k in range(4)], views))
+    pieces = [parts[0]] + [y_turn(parts[k], k) for k in (1, 2, 3)]
     mats = matrices(axial_taps, lateral_taps)
     shown = [view_rows(k) for k in range(4)]
     pieces, mats = lax.optimization_barrier((pieces, mats))

time: 265 us -> 265 us (level)
  no operation moved by 1% of the time
where the time goes in v7:
time: 265 us; the launch traced here: 264 us
  waiting for transfers between devices  112 us (42%)
  starting transfers between devices  96.3 us (36%)
  Pallas kernels  35.3 us (13%)
  local copies, waits for them, and re-layouts  17.3 us (7%)
  other arithmetic  2.82 us (1%)
    ppermute x12, waiting for transfers between devices, x_turn(): return lax.ppermute(value, 'view', pairs)  47.6 us
    ppermute x14, starting transfers between devices, blk_shift(): return lax.ppermute(value, 'blk', pairs)  40.4 us
    ppermute x17, starting transfers between devices, core_swap(): return lax.ppermute(value, 'view', [(i, i ^ 1) for i in range(2 * XD)])  24.9 us
    ppermute x14, waiting for transfers between devices, blk_shift(): return lax.ppermute(value, 'blk', pairs)  24.8 us
    ppermute x9, waiting for transfers between devices, y_turn(): return lax.ppermute(value, 'blk', pairs)  24.6 us
    pallas_call x2, Pallas kernels, forward(): pl.pallas_call(functools.partial(forward_kernel, first), out_shape=tuple(...  16.3 us
    pallas_call x2, Pallas kernels, backward(): pl.pallas_call(backward_kernel, out_shape=(half, half), in_specs=[SMEM] +...  14.9 us
    ppermute x12, starting transfers between devices, x_turn(): return lax.ppermute(value, 'view', pairs)  12 us
  transfers between devices with their start and end apart: 56, of which 39 were waited for; matrix products, arithmetic and copies ran while one was open for 4% of the time, Pallas kernels for 1%

profile of v7, /device:TPU:97, one launch (start us, length us, event | category | flops | bytes accessed | tf_op | source)
XLA Modules:
  0.0 264.1 jit_solution(15075193649630720626)
XLA Ops:
  19.1 7.4 %collective-permute-done.1.refs_7_ = f32[4,2,6,8,256]{4,3,2,1,0:T(8,128)} collective-permute-done((f32[4,2,6,8,256]{4,3,2,1,0:T(8,128)}, f32[4,2,6,8,256]{4,3,2,1,0:T(8,128)}, u32[]{:S(2)}, u32[]{:S(2)}) %collective-permute-start.1) | collective-permute-done | bytes 393248 | tf_op jit(solution)/shard_map/ppermute | solution.py:58
  28.0 4.8 %collective-permute-start.7 = (f32[4,2,6,8,256]{4,3,2,1,0:T(8,128)S(1)}, f32[4,2,6,8,256]{4,3,2,1,0:T(8,128)S(1)}, u32[]{:S(2)}, u32[]{:S(2)}) collective-permute-start(f32[4,2,6,8,256]{4,3,2,1,0:T(8,128)S(1)} %get-tuple-element.112), channel_id=1, source_target_pairs={{0,32},{8,40},{16,48},{24,56},{32,64},{40,72},{48,80},{56,88},{64,... | collective-permute-start | bytes 1179656 | tf_op jit(solution)/shard_map/ppermute | solution.py:38
  38.8 10.2 %collective-permute-done.10.refs_19_.refs_20_ = f32[4,2,4,2,8,256]{5,4,3,2,1,0:T(8,128)} collective-permute-done((f32[4,2,4,2,8,256]{5,4,3,2,1,0:T(8,128)}, f32[4,2,4,2,8,256]{5,4,3,2,1,0:T(8,128)}, u32[]{:S(2)}, u32[]{:S(2)}) %collective-permute-start.10) | collective-permute-done | bytes 524320 | tf_op jit(solution)/shard_map/ppermute | solution.py:58
  54.1 9.0 %forward.2 = (f32[4,4,2,4,2,8,256]{6,5,4,3,2,1,0:T(8,128)S(1)}, f32[4,2,4,2,8,256]{5,4,3,2,1,0:T(8,128)}, f32[4,2,4,2,8,256]{5,4,3,2,1,0:T(8,128)}, f32[4,2,4,2,...) custom-call(bf16[2,32,144]{2,1,0:T(8,128)(2,1)S(1)} %get-tuple-element.69.refs_0_, ...), custom_call_target="tpu_custom_call" | custom-call | tf_op jit(solution)/shard_map/forward/pallas_call | solution.py:336
  68.2 4.8 %collective-permute-start.14 = (f32[4,2,4,2,8,256]{5,4,3,2,1,0:T(8,128)}, f32[4,2,4,2,8,256]{5,4,3,2,1,0:T(8,128)}, u32[]{:S(2)}, u32[]{:S(2)}) collective-permute-start(f32[4,2,4,2,8,256]{5,4,3,2,1,0:T(8,128)} %get-tuple-element.82), channel_id=1, source_target_pairs={{0,32},{8,40},{16,48},{24,56},{32,64},{40,72},{48,80},{56,88},{64,... | collective-permute-start | bytes 1572872 | tf_op jit(solution)/shard_map/ppermute | solution.py:38
  73.0 6.6 %collective-permute-start.16 = (f32[4,2,4,2,8,256]{5,4,3,2,1,0:T(8,128)}, f32[4,2,4,2,8,256]{5,4,3,2,1,0:T(8,128)S(1)}, u32[]{:S(2)}, u32[]{:S(2)}) collective-permute-start(f32[4,2,4,2,8,256]{5,4,3,2,1,0:T(8,128)} %copy-done.16), channel_id=1, source_target_pairs={{0,8},{8,16},{16,24},{32,40},{40,48},{48,56},{64,72},{72,80},{80,8... | collective-permute-start | bytes 1572872 | tf_op jit(solution)/shard_map/ppermute | solution.py:38
  85.3 6.1 %collective-permute-start.18 = (f32[2,2,4,2,8,256]{5,4,3,2,1,0:T(8,128)S(1)}, f32[2,2,4,2,8,256]{5,4,3,2,1,0:T(8,128)S(1)}, u32[]{:S(2)}, u32[]{:S(2)}) collective-permute-start(f32[2,2,4,2,8,256]{5,4,3,2,1,0:T(8,128)S(1)} %pad_maximum_fusion.1), channel_id=1, source_target_pairs={{0,8},{8,16},{16,24},{32,40},{40,48},{48,56},{64,72},{72,80},{80,8... | collective-permute-start | bytes 786440 | tf_op jit(solution)/shard_map/ppermute | solution.py:38
  95.4 3.9 %collective-permute-done.19.refs_11_ = f32[2,2,4,2,8,256]{5,4,3,2,1,0:T(8,128)S(1)} collective-permute-done((f32[2,2,4,2,8,256]{5,4,3,2,1,0:T(8,128)S(1)}, f32[2,2,4,2,8,256]{5,4,3,2,1,0:T(8,128)S(1)}, u32[]{:S(2)}, u32[]{:S(2)}) %collective-permute-start.19) | collective-permute-done | bytes 262176 | tf_op jit(solution)/shard_map/ppermute | solution.py:38
  99.3 7.4 %backward.2 = (f32[4,4,2,4,8,256]{5,4,3,2,1,0:T(8,128)S(1)}, f32[4,4,2,4,8,256]{5,4,3,2,1,0:T(8,128)S(1)}) custom-call(s32[1,2]{1,0:T(1,128)S(1)} %copy-done.14, bf16[2,32,144]{2,1,0:T(8,128)(2,1)S(1)} %copy-done.9, bf16[2,64,96]{2,1,0:T(8,128)(2,1)S(1)} %copy-done.11, bf16[2,64,96]{2,1,0:T(8,128)(2,1)S(1)} %copy-done.13, ...), custom_call_target="tpu_custom_call" | custom-call | tf_op jit(solution)/shard_map/backward/pallas_call | solution.py:408
  106.8 2.9 %collective-permute-start.20 = (f32[4,4,2,4,8,256]{5,4,3,2,1,0:T(8,128)S(1)}, f32[4,4,2,4,8,256]{5,4,3,2,1,0:T(8,128)S(1)}, u32[]{:S(2)}, u32[]{:S(2)}) collective-permute-start(f32[4,4,2,4,8,256]{5,4,3,2,1,0:T(8,128)S(1)} %get-tuple-element.87), channel_id=1, source_target_pairs={{0,1},{1,0},{2,3},{3,2},{4,5},{5,4},{6,7},{7,6},{8,9},{9,8},{10,11... | collective-permute-start | bytes 3145736 | tf_op jit(solution)/shard_map/ppermute | solution.py:67
  116.0 9.5 %collective-permute-done.23 = f32[4,2,4,8,256]{4,3,2,1,0:T(8,128)S(1)} collective-permute-done((f32[4,2,4,8,256]{4,3,2,1,0:T(8,128)S(1)}, f32[4,2,4,8,256]{4,3,2,1,0:T(8,128)S(1)}, u32[]{:S(2)}, u32[]{:S(2)}) %collective-permute-start.23) | collective-permute-done | bytes 262176 | tf_op jit(solution)/shard_map/ppermute | solution.py:63
  125.5 4.6 %collective-permute-done.21 = f32[4,2,4,8,256]{4,3,2,1,0:T(8,128)S(1)} collective-permute-done((f32[4,2,4,8,256]{4,3,2,1,0:T(8,128)S(1)}, f32[4,2,4,8,256]{4,3,2,1,0:T(8,128)S(1)}, u32[]{:S(2)}, u32[]{:S(2)}) %collective-permute-start.21) | collective-permute-done | bytes 262176 | tf_op jit(solution)/shard_map/ppermute | solution.py:63
  134.3 10.2 %collective-permute-done.24.refs_1_.refs_6_ = f32[4,2,4,8,256]{4,3,2,1,0:T(8,128)S(1)} collective-permute-done((f32[4,2,4,8,256]{4,3,2,1,0:T(8,128)S(1)}, f32[4,2,4,8,256]{4,3,2,1,0:T(8,128)S(1)}, u32[]{:S(2)}, u32[]{:S(2)}) %collective-permute-start.24) | collective-permute-done | bytes 262176 | tf_op jit(solution)/shard_map/ppermute | solution.py:63
  152.8 4.9 %collective-permute-start.34 = (f32[2,4,2,8,256]{4,3,2,1,0:T(8,128)S(1)}, f32[2,4,2,8,256]{4,3,2,1,0:T(8,128)S(1)}, u32[]{:S(2)}, u32[]{:S(2)}) collective-permute-start(f32[2,4,2,8,256]{4,3,2,1,0:T(8,128)S(1)} %get-tuple-element.95), channel_id=1, source_target_pairs={{33,9},{35,11},{37,13},{39,15},{40,0},{41,17},{42,2},{43,19},{44,4... | collective-permute-start | bytes 393224 | tf_op jit(solution)/shard_map/ppermute | solution.py:52
  161.9 8.1 %collective-permute-start.35 = (f32[160,8,256]{2,1,0:T(8,128)S(1)}, f32[160,8,256]{2,1,0:T(8,128)S(1)}, u32[]{:S(2)}, u32[]{:S(2)}) collective-permute-start(f32[160,8,256]{2,1,0:T(8,128)S(1)} %pad_maximum_fusion), channel_id=1, source_target_pairs={{0,1},{1,0},{2,3},{3,2},{4,5},{5,4},{6,7},{7,6},{8,9},{9,8},{10,11... | collective-permute-start | bytes 3932168 | tf_op jit(solution)/shard_map/ppermute | solution.py:67
  172.6 7.2 %forward.3 = (f32[4,4,2,4,2,8,256]{6,5,4,3,2,1,0:T(8,128)S(1)}, f32[4,2,4,2,8,256]{5,4,3,2,1,0:T(8,128)S(1)}, f32[4,2,4,2,8,256]{5,4,3,2,1,0:T(8,128)S(1)}, f32[...) custom-call(bf16[2,32,144]{2,1,0:T(8,128)(2,1)S(1)} %copy-done.9, bf16[2,64,96]{2,1,0:T(8,128)(2,1)S(1)} %copy-done.11, ...), custom_call_target="tpu_custom_call" | custom-call | tf_op jit(solution)/shard_map/forward/pallas_call | solution.py:336
  181.8 4.6 %collective-permute-start.36 = (f32[4,2,4,2,8,256]{5,4,3,2,1,0:T(8,128)S(1)}, f32[4,2,4,2,8,256]{5,4,3,2,1,0:T(8,128)S(1)}, u32[]{:S(2)}, u32[]{:S(2)}) collective-permute-start(f32[4,2,4,2,8,256]{5,4,3,2,1,0:T(8,128)S(1)} %get-tuple-element.97), channel_id=1, source_target_pairs={{0,32},{8,40},{16,48},{24,56},{32,64},{40,72},{48,80},{56,88},{64,... | collective-permute-start | bytes 1572872 | tf_op jit(solution)/shard_map/ppermute | solution.py:38
  189.0 7.1 %collective-permute-done.37.refs_7_ = f32[4,2,4,2,8,256]{5,4,3,2,1,0:T(8,128)S(1)} collective-permute-done((f32[4,2,4,2,8,256]{5,4,3,2,1,0:T(8,128)S(1)}, f32[4,2,4,2,8,256]{5,4,3,2,1,0:T(8,128)S(1)}, u32[]{:S(2)}, u32[]{:S(2)}) %collective-permute-start.37) | collective-permute-done | bytes 524320 | tf_op jit(solution)/shard_map/ppermute | solution.py:38
  203.7 3.9 %collective-permute-done.41.refs_11_ = f32[2,2,4,2,8,256]{5,4,3,2,1,0:T(8,128)S(1)} collective-permute-done((f32[2,2,4,2,8,256]{5,4,3,2,1,0:T(8,128)S(1)}, f32[2,2,4,2,8,256]{5,4,3,2,1,0:T(8,128)S(1)}, u32[]{:S(2)}, u32[]{:S(2)}) %collective-permute-start.41) | collective-permute-done | bytes 262176 | tf_op jit(solution)/shard_map/ppermute | solution.py:38
  207.5 7.5 %backward.3 = (f32[4,4,2,4,8,256]{5,4,3,2,1,0:T(8,128)S(1)}, f32[4,4,2,4,8,256]{5,4,3,2,1,0:T(8,128)S(1)}) custom-call(s32[1,2]{1,0:T(1,128)S(1)} %copy-done.14, bf16[2,32,144]{2,1,0:T(8,128)(2,1)S(1)} %copy-done.9, bf16[2,64,96]{2,1,0:T(8,128)(2,1)S(1)} %copy-done.11, bf16[2,64,96]{2,1,0:T(8,128)(2,1)S(1)} %copy-done.13, ...), custom_call_target="tpu_custom_call" | custom-call | tf_op jit(solution)/shard_map/backward/pallas_call | solution.py:408
  222.6 5.0 %collective-permute-done.45 = f32[4,2,4,8,256]{4,3,2,1,0:T(8,128)} collective-permute-done((f32[4,2,4,8,256]{4,3,2,1,0:T(8,128)S(1)}, f32[4,2,4,8,256]{4,3,2,1,0:T(8,128)}, u32[]{:S(2)}, u32[]{:S(2)}) %collective-permute-start.45) | collective-permute-done | bytes 262176 | tf_op jit(solution)/shard_map/ppermute | solution.py:63
  227.6 3.2 %collective-permute-done.44 = f32[4,2,4,8,256]{4,3,2,1,0:T(8,128)} collective-permute-done((f32[4,2,4,8,256]{4,3,2,1,0:T(8,128)S(1)}, f32[4,2,4,8,256]{4,3,2,1,0:T(8,128)}, u32[]{:S(2)}, u32[]{:S(2)}) %collective-permute-start.44) | collective-permute-done | bytes 262176 | tf_op jit(solution)/shard_map/ppermute | solution.py:63
  230.8 6.0 %collective-permute-done.43 = f32[4,2,4,8,256]{4,3,2,1,0:T(8,128)} collective-permute-done((f32[4,2,4,8,256]{4,3,2,1,0:T(8,128)S(1)}, f32[4,2,4,8,256]{4,3,2,1,0:T(8,128)}, u32[]{:S(2)}, u32[]{:S(2)}) %collective-permute-start.43) | collective-permute-done | bytes 262176 | tf_op jit(solution)/shard_map/ppermute | solution.py:63
  249.9 9.1 %collective-permute-done.49.refs_1_ = f32[2,128,256]{2,1,0:T(8,128)S(1)} collective-permute-done((f32[2,128,256]{2,1,0:T(8,128)S(1)}, f32[2,128,256]{2,1,0:T(8,128)S(1)}, u32[]{:S(2)}, u32[]{:S(2)}) %collective-permute-start.49) | collective-permute-done | bytes 262176 | tf_op jit(solution)/shard_map/ppermute | solution.py:63
  (176 shorter events, 109.4 us)
Async XLA Ops:
  6.6 19.9 %collective-permute-start.1 = (f32[4,2,6,8,256]{4,3,2,1,0:T(8,128)}, f32[4,2,6,8,256]{4,3,2,1,0:T(8,128)}, u32[]{:S(2)}, u32[]{:S(2)}) collective-permute-start(f32[4,2,6,8,256]{4,3,2,1,0:T(8,128)} %get-tuple-element.58), channel_id=1, source_target_pairs={{0,16},{8,24},{16,0},{24,8},{32,48},{40,56},{48,32},{56,40},{64,80... | collective-permute-start | bytes 1179656 | tf_op jit(solution)/shard_map/ppermute | solution.py:58
  9.2 17.4 %collective-permute-start.2 = (f32[4,2,6,8,256]{4,3,2,1,0:T(8,128)}, f32[4,2,6,8,256]{4,3,2,1,0:T(8,128)}, u32[]{:S(2)}, u32[]{:S(2)}) collective-permute-start(f32[4,2,6,8,256]{4,3,2,1,0:T(8,128)} %get-tuple-element.59), channel_id=1, source_target_pairs={{0,24},{8,0},{16,8},{24,16},{32,56},{40,32},{48,40},{56,48},{64,88... | collective-permute-start | bytes 1179656 | tf_op jit(solution)/shard_map/ppermute | solution.py:58
  13.6 23.0 %collective-permute-start.9 = (f32[4,2,4,2,8,256]{5,4,3,2,1,0:T(8,128)}, f32[4,2,4,2,8,256]{5,4,3,2,1,0:T(8,128)S(1)}, u32[]{:S(2)}, u32[]{:S(2)}) collective-permute-start(f32[4,2,4,2,8,256]{5,4,3,2,1,0:T(8,128)} %bitcast.13), channel_id=1, source_target_pairs={{0,8},{8,16},{16,24},{24,0},{32,40},{40,48},{48,56},{56,32},{64,72... | collective-permute-start | bytes 1572872 | tf_op jit(solution)/shard_map/ppermute | solution.py:58
  14.8 34.1 %collective-permute-start.10 = (f32[4,2,4,2,8,256]{5,4,3,2,1,0:T(8,128)}, f32[4,2,4,2,8,256]{5,4,3,2,1,0:T(8,128)}, u32[]{:S(2)}, u32[]{:S(2)}) collective-permute-start(f32[4,2,4,2,8,256]{5,4,3,2,1,0:T(8,128)} %bitcast.15), channel_id=1, source_target_pairs={{0,16},{8,24},{16,0},{24,8},{32,48},{40,56},{48,32},{56,40},{64,80... | collective-permute-start | bytes 1572872 | tf_op jit(solution)/shard_map/ppermute | solution.py:58
  17.4 33.1 %collective-permute-start.11 = (f32[4,2,4,2,8,256]{5,4,3,2,1,0:T(8,128)S(1)}, f32[4,2,4,2,8,256]{5,4,3,2,1,0:T(8,128)S(1)}, u32[]{:S(2)}, u32[]{:S(2)}) collective-permute-start(f32[4,2,4,2,8,256]{5,4,3,2,1,0:T(8,128)S(1)} %bitcast.84), channel_id=1, source_target_pairs={{0,24},{8,0},{16,8},{24,16},{32,56},{40,32},{48,40},{56,48},{64,88... | collective-permute-start | bytes 1572872 | tf_op jit(solution)/shard_map/ppermute | solution.py:58
  28.0 22.6 %collective-permute-start.7 = (f32[4,2,6,8,256]{4,3,2,1,0:T(8,128)S(1)}, f32[4,2,6,8,256]{4,3,2,1,0:T(8,128)S(1)}, u32[]{:S(2)}, u32[]{:S(2)}) collective-permute-start(f32[4,2,6,8,256]{4,3,2,1,0:T(8,128)S(1)} %get-tuple-element.112), channel_id=1, source_target_pairs={{0,32},{8,40},{16,48},{24,56},{32,64},{40,72},{48,80},{56,88},{64,... | collective-permute-start | bytes 1179656 | tf_op jit(solution)/shard_map/ppermute | solution.py:38
  32.7 18.3 %collective-permute-start.8 = (f32[4,2,6,8,256]{4,3,2,1,0:T(8,128)S(1)}, f32[4,2,6,8,256]{4,3,2,1,0:T(8,128)S(1)}, u32[]{:S(2)}, u32[]{:S(2)}) collective-permute-start(f32[4,2,6,8,256]{4,3,2,1,0:T(8,128)S(1)} %get-tuple-element.111), channel_id=1, source_target_pairs={{32,0},{40,8},{48,16},{56,24},{64,32},{72,40},{80,48},{88,56},{96,... | collective-permute-start | bytes 1179656 | tf_op jit(solution)/shard_map/ppermute | solution.py:38
  37.3 13.8 %collective-permute-start.3 = (f32[4,2,6,8,256]{4,3,2,1,0:T(8,128)S(1)}, f32[4,2,6,8,256]{4,3,2,1,0:T(8,128)S(1)}, u32[]{:S(2)}, u32[]{:S(2)}) collective-permute-start(f32[4,2,6,8,256]{4,3,2,1,0:T(8,128)S(1)} %get-tuple-element.65.refs_5_), channel_id=1, source_target_pairs={{0,1},{1,0},{2,3},{3,2},{4,5},{5,4},{6,7},{7,6},{8,9},{9,8},{10,11... | collective-permute-start | bytes 1179656 | tf_op jit(solution)/shard_map/ppermute | solution.py:67
  66.1 17.1 %collective-permute-start.15 = (f32[4,2,4,2,8,256]{5,4,3,2,1,0:T(8,128)}, f32[4,2,4,2,8,256]{5,4,3,2,1,0:T(8,128)}, u32[]{:S(2)}, u32[]{:S(2)}) collective-permute-start(f32[4,2,4,2,8,256]{5,4,3,2,1,0:T(8,128)} %get-tuple-element.83), channel_id=1, source_target_pairs={{32,0},{40,8},{48,16},{56,24},{64,32},{72,40},{80,48},{88,56},{96,... | collective-permute-start | bytes 1572872 | tf_op jit(solution)/shard_map/ppermute | solution.py:38
  68.2 16.1 %collective-permute-start.14 = (f32[4,2,4,2,8,256]{5,4,3,2,1,0:T(8,128)}, f32[4,2,4,2,8,256]{5,4,3,2,1,0:T(8,128)}, u32[]{:S(2)}, u32[]{:S(2)}) collective-permute-start(f32[4,2,4,2,8,256]{5,4,3,2,1,0:T(8,128)} %get-tuple-element.82), channel_id=1, source_target_pairs={{0,32},{8,40},{16,48},{24,56},{32,64},{40,72},{48,80},{56,88},{64,... | collective-permute-start | bytes 1572872 | tf_op jit(solution)/shard_map/ppermute | solution.py:38
  73.0 19.7 %collective-permute-start.16 = (f32[4,2,4,2,8,256]{5,4,3,2,1,0:T(8,128)}, f32[4,2,4,2,8,256]{5,4,3,2,1,0:T(8,128)S(1)}, u32[]{:S(2)}, u32[]{:S(2)}) collective-permute-start(f32[4,2,4,2,8,256]{5,4,3,2,1,0:T(8,128)} %copy-done.16), channel_id=1, source_target_pairs={{0,8},{8,16},{16,24},{32,40},{40,48},{48,56},{64,72},{72,80},{80,8... | collective-permute-start | bytes 1572872 | tf_op jit(solution)/shard_map/ppermute | solution.py:38
  79.6 14.2 %collective-permute-start.17 = (f32[4,2,4,2,8,256]{5,4,3,2,1,0:T(8,128)}, f32[4,2,4,2,8,256]{5,4,3,2,1,0:T(8,128)S(1)}, u32[]{:S(2)}, u32[]{:S(2)}) collective-permute-start(f32[4,2,4,2,8,256]{5,4,3,2,1,0:T(8,128)} %copy-done.15), channel_id=1, source_target_pairs={{8,0},{16,8},{24,16},{40,32},{48,40},{56,48},{72,64},{80,72},{88,8... | collective-permute-start | bytes 1572872 | tf_op jit(solution)/shard_map/ppermute | solution.py:38
  115.3 14.8 %collective-permute-start.21 = (f32[4,2,4,8,256]{4,3,2,1,0:T(8,128)S(1)}, f32[4,2,4,8,256]{4,3,2,1,0:T(8,128)S(1)}, u32[]{:S(2)}, u32[]{:S(2)}) collective-permute-start(f32[4,2,4,8,256]{4,3,2,1,0:T(8,128)S(1)} %get-tuple-element.89), channel_id=1, source_target_pairs={{0,2},{1,3},{2,4},{3,5},{4,6},{5,7},{6,0},{7,1},{8,10},{9,11},{10,... | collective-permute-start | bytes 786440 | tf_op jit(solution)/shard_map/ppermute | solution.py:63
  130.2 14.3 %collective-permute-start.24 = (f32[4,2,4,8,256]{4,3,2,1,0:T(8,128)S(1)}, f32[4,2,4,8,256]{4,3,2,1,0:T(8,128)S(1)}, u32[]{:S(2)}, u32[]{:S(2)}) collective-permute-start(f32[4,2,4,8,256]{4,3,2,1,0:T(8,128)S(1)} %exponential_multiply_fusion.refs_0_.refs_5_), channel_id=1, source_target_pairs={{0,2},{1,3},{2,4},{3,5},{4,6},{5,7},{6,0},{7,1},{8,10},{9,11},{10,... | collective-permute-start | bytes 786440 | tf_op jit(solution)/shard_map/ppermute | solution.py:63
  130.3 15.5 %collective-permute-start.25 = (f32[4,2,4,8,256]{4,3,2,1,0:T(8,128)S(1)}, f32[4,2,4,8,256]{4,3,2,1,0:T(8,128)S(1)}, u32[]{:S(2)}, u32[]{:S(2)}) collective-permute-start(f32[4,2,4,8,256]{4,3,2,1,0:T(8,128)S(1)} %exponential_multiply_fusion.refs_0_.refs_5_), channel_id=1, source_target_pairs={{0,4},{1,5},{2,6},{3,7},{4,0},{5,1},{6,2},{7,3},{8,12},{9,13},{10,... | collective-permute-start | bytes 786440 | tf_op jit(solution)/shard_map/ppermute | solution.py:63
  130.9 14.9 %collective-permute-start.26 = (f32[4,2,4,8,256]{4,3,2,1,0:T(8,128)S(1)}, f32[4,2,4,8,256]{4,3,2,1,0:T(8,128)S(1)}, u32[]{:S(2)}, u32[]{:S(2)}) collective-permute-start(f32[4,2,4,8,256]{4,3,2,1,0:T(8,128)S(1)} %exponential_multiply_fusion.refs_0_.refs_5_), channel_id=1, source_target_pairs={{0,6},{1,7},{2,0},{3,1},{4,2},{5,3},{6,4},{7,5},{8,14},{9,15},{10,... | collective-permute-start | bytes 786440 | tf_op jit(solution)/shard_map/ppermute | solution.py:63
  132.9 13.5 %collective-permute-start.27 = (f32[4,2,4,8,256]{4,3,2,1,0:T(8,128)S(1)}, f32[4,2,4,8,256]{4,3,2,1,0:T(8,128)S(1)}, u32[]{:S(2)}, u32[]{:S(2)}) collective-permute-start(f32[4,2,4,8,256]{4,3,2,1,0:T(8,128)S(1)} %exponential_multiply_fusion.refs_0_.refs_5_), channel_id=1, source_target_pairs={{0,1},{1,0},{2,3},{3,2},{4,5},{5,4},{6,7},{7,6},{8,9},{9,8},{10,11... | collective-permute-start | bytes 786440 | tf_op jit(solution)/shard_map/ppermute | solution.py:67
  179.9 16.2 %collective-permute-start.37 = (f32[4,2,4,2,8,256]{5,4,3,2,1,0:T(8,128)S(1)}, f32[4,2,4,2,8,256]{5,4,3,2,1,0:T(8,128)S(1)}, u32[]{:S(2)}, u32[]{:S(2)}) collective-permute-start(f32[4,2,4,2,8,256]{5,4,3,2,1,0:T(8,128)S(1)} %get-tuple-element.98), channel_id=1, source_target_pairs={{32,0},{40,8},{48,16},{56,24},{64,32},{72,40},{80,48},{88,56},{96,... | collective-permute-start | bytes 1572872 | tf_op jit(solution)/shard_map/ppermute | solution.py:38
  181.8 15.2 %collective-permute-start.36 = (f32[4,2,4,2,8,256]{5,4,3,2,1,0:T(8,128)S(1)}, f32[4,2,4,2,8,256]{5,4,3,2,1,0:T(8,128)S(1)}, u32[]{:S(2)}, u32[]{:S(2)}) collective-permute-start(f32[4,2,4,2,8,256]{5,4,3,2,1,0:T(8,128)S(1)} %get-tuple-element.97), channel_id=1, source_target_pairs={{0,32},{8,40},{16,48},{24,56},{32,64},{40,72},{48,80},{56,88},{64,... | collective-permute-start | bytes 1572872 | tf_op jit(solution)/shard_map/ppermute | solution.py:38
  187.7 14.2 %collective-permute-start.39 = (f32[4,2,4,2,8,256]{5,4,3,2,1,0:T(8,128)S(1)}, f32[4,2,4,2,8,256]{5,4,3,2,1,0:T(8,128)S(1)}, u32[]{:S(2)}, u32[]{:S(2)}) collective-permute-start(f32[4,2,4,2,8,256]{5,4,3,2,1,0:T(8,128)S(1)} %get-tuple-element.100), channel_id=1, source_target_pairs={{8,0},{16,8},{24,16},{40,32},{48,40},{56,48},{72,64},{80,72},{88,8... | collective-permute-start | bytes 1572872 | tf_op jit(solution)/shard_map/ppermute | solution.py:38
  221.9 14.9 %collective-permute-start.43 = (f32[4,2,4,8,256]{4,3,2,1,0:T(8,128)S(1)}, f32[4,2,4,8,256]{4,3,2,1,0:T(8,128)}, u32[]{:S(2)}, u32[]{:S(2)}) collective-permute-start(f32[4,2,4,8,256]{4,3,2,1,0:T(8,128)S(1)} %get-tuple-element.104), channel_id=1, source_target_pairs={{0,2},{1,3},{2,4},{3,5},{4,6},{5,7},{6,0},{7,1},{8,10},{9,11},{10,... | collective-permute-start | bytes 786440 | tf_op jit(solution)/shard_map/ppermute | solution.py:63
  244.8 14.2 %collective-permute-start.49 = (f32[2,128,256]{2,1,0:T(8,128)S(1)}, f32[2,128,256]{2,1,0:T(8,128)S(1)}, u32[]{:S(2)}, u32[]{:S(2)}) collective-permute-start(f32[2,128,256]{2,1,0:T(8,128)S(1)} %bitcast.75), channel_id=1, source_target_pairs={{0,2},{1,3},{2,4},{3,5},{4,6},{5,7},{6,0},{7,1},{8,10},{9,11},{10,... | collective-permute-start | bytes 786440 | tf_op jit(solution)/shard_map/ppermute | solution.py:63
  244.9 15.5 %collective-permute-start.50 = (f32[2,128,256]{2,1,0:T(8,128)S(1)}, f32[2,128,256]{2,1,0:T(8,128)S(1)}, u32[]{:S(2)}, u32[]{:S(2)}) collective-permute-start(f32[2,128,256]{2,1,0:T(8,128)S(1)} %bitcast.76), channel_id=1, source_target_pairs={{0,4},{1,5},{2,6},{3,7},{4,0},{5,1},{6,2},{7,3},{8,12},{9,13},{10,... | collective-permute-start | bytes 786440 | tf_op jit(solution)/shard_map/ppermute | solution.py:63
  245.3 15.1 %collective-permute-start.51 = (f32[2,128,256]{2,1,0:T(8,128)S(1)}, f32[2,128,256]{2,1,0:T(8,128)S(1)}, u32[]{:S(2)}, u32[]{:S(2)}) collective-permute-start(f32[2,128,256]{2,1,0:T(8,128)S(1)} %bitcast.77), channel_id=1, source_target_pairs={{0,6},{1,7},{2,0},{3,1},{4,2},{5,3},{6,4},{7,5},{8,14},{9,15},{10,... | collective-permute-start | bytes 786440 | tf_op jit(solution)/shard_map/ppermute | solution.py:63
  (52 other events, 545.0 us)
